TPU v7x, 32 devices: a whole 2x2x4 slice. The times are simulated.
32 devices in a mesh: row: 2 (over core), col: 16 (over z, y, x).
Axes of the slice: x: 2, y: 2, z: 4, core: 2. Of those that a mesh axis runs over, the one named last changes fastest.
Arguments:
- tiles: bfloat16 [2, 2, 96, 128, 128], P(None, 'row', 'col'), may hold values from -0.21875 to 0.21875
- block_rows: int32 [2, 2, 96], P(None, 'row', 'col'), may hold values from 0 to 31, as said below
- block_cols: int32 [2, 2, 96], P(None, 'row', 'col'), may hold values from 0 to 15
- live_counts: int32 [2, 2, 16], P(None, 'row', 'col'), may hold values from 1 to 6, as said below
- panels: bfloat16 [2, 2048, 4096], P(None, 'row', 'col'), may hold values from -6 to 6
Outputs:
- voltages: float32 [8192, 4096], P('row', 'col')
Inputs may be any that keep to these rules, and one draw needn't show every extreme that they name: `block_rows`: within one step and one bus-row group, all slots name distinct (block row, block column) pairs, and among them are block (0, 0) and block (31, 15). `live_counts`: in every step some bus-row group has all its slots live.
All inputs are finite; a program needn't handle non-finite values.
Results may differ from a plain program's by a relative error of at most 0.0003.
Values may be sent and summed in bfloat16 or wider, within the bound.
No kernel may reach another device: no remote copies, remote signals or barrier semaphores. Data moves between devices by JAX's collectives and lax.ppermute only.
A program may use at most 192 MiB of HBM per device.

v0:
```python
import jax
import jax.numpy as jnp
from jax import lax
from jax.sharding import PartitionSpec as P

RB_DEV = 32


def place_blocks(dense, blocks, rows_idx, cols_idx, counts, per_dev):
    width = blocks.shape[0]
    live = jnp.arange(width) % per_dev < jnp.repeat(counts, per_dev)
    masked = jnp.where(live[:, None, None], blocks, jnp.zeros_like(blocks))
    return dense.at[rows_idx, :, cols_idx, :].add(masked)


def per_device(tiles, block_rows, block_cols, live_counts, panels):
    steps = tiles.shape[0]
    per_dev = tiles.shape[2]
    size = tiles.shape[3]
    scen = panels.shape[2]
    whole = lax.all_gather(panels, "row", axis=1, tiled=True)
    nblocks = whole.shape[1] // size
    start_one = jnp.zeros((RB_DEV, size, nblocks, size), jnp.bfloat16)

    def apply_step(carry, blocks, rows_idx, cols_idx, counts):
        return place_blocks(carry, blocks, rows_idx, cols_idx, counts, per_dev)

    total = jnp.zeros((RB_DEV * size, scen), jnp.float32)
    for step in range(steps):

        def fold_step(carry, piece, start, step=step):
            blocks, rows_idx, cols_idx, counts = piece
            return apply_step(carry, blocks[0, 0], rows_idx[0, 0], cols_idx[0, 0], counts[0, 0])

        carry = fold_step(
            start_one,
            (
                lax.all_gather(tiles[step : step + 1], "col", axis=2, tiled=True),
                lax.all_gather(block_rows[step : step + 1], "col", axis=2, tiled=True),
                lax.all_gather(block_cols[step : step + 1], "col", axis=2, tiled=True),
                lax.all_gather(live_counts[step : step + 1], "col", axis=2, tiled=True),
            ),
            jnp.int32(0),
        )
        matrix = carry.reshape(RB_DEV * size, nblocks * size)
        total = total + jnp.dot(matrix, whole[step], preferred_element_type=jnp.float32)
    return total


def solution(mesh):
    placed = (
        P(None, "row", "col", None, None),
        P(None, "row", "col"),
        P(None, "row", "col"),
        P(None, "row", "col"),
        P(None, "row", "col"),
    )
    return jax.shard_map(
        per_device, mesh=mesh, in_specs=placed, out_specs=P("row", "col"), check_vma=False
    )
```

profile of v0, /device:TPU:0, one launch (start us, length us, event | category | flops | bytes accessed | tf_op | source)
XLA Modules:
  0.0 226.6 jit_solution(7951545144433139392)
XLA Ops:
  6.5 0.0 all-gather.8.cloned.1.call-start
  6.5 1.8 slice_bitcast_fusion.5
  8.3 0.0 all-gather.8.cloned.1.call-update
  8.3 0.0 all-gather.4.cloned.1.call-start
  8.4 0.7 all-gather.4.cloned.1.call-update
  9.1 0.0 all-gather.6.cloned.1.call-start
  9.1 0.7 all-gather.6.cloned.1.call-update
  9.8 1.3 dynamic-slice
  11.7 0.8 bitcast_dynamic-update-slice_fusion.4
  12.5 0.7 bitcast_dynamic-update-slice_fusion.1
  13.2 1.4 fusion.15
  14.6 1.2 bitcast_dynamic-update-slice_fusion.3
  15.9 1.3 bitcast_dynamic-update-slice_fusion
  17.2 0.8 bitcast_dynamic-update-slice_fusion.2
  17.9 0.7 bitcast_dynamic-update-slice_fusion.5
  18.6 16.2 %all-reduce.6 = (s32[96]{0:T(128)S(1)}, s32[96]{0:T(128)S(1)}, s32[16]{0:T(128)S(1)}, s32[96]{0:T(128)S(1)}, s32[96]{0:T(128)S(1)}, /*index=5*/s32[16]{0:T(128)S(1)}) all-reduce(s32[96]{0:T(128)S(1)} %bitcast_dynamic-update-slice_fusion.1, s32[96]{0:T(128)S(1)} %bitcast_dynamic-update-slice_fusion.2, ...), channel_id=1, replica_groups=mesh['row'=2,'col'=16] {'col'}, use_global_device_ids=true, to_apply=%add.4 | all-reduce | flops 416 | bytes 3328
  34.8 0.1 broadcast_in_dim.31
  34.9 0.1 reshape.147
  35.0 0.1 broadcast_in_dim.29
  35.1 0.1 reshape.145
  35.2 45.9 %all-gather.8.cloned.1.call-done = bf16[1,1,96,128,128]{4,3,1,0,2:T(8,128)(2,1)} async-done(((bf16[1,1,6,128,128]{4,3,1,0,2:T(8,128)(2,1)}), bf16[1,1,96,128,128]{4,3,1,0,2:T(8,128)(2,1)}) %all-gather.8.cloned.1.call-update) | async-done | bytes 3145744 | tf_op jit(solution)/shard_map/all_gather | solution.py:38
  81.1 2.2 bitcast_select_fusion
  83.3 6.3 %broadcast_in_dim.28.clone = bf16[32,128,16,128]{3,1,2,0:T(8,128)(2,1)} broadcast(bf16[]{:T(256)} %constant.18.clone.1), dimensions={} | broadcast | bytes 16777218 | tf_op jit(solution)/shard_map/broadcast_in_dim | solution.py:23
  89.6 18.4 %scatter_fusion.1 = bf16[32,128,16,128]{3,1,2,0:T(8,128)(2,1)} fusion(bf16[32,128,16,128]{3,1,2,0:T(8,128)(2,1)} %broadcast_in_dim.28.clone, s32[96]{0:T(128)S(1)} %fusion.12, bf16[96,128,128]{2,1,0:T(8,128)(2,1)S(1)} %bitcast_select_fusion), kind=kCustom, calls=%fused_computation.1 | custom fusion | flops 1572864 | bytes 9437952 | tf_op jit(solution)/shard_map/scatter-add | solution.py:13
  108.0 18.5 %copy.11 = bf16[32,128,16,128]{3,2,1,0:T(8,128)(2,1)} copy(bf16[32,128,16,128]{3,1,2,0:T(8,128)(2,1)} %scatter_fusion.1) | data formatting | bytes 33554432 | tf_op jit(solution)/shard_map/scatter-add | solution.py:13
  126.5 24.0 %all-gather.4.cloned.1.call-done = bf16[1,1,96,128,128]{4,3,1,0,2:T(8,128)(2,1)} async-done(((bf16[1,1,6,128,128]{4,3,1,0,2:T(8,128)(2,1)}), bf16[1,1,96,128,128]{4,3,1,0,2:T(8,128)(2,1)}) %all-gather.4.cloned.1.call-update) | async-done | bytes 3145744 | tf_op jit(solution)/shard_map/all_gather | solution.py:38
  150.5 2.2 bitcast_select_fusion.1
  152.7 6.8 %broadcast_in_dim.28.clone.1 = bf16[32,128,16,128]{3,1,2,0:T(8,128)(2,1)} broadcast(bf16[]{:T(256)} %constant.18.clone.1), dimensions={} | broadcast | bytes 16777218 | tf_op jit(solution)/shard_map/broadcast_in_dim | solution.py:23
  159.5 18.5 %scatter_fusion = bf16[32,128,16,128]{3,1,2,0:T(8,128)(2,1)} fusion(bf16[32,128,16,128]{3,1,2,0:T(8,128)(2,1)} %broadcast_in_dim.28.clone.1, s32[96]{0:T(128)S(1)} %fusion.11, bf16[96,128,128]{2,1,0:T(8,128)(2,1)S(1)} %bitcast_select_fusion.1), kind=kCustom, calls=%fused_computation | custom fusion | flops 1572864 | bytes 9437952 | tf_op jit(solution)/shard_map/scatter-add | solution.py:13
  177.9 18.5 %copy.9 = bf16[32,128,16,128]{3,2,1,0:T(8,128)(2,1)} copy(bf16[32,128,16,128]{3,1,2,0:T(8,128)(2,1)} %scatter_fusion) | data formatting | bytes 33554432 | tf_op jit(solution)/shard_map/scatter-add | solution.py:13
  196.5 0.0 all-gather.6.cloned.1.call-done
  196.5 0.0 copy-start
  196.5 10.8 %fusion = f32[4096,256]{1,0:T(8,128)S(1)} fusion(bf16[512,8,16,128]{3,2,1,0:T(8,128)(2,1)} %bitcast.60, bf16[2,2048,256]{2,1,0:T(8,128)(2,1)} %all-gather.6.cloned.1.call-done), kind=kOutput, calls=%fused_computation.2 | convolution fusion | flops 4294967296 | bytes 22020096 | tf_op jit(solution)/shard_map/dot_general | solution.py:46
  207.3 0.0 copy-done
  207.3 12.8 %fusion.6 = f32[4096,256]{1,0:T(8,128)} fusion(f32[4096,256]{1,0:T(8,128)S(1)} %fusion, bf16[512,8,16,128]{3,2,1,0:T(8,128)(2,1)} %bitcast.61, bf16[2,2048,256]{2,1,0:T(8,128)(2,1)S(1)} %copy-done), kind=kOutput, calls=%fused_computation.8 | convolution fusion | flops 4296015872 | bytes 26214400 | tf_op jit(solution)/shard_map/dot_general | solution.py:46
  (10 shorter events, 0.1 us)
Async XLA Ops:
  6.5 74.6 %all-gather.8.cloned.1.call-start = ((), (), s32[]{:S(2)}) async-start(), calls=%async_computation.2 | async-start | bytes 3342336 | tf_op jit(solution)/shard_map/all_gather | solution.py:38
  8.3 142.2 %all-gather.4.cloned.1.call-start = ((), (), s32[]{:S(2)}) async-start(), calls=%async_computation | async-start | bytes 3342336 | tf_op jit(solution)/shard_map/all_gather | solution.py:38
  9.1 187.4 %all-gather.6.cloned.1.call-start = ((), (), s32[]{:S(2)}) async-start(), calls=%async_computation.1 | async-start | bytes 3145728 | tf_op jit(solution)/shard_map/all_gather | solution.py:21
  196.5 10.8 %copy-start = (bf16[2,2048,256]{2,1,0:T(8,128)(2,1)S(1)}, bf16[2,2048,256]{2,1,0:T(8,128)(2,1)}, u32[]{:S(2)}) copy-start(bf16[2,2048,256]{2,1,0:T(8,128)(2,1)} %all-gather.6.cloned.1.call-done) | copy-start | bytes 6291460
Sparse Core Ops, SparseCore 0:
  10.1 70.9 all-gather.7
  83.9 66.6 all-gather.3
  152.1 9.0 all-gather.5
where the time goes:
time: 228 us; the launch traced here: 227 us
  waiting for transfers between devices  71.3 us (31%)
  local copies, waits for them, and re-layouts  60.4 us (26%)
  other arithmetic  41.2 us (18%)
  matrix products  23.6 us (10%)
  blocking collectives  16.2 us (7%)
  between operations  13.8 us (6%)
    all_gather x2, waiting for transfers between devices, per_device(): lax.all_gather(tiles[step:step + 1], 'col', axis=2, tiled=True)  69.9 us
    scatter-add x2, local copies, waits for them, and re-layouts, place_blocks(): return dense.at[rows_idx, :, cols_idx, :].add(masked)  37.1 us
    scatter-add x2, other arithmetic, place_blocks(): return dense.at[rows_idx, :, cols_idx, :].add(masked)  36.8 us
    dot_general x2, matrix products, per_device(): jnp.dot(matrix, whole[step], preferred_element_type=jnp.float32)  23.6 us
    unnamed x1, blocking collectives  16.2 us
    broadcast_in_dim x2, local copies, waits for them, and re-layouts, per_device(): start_one = jnp.zeros((RB_DEV, size, nblocks, size), jnp.bfloat16)  13.1 us
    unnamed x16, local copies, waits for them, and re-layouts  8.56 us
  transfers between devices with their start and end apart: 3, of which 2 were waited for; matrix products, arithmetic and copies ran while one was open for 44% of the time, Pallas kernels for 0%

commit v1 on v0

v1 whole, which is shorter than its diff:
```python
import functools

import jax
import jax.numpy as jnp
from jax import lax
from jax.experimental import pallas as pl
from jax.experimental.pallas import tpu as pltpu
from jax.sharding import PartitionSpec as P

RB_DEV = 32
META = 16


def col_dims(n_col):
    return (4, 2, n_col // 8) if n_col % 8 == 0 else (n_col,)


def flat(dims, offset):
    index = 0
    for size, part in zip(dims, offset):
        index = index * size + part % size
    return index


def unflat(dims, index):
    parts = []
    for size in reversed(dims):
        parts.append(index % size)
        index //= size
    return tuple(reversed(parts))


def hop(dims, axis, unit):
    n_col = 1
    for size in dims:
        n_col *= size
    pairs = []
    for index in range(n_col):
        at = list(unflat(dims, index))
        at[axis] += 1
        pairs.append((index, flat(dims, at)))
    return lax.ppermute(unit, "col", pairs)


def back(dims, axis, offset):
    at = list(offset)
    at[axis] = (at[axis] - 1) % dims[axis]
    return tuple(at)


def gather_plan(dims):
    if dims == (4, 2, 2):
        return [
            [((0, 0, 1), 2), ((0, 1, 0), 1), ((1, 0, 0), 0)],
            [((2, 0, 0), 0), ((0, 1, 1), 2), ((1, 1, 0), 1)],
            [((3, 0, 0), 0), ((1, 1, 1), 2), ((2, 1, 0), 1)],
            [((3, 0, 1), 2), ((3, 1, 0), 1), ((1, 0, 1), 0)],
            [((2, 1, 1), 2), ((3, 1, 1), 1), ((2, 0, 1), 0)],
        ]
    total = 1
    for size in dims:
        total *= size
    held = {(0,) * len(dims)}
    slots = []
    while len(held) < total:
        slot = []
        taken = set()
        for axis in range(len(dims)):
            for index in range(1, total):
                offset = unflat(dims, index)
                if offset not in held and offset not in taken and back(dims, axis, offset) in held:
                    slot.append((offset, axis))
                    taken.add(offset)
                    break
        held |= taken
        slots.append(slot)
    return slots


def pack_kernel(rows_ref, cols_ref, counts_ref, tiles_ref, unit_ref, sem):
    steps, _, per_dev = rows_ref.shape
    body = tiles_ref.shape[0]
    copy = pltpu.make_async_copy(tiles_ref, unit_ref.at[pl.ds(0, body)], sem)
    copy.start()
    lane = lax.broadcasted_iota(jnp.int32, (META, 128), 1)
    meta = jnp.zeros((META, 128), jnp.int32)
    n_slots = steps * per_dev
    for step in range(steps):
        for q in range(per_dev):
            at = step * per_dev + q
            row = jnp.where(q < counts_ref[step, 0, 0], rows_ref[step, 0, q], RB_DEV)
            meta = jnp.where(lane == at, row, meta)
            meta = jnp.where(lane == n_slots + at, cols_ref[step, 0, q], meta)
    unit_ref[pl.ds(body, META), :] = meta.astype(jnp.float32).astype(jnp.bfloat16)
    copy.wait()


def pack(rows, cols, counts, tiles):
    steps, _, per_dev, size, _ = tiles.shape
    body = steps * per_dev * size
    smem = pl.BlockSpec(memory_space=pltpu.SMEM)
    return pl.pallas_call(
        pack_kernel,
        out_shape=jax.ShapeDtypeStruct((body + META, size), jnp.bfloat16),
        in_specs=[smem, smem, smem, pl.BlockSpec(memory_space=pl.ANY)],
        out_specs=pl.BlockSpec(memory_space=pltpu.VMEM),
        scratch_shapes=[pltpu.SemaphoreType.DMA],
        compiler_params=pltpu.CompilerParams(vmem_limit_bytes=2 << 20),
        name="pack",
    )(rows, cols, counts, tiles.reshape(body, size))


def panel_kernel(*refs, n_row):
    pieces, whole_ref, acc_ref, sem = refs[:n_row], refs[n_row], refs[n_row + 1], refs[n_row + 2]
    steps, depth, _ = pieces[0].shape
    me = lax.axis_index("row")
    copies = []
    for back_by, piece in enumerate(pieces):
        owner = lax.rem(me - back_by + n_row, n_row)
        for step in range(steps):
            copies.append(
                pltpu.make_async_copy(
                    piece.at[step],
                    whole_ref.at[step, pl.ds(owner * depth, depth)],
                    sem.at[back_by * steps + step],
                )
            )
    for copy in copies:
        copy.start()
    acc_ref[...] = jnp.zeros_like(acc_ref)
    for copy in copies:
        copy.wait()


def whole_panels(pieces, size):
    n_row = len(pieces)
    steps, depth, scen = pieces[0].shape
    return pl.pallas_call(
        functools.partial(panel_kernel, n_row=n_row),
        out_shape=(
            pltpu.VMEM((steps, n_row * depth, scen), jnp.bfloat16),
            pltpu.VMEM(((RB_DEV + 1) * size, scen), jnp.float32),
        ),
        in_specs=[pl.BlockSpec(memory_space=pl.ANY)] * n_row,
        out_specs=(pl.BlockSpec(memory_space=pltpu.VMEM),) * 2,
        scratch_shapes=[pltpu.SemaphoreType.DMA((n_row * steps,))],
        compiler_params=pltpu.CompilerParams(vmem_limit_bytes=2 << 20),
        name="panels",
    )(*pieces)


def add_units(n, steps, size, unit_refs, panel_ref, acc_ref, meta_ref, index_ref, sem):
    body = unit_refs[0].shape[0] - META
    n_slots = body // size
    per_step = n_slots // steps
    for k in range(n):
        meta = unit_refs[k][pl.ds(body, META), :].astype(jnp.float32).astype(jnp.int32)
        meta_ref[pl.ds(8 * k, 8), :] = meta[:8]
    copy = pltpu.make_async_copy(meta_ref, index_ref, sem)
    copy.start()
    copy.wait()
    for k in range(n):
        for q in range(n_slots):
            row = index_ref[8 * k, q]
            col = index_ref[8 * k, n_slots + q]
            product = jnp.dot(
                unit_refs[k][pl.ds(q * size, size), :],
                panel_ref[q // per_step, pl.ds(pl.multiple_of(col * size, size), size), :],
                preferred_element_type=jnp.float32,
            )
            at = pl.ds(pl.multiple_of(row * size, size), size)
            acc_ref[at, :] = acc_ref[at, :] + product


def fold_kernel(*refs, n, steps, size):
    unit_refs, panel_ref, _, acc_ref, meta_ref, index_ref, sem = refs[:n], *refs[n:]
    add_units(n, steps, size, unit_refs, panel_ref, acc_ref, meta_ref, index_ref, sem)


def last_kernel(*refs, n, steps, size):
    unit_refs, panel_ref, _, acc_ref, out_ref, meta_ref, index_ref, sem, out_sem = refs[:n], *refs[n:]
    add_units(n, steps, size, unit_refs, panel_ref, acc_ref, meta_ref, index_ref, sem)
    copy = pltpu.make_async_copy(acc_ref.at[pl.ds(0, out_ref.shape[0])], out_ref, out_sem)
    copy.start()
    copy.wait()


def fold(units, panels, acc, last):
    n = len(units)
    steps = panels.shape[0]
    rows, size = units[0].shape
    scen = panels.shape[2]
    vmem = pl.BlockSpec(memory_space=pltpu.VMEM)
    acc_shape = pltpu.VMEM(acc.shape, jnp.float32)
    scratch = [
        pltpu.VMEM((8 * n, 128), jnp.int32),
        pltpu.SMEM((8 * n, 128), jnp.int32),
        pltpu.SemaphoreType.DMA,
    ]
    cost = pl.CostEstimate(
        flops=2 * n * (rows - META) * size * scen, bytes_accessed=n * rows * size * 2, transcendentals=0
    )
    if last:
        _, out = pl.pallas_call(
            functools.partial(last_kernel, n=n, steps=steps, size=size),
            out_shape=(acc_shape, jax.ShapeDtypeStruct((RB_DEV * size, scen), jnp.float32)),
            in_specs=[vmem] * (n + 2),
            out_specs=(vmem, pl.BlockSpec(memory_space=pl.ANY)),
            input_output_aliases={n + 1: 0},
            scratch_shapes=scratch + [pltpu.SemaphoreType.DMA],
            cost_estimate=cost,
            compiler_params=pltpu.CompilerParams(vmem_limit_bytes=8 << 20),
            name="last",
        )(*units, panels, acc)
        return out
    return pl.pallas_call(
        functools.partial(fold_kernel, n=n, steps=steps, size=size),
        out_shape=acc_shape,
        in_specs=[vmem] * (n + 2),
        out_specs=vmem,
        input_output_aliases={n + 1: 0},
        scratch_shapes=scratch,
        cost_estimate=cost,
        compiler_params=pltpu.CompilerParams(vmem_limit_bytes=8 << 20),
        name="fold",
    )(*units, panels, acc)


def per_device(tiles, block_rows, block_cols, live_counts, panels, n_row, n_col):
    size = tiles.shape[3]
    dims = col_dims(n_col)
    ring = [(i, (i + 1) % n_row) for i in range(n_row)]
    pieces = [panels]
    for _ in range(n_row - 1):
        pieces.append(lax.ppermute(pieces[-1], "row", ring))
    own = pack(block_rows, block_cols, live_counts, tiles)
    held = {(0,) * len(dims): own}
    waiting = [own]
    acc = None
    for slot in gather_plan(dims):
        arrived = tuple(hop(dims, axis, held[back(dims, axis, offset)]) for offset, axis in slot)
        if acc is None:
            whole, acc = whole_panels(pieces, size)
        acc = fold(waiting, whole, acc, False)
        arrived = lax.optimization_barrier(arrived)
        for (offset, _), unit in zip(slot, arrived):
            held[offset] = unit
        waiting = list(arrived)
    return fold(waiting, whole, acc, True)


def solution(mesh):
    placed = (
        P(None, "row", "col", None, None),
        P(None, "row", "col"),
        P(None, "row", "col"),
        P(None, "row", "col"),
        P(None, "row", "col"),
    )
    body = functools.partial(per_device, n_row=mesh.shape["row"], n_col=mesh.shape["col"])
    return jax.shard_map(body, mesh=mesh, in_specs=placed, out_specs=P("row", "col"), check_vma=False)
```

time: 228 us -> 71.1 us (0.31)
  local copies, waits for them, and re-layouts: 60.4 us -> 4.31 us
  other arithmetic: 41.2 us -> 0 us
  waiting for transfers between devices: 71.3 us -> 42 us
  matrix products: 23.6 us -> 0 us
  blocking collectives: 16.2 us -> 0 us
  between operations: 13.8 us -> 0.11 us
  Pallas kernels: 0 us -> 12.2 us
  starting transfers between devices: 0.08 us -> 12.2 us
    all_gather x3 -> x0, waiting for transfers between devices: 69.9 us -> none  [the longest x2 69.9 us: per_device(): lax.all_gather(tiles[step:step + 1], 'col', axis=2, tiled=True)]
    ppermute x0 -> x16, waiting for transfers between devices: none -> 42 us  [the longest x15 42 us: hop(): return lax.ppermute(unit, 'col', pairs)]
    scatter-add x2 -> x0, local copies, waits for them, and re-layouts: 37.1 us -> none  [place_blocks(): return dense.at[rows_idx, :, cols_idx, :].add(masked)]
    scatter-add x2 -> x0, other arithmetic: 36.8 us -> none  [place_blocks(): return dense.at[rows_idx, :, cols_idx, :].add(masked)]
    dot_general x2 -> x0, matrix products: 23.6 us -> none  [per_device(): jnp.dot(matrix, whole[step], preferred_element_type=jnp.float32)]
    unnamed x1 -> x0, blocking collectives: 16.2 us -> none
    broadcast_in_dim x4 -> x0, local copies, waits for them, and re-layouts: 13.2 us -> none  [the longest x2 13.1 us: per_device(): start_one = jnp.zeros((RB_DEV, size, nblocks, size), jnp.bfloat16)]
    ppermute x0 -> x16, starting transfers between devices: none -> 12.2 us  [the longest x15 12.2 us: hop(): return lax.ppermute(unit, 'col', pairs)]
  transfers between devices with their start and end apart: 3 -> 16, of which waited for: 2 -> 9; matrix products, arithmetic and copies ran while one was open for 44% -> 0% of each run, Pallas kernels for 0% -> 11%
where the time goes in v1:
time: 71.1 us; the launch traced here: 70.9 us
  waiting for transfers between devices  42 us (59%)
  Pallas kernels  12.2 us (17%)
  starting transfers between devices  12.2 us (17%)
  local copies, waits for them, and re-layouts  4.31 us (6%)
    ppermute x15, waiting for transfers between devices, hop(): return lax.ppermute(unit, 'col', pairs)  42 us
    ppermute x15, starting transfers between devices, hop(): return lax.ppermute(unit, 'col', pairs)  12.2 us
    pallas_call x5, Pallas kernels, fold(): pl.pallas_call(functools.partial(fold_kernel, n=n, steps=steps, size=size...  7.36 us
    unnamed x9, local copies, waits for them, and re-layouts  4.31 us
    pallas_call x1, Pallas kernels, fold(): pl.pallas_call(functools.partial(last_kernel, n=n, steps=steps, size=size...  3.61 us
  transfers between devices with their start and end apart: 16, of which 9 were waited for; matrix products, arithmetic and copies ran while one was open for 0% of the time, Pallas kernels for 11%

profile of v1, /device:TPU:0, one launch (start us, length us, event | category | flops | bytes accessed | tf_op | source)
XLA Modules:
  0.0 70.9 jit_solution(13096924584101817766)
XLA Ops:
  0.0 0.7 %copy.12.counts_ref = s32[2,1,1]{2,1,0:T(1,128)S(1)} copy(s32[2,1,1]{0,2,1:T(1,128)} %param.8) | data formatting | bytes 16 | tf_op args[3]
  0.7 0.0 copy-start.1
  0.7 1.0 %copy-done.1 = bf16[2,1,6,128,128]{4,3,2,1,0:T(8,128)(2,1)S(1)} copy-done((bf16[2,1,6,128,128]{4,3,2,1,0:T(8,128)(2,1)S(1)}, bf16[2,1,6,128,128]{4,3,2,1,0:T(8,128)(2,1)}, u32[]{:S(2)}) %copy-start.1) | copy-done | bytes 393240
  1.7 0.0 copy-start.2
  1.7 0.7 copy-done.2
  2.4 0.7 copy-done.3
  3.1 0.8 %pack.1.refs_0_ = bf16[1552,128]{1,0:T(8,128)(2,1)S(1)} custom-call(s32[2,1,6]{2,1,0:T(1,128)S(1)} %copy-done.2, s32[2,1,6]{2,1,0:T(1,128)S(1)} %copy-done.3, s32[2,1,1]{2,1,0:T(1,128)S(1)} %copy.12.counts_ref, bf16[1536,128]{1,0:T(8,128)(2,1)S(1)} %bitcast.1), custom_call_target="tpu_custom_call" | custom-call | tf_op jit(solution)/shard_map/pack/pallas_call | solution.py:102
  3.9 3.0 %collective-permute-start = (bf16[1552,128]{1,0:T(8,128)(2,1)S(1)}, bf16[1552,128]{1,0:T(8,128)(2,1)S(1)}, u32[]{:S(2)}, u32[]{:S(2)}) collective-permute-start(bf16[1552,128]{1,0:T(8,128)(2,1)S(1)} %pack.1.refs_0_), channel_id=1, source_target_pairs={{0,1},{1,0},{2,3},{3,2},{4,5},{5,4},{6,7},{7,6},{8,9},{9,8},{10,11... | collective-permute-start | bytes 1191944 | tf_op jit(solution)/shard_map/ppermute | solution.py:42
  6.9 1.5 %collective-permute-start.1 = (bf16[1552,128]{1,0:T(8,128)(2,1)S(1)}, bf16[1552,128]{1,0:T(8,128)(2,1)S(1)}, u32[]{:S(2)}, u32[]{:S(2)}) collective-permute-start(bf16[1552,128]{1,0:T(8,128)(2,1)S(1)} %pack.1.refs_0_), channel_id=1, source_target_pairs={{0,2},{1,3},{2,0},{3,1},{4,6},{5,7},{6,4},{7,5},{8,10},{9,11},{10,... | collective-permute-start | bytes 1191944 | tf_op jit(solution)/shard_map/ppermute | solution.py:42
  8.4 1.6 %collective-permute-start.2 = (bf16[1552,128]{1,0:T(8,128)(2,1)S(1)}, bf16[1552,128]{1,0:T(8,128)(2,1)S(1)}, u32[]{:S(2)}, u32[]{:S(2)}) collective-permute-start(bf16[1552,128]{1,0:T(8,128)(2,1)S(1)} %pack.1.refs_0_), channel_id=1, source_target_pairs={{0,4},{1,5},{2,6},{3,7},{4,8},{5,9},{6,10},{7,11},{8,12},{9,13},{1... | collective-permute-start | bytes 1191944 | tf_op jit(solution)/shard_map/ppermute | solution.py:42
  10.0 6.1 %collective-permute-done.refs_0_ = bf16[1552,128]{1,0:T(8,128)(2,1)S(1)} collective-permute-done((bf16[1552,128]{1,0:T(8,128)(2,1)S(1)}, bf16[1552,128]{1,0:T(8,128)(2,1)S(1)}, u32[]{:S(2)}, u32[]{:S(2)}) %collective-permute-start) | collective-permute-done | bytes 397344 | tf_op jit(solution)/shard_map/ppermute | solution.py:42
  16.1 1.5 %collective-permute-done.1.refs_1_ = bf16[1552,128]{1,0:T(8,128)(2,1)S(1)} collective-permute-done((bf16[1552,128]{1,0:T(8,128)(2,1)S(1)}, bf16[1552,128]{1,0:T(8,128)(2,1)S(1)}, u32[]{:S(2)}, u32[]{:S(2)}) %collective-permute-start.1) | collective-permute-done | bytes 397344 | tf_op jit(solution)/shard_map/ppermute | solution.py:42
  17.6 3.1 %collective-permute-done.2.refs_2_ = bf16[1552,128]{1,0:T(8,128)(2,1)S(1)} collective-permute-done((bf16[1552,128]{1,0:T(8,128)(2,1)S(1)}, bf16[1552,128]{1,0:T(8,128)(2,1)S(1)}, u32[]{:S(2)}, u32[]{:S(2)}) %collective-permute-start.2) | collective-permute-done | bytes 397344 | tf_op jit(solution)/shard_map/ppermute | solution.py:42
  20.7 0.0 collective-permute-start.3
  20.7 0.5 collective-permute-start.5
  21.2 0.5 collective-permute-start.4
  21.7 10.3 %collective-permute-done.3.refs_0_ = bf16[1552,128]{1,0:T(8,128)(2,1)S(1)} collective-permute-done((bf16[1552,128]{1,0:T(8,128)(2,1)S(1)}, bf16[1552,128]{1,0:T(8,128)(2,1)S(1)}, u32[]{:S(2)}, u32[]{:S(2)}) %collective-permute-start.3) | collective-permute-done | bytes 397344 | tf_op jit(solution)/shard_map/ppermute | solution.py:42
  32.0 0.0 collective-permute-done.5.refs_2_
  32.0 0.0 collective-permute-done.4.refs_1_
  32.0 0.0 collective-permute-start.6
  32.0 0.9 %collective-permute-start.8 = (bf16[1552,128]{1,0:T(8,128)(2,1)S(1)}, bf16[1552,128]{1,0:T(8,128)(2,1)S(1)}, u32[]{:S(2)}, u32[]{:S(2)}) collective-permute-start(bf16[1552,128]{1,0:T(8,128)(2,1)S(1)} %collective-permute-done.3.refs_0_), channel_id=1, source_target_pairs={{0,2},{1,3},{2,0},{3,1},{4,6},{5,7},{6,4},{7,5},{8,10},{9,11},{10,... | collective-permute-start | bytes 1191944 | tf_op jit(solution)/shard_map/ppermute | solution.py:42
  32.9 0.5 collective-permute-start.7
  33.4 0.0 collective-permute-start.15
  33.4 1.6 %collective-permute-start.12 = (bf16[1552,128]{1,0:T(8,128)(2,1)S(1)}, bf16[1552,128]{1,0:T(8,128)(2,1)S(1)}, u32[]{:S(2)}, u32[]{:S(2)}) collective-permute-start(bf16[1552,128]{1,0:T(8,128)(2,1)S(1)} %collective-permute-done.refs_0_), channel_id=1, source_target_pairs={{0,4},{1,5},{2,6},{3,7},{4,8},{5,9},{6,10},{7,11},{8,12},{9,13},{1... | collective-permute-start | bytes 1191944 | tf_op jit(solution)/shard_map/ppermute | solution.py:42
  35.0 10.9 %collective-permute-done.6.refs_0_ = bf16[1552,128]{1,0:T(8,128)(2,1)S(1)} collective-permute-done((bf16[1552,128]{1,0:T(8,128)(2,1)S(1)}, bf16[1552,128]{1,0:T(8,128)(2,1)S(1)}, u32[]{:S(2)}, u32[]{:S(2)}) %collective-permute-start.6) | collective-permute-done | bytes 397344 | tf_op jit(solution)/shard_map/ppermute | solution.py:42
  45.9 0.0 collective-permute-done.8.refs_2_
  45.9 0.0 collective-permute-done.7.refs_1_
  45.9 0.0 collective-permute-start.10
  46.0 0.5 collective-permute-start.11
  46.5 1.5 %collective-permute-start.9 = (bf16[1552,128]{1,0:T(8,128)(2,1)S(1)}, bf16[1552,128]{1,0:T(8,128)(2,1)S(1)}, u32[]{:S(2)}, u32[]{:S(2)}) collective-permute-start(bf16[1552,128]{1,0:T(8,128)(2,1)S(1)} %collective-permute-done.8.refs_2_), channel_id=1, source_target_pairs={{0,1},{1,0},{2,3},{3,2},{4,5},{5,4},{6,7},{7,6},{8,9},{9,8},{10,11... | collective-permute-start | bytes 1191944 | tf_op jit(solution)/shard_map/ppermute | solution.py:42
  48.0 2.9 %collective-permute-done.12.refs_2_ = bf16[1552,128]{1,0:T(8,128)(2,1)S(1)} collective-permute-done((bf16[1552,128]{1,0:T(8,128)(2,1)S(1)}, bf16[1552,128]{1,0:T(8,128)(2,1)S(1)}, u32[]{:S(2)}, u32[]{:S(2)}) %collective-permute-start.12) | collective-permute-done | bytes 397344 | tf_op jit(solution)/shard_map/ppermute | solution.py:42
  50.9 3.4 %collective-permute-done.10.refs_0_ = bf16[1552,128]{1,0:T(8,128)(2,1)S(1)} collective-permute-done((bf16[1552,128]{1,0:T(8,128)(2,1)S(1)}, bf16[1552,128]{1,0:T(8,128)(2,1)S(1)}, u32[]{:S(2)}, u32[]{:S(2)}) %collective-permute-start.10) | collective-permute-done | bytes 397344 | tf_op jit(solution)/shard_map/ppermute | solution.py:42
  54.3 3.3 %collective-permute-done.11.refs_1_ = bf16[1552,128]{1,0:T(8,128)(2,1)S(1)} collective-permute-done((bf16[1552,128]{1,0:T(8,128)(2,1)S(1)}, bf16[1552,128]{1,0:T(8,128)(2,1)S(1)}, u32[]{:S(2)}, u32[]{:S(2)}) %collective-permute-start.11) | collective-permute-done | bytes 397344 | tf_op jit(solution)/shard_map/ppermute | solution.py:42
  57.7 0.0 collective-permute-start.13
  57.7 0.0 collective-permute-start.14
  57.7 0.0 collective-permute-done.15.refs_1_
  57.7 0.0 copy-start
  57.7 1.2 %copy-done = bf16[2,1024,256]{2,1,0:T(8,128)(2,1)S(1)} copy-done((bf16[2,1024,256]{2,1,0:T(8,128)(2,1)S(1)}, bf16[2,1024,256]{2,1,0:T(8,128)(2,1)}, u32[]{:S(2)}) %copy-start) | copy-done | bytes 1048600
  58.9 0.5 panels.1
  59.4 1.0 %fold.5.refs_4_ = f32[4224,256]{1,0:T(8,128)S(1)} custom-call(bf16[1552,128]{1,0:T(8,128)(2,1)S(1)} %pack.1.refs_0_, bf16[2,2048,256]{2,1,0:T(8,128)(2,1)S(1)} %get-tuple-element.35.refs_1_.refs_3_, f32[4224,256]{1,0:T(8,128)S(1)} %get-tuple-element.39.refs_2_), custom_call_target="tpu_custom_call", output_to_operand_aliasing={{}: (2, {})} | custom-call | flops 100663296 | bytes 397312 | tf_op jit(solution)/shard_map/fold/pallas_call | solution.py:216
  60.4 1.6 %fold.6.refs_4_ = f32[4224,256]{1,0:T(8,128)S(1)} custom-call(bf16[1552,128]{1,0:T(8,128)(2,1)S(1)} %collective-permute-done.refs_0_, bf16[1552,128]{1,0:T(8,128)(2,1)S(1)} %collective-permute-done.1.refs_1_, bf16[1552,128]{1,0:T(8,128)(2,1)S(1)} %collective-permute-done.2.refs_2_, ...), custom_call_target="tpu_custom_call", output_to_operand_aliasing={{}: (4, {})} | custom-call | flops 301989888 | bytes 1191936 | tf_op jit(solution)/shard_map/fold/pallas_call | solution.py:216
  62.0 1.6 %fold.7.refs_4_ = f32[4224,256]{1,0:T(8,128)S(1)} custom-call(bf16[1552,128]{1,0:T(8,128)(2,1)S(1)} %collective-permute-done.3.refs_0_, bf16[1552,128]{1,0:T(8,128)(2,1)S(1)} %collective-permute-done.4.refs_1_, bf16[1552,128]{1,0:T(8,128)(2,1)S(1)} %collective-permute-done.5.refs_2_, ...), custom_call_target="tpu_custom_call", output_to_operand_aliasing={{}: (4, {})} | custom-call | flops 301989888 | bytes 1191936 | tf_op jit(solution)/shard_map/fold/pallas_call | solution.py:216
  63.6 1.6 %fold.8.refs_4_ = f32[4224,256]{1,0:T(8,128)S(1)} custom-call(bf16[1552,128]{1,0:T(8,128)(2,1)S(1)} %collective-permute-done.6.refs_0_, bf16[1552,128]{1,0:T(8,128)(2,1)S(1)} %collective-permute-done.7.refs_1_, bf16[1552,128]{1,0:T(8,128)(2,1)S(1)} %collective-permute-done.8.refs_2_, ...), custom_call_target="tpu_custom_call", output_to_operand_aliasing={{}: (4, {})} | custom-call | flops 301989888 | bytes 1191936 | tf_op jit(solution)/shard_map/fold/pallas_call | solution.py:216
  65.2 1.6 %fold.9.refs_4_ = f32[4224,256]{1,0:T(8,128)S(1)} custom-call(bf16[1552,128]{1,0:T(8,128)(2,1)S(1)} %collective-permute-done.10.refs_0_, bf16[1552,128]{1,0:T(8,128)(2,1)S(1)} %collective-permute-done.11.refs_1_, bf16[1552,128]{1,0:T(8,128)(2,1)S(1)} %collective-permute-done.12.refs_2_, ...), custom_call_target="tpu_custom_call", output_to_operand_aliasing={{}: (4, {})} | custom-call | flops 301989888 | bytes 1191936 | tf_op jit(solution)/shard_map/fold/pallas_call | solution.py:216
  66.8 0.0 collective-permute-done.9.refs_0_
  66.8 0.0 collective-permute-done.13.refs_1_
  66.8 0.5 collective-permute-done.14.refs_2_
  67.3 3.6 %last.1 = (f32[4224,256]{1,0:T(8,128)S(1)}, f32[4096,256]{1,0:T(8,128)}) custom-call(bf16[1552,128]{1,0:T(8,128)(2,1)S(1)} %collective-permute-done.9.refs_0_, bf16[1552,128]{1,0:T(8,128)(2,1)S(1)} %collective-permute-done.13.refs_1_, bf16[1552,128]{1,0:T(8,128)(2,1)S(1)} %collective-permute-done.14.refs_2_, ...), custom_call_target="tpu_custom_call", output_to_operand_aliasing={{0}: (4, {})} | custom-call | flops 301989888 | bytes 1191936 | tf_op jit(solution)/shard_map/last/pallas_call | solution.py:204
  (1 shorter events, 0.0 us)
Async XLA Ops:
  0.7 1.0 %copy-start.1 = (bf16[2,1,6,128,128]{4,3,2,1,0:T(8,128)(2,1)S(1)}, bf16[2,1,6,128,128]{4,3,2,1,0:T(8,128)(2,1)}, u32[]{:S(2)}) copy-start(bf16[2,1,6,128,128]{4,3,2,1,0:T(8,128)(2,1)} %param.5) | copy-start | bytes 1179652
  1.7 0.7 copy-start.2
  2.4 0.7 copy-start.3
  3.9 12.2 %collective-permute-start = (bf16[1552,128]{1,0:T(8,128)(2,1)S(1)}, bf16[1552,128]{1,0:T(8,128)(2,1)S(1)}, u32[]{:S(2)}, u32[]{:S(2)}) collective-permute-start(bf16[1552,128]{1,0:T(8,128)(2,1)S(1)} %pack.1.refs_0_), channel_id=1, source_target_pairs={{0,1},{1,0},{2,3},{3,2},{4,5},{5,4},{6,7},{7,6},{8,9},{9,8},{10,11... | collective-permute-start | bytes 1191944 | tf_op jit(solution)/shard_map/ppermute | solution.py:42
  6.9 10.7 %collective-permute-start.1 = (bf16[1552,128]{1,0:T(8,128)(2,1)S(1)}, bf16[1552,128]{1,0:T(8,128)(2,1)S(1)}, u32[]{:S(2)}, u32[]{:S(2)}) collective-permute-start(bf16[1552,128]{1,0:T(8,128)(2,1)S(1)} %pack.1.refs_0_), channel_id=1, source_target_pairs={{0,2},{1,3},{2,0},{3,1},{4,6},{5,7},{6,4},{7,5},{8,10},{9,11},{10,... | collective-permute-start | bytes 1191944 | tf_op jit(solution)/shard_map/ppermute | solution.py:42
  8.4 12.2 %collective-permute-start.2 = (bf16[1552,128]{1,0:T(8,128)(2,1)S(1)}, bf16[1552,128]{1,0:T(8,128)(2,1)S(1)}, u32[]{:S(2)}, u32[]{:S(2)}) collective-permute-start(bf16[1552,128]{1,0:T(8,128)(2,1)S(1)} %pack.1.refs_0_), channel_id=1, source_target_pairs={{0,4},{1,5},{2,6},{3,7},{4,8},{5,9},{6,10},{7,11},{8,12},{9,13},{1... | collective-permute-start | bytes 1191944 | tf_op jit(solution)/shard_map/ppermute | solution.py:42
  20.7 11.3 %collective-permute-start.3 = (bf16[1552,128]{1,0:T(8,128)(2,1)S(1)}, bf16[1552,128]{1,0:T(8,128)(2,1)S(1)}, u32[]{:S(2)}, u32[]{:S(2)}) collective-permute-start(bf16[1552,128]{1,0:T(8,128)(2,1)S(1)} %collective-permute-done.2.refs_2_), channel_id=1, source_target_pairs={{0,4},{1,5},{2,6},{3,7},{4,8},{5,9},{6,10},{7,11},{8,12},{9,13},{1... | collective-permute-start | bytes 1191944 | tf_op jit(solution)/shard_map/ppermute | solution.py:42
  20.7 11.3 %collective-permute-start.5 = (bf16[1552,128]{1,0:T(8,128)(2,1)S(1)}, bf16[1552,128]{1,0:T(8,128)(2,1)S(1)}, u32[]{:S(2)}, u32[]{:S(2)}) collective-permute-start(bf16[1552,128]{1,0:T(8,128)(2,1)S(1)} %collective-permute-done.2.refs_2_), channel_id=1, source_target_pairs={{0,2},{1,3},{2,0},{3,1},{4,6},{5,7},{6,4},{7,5},{8,10},{9,11},{10,... | collective-permute-start | bytes 1191944 | tf_op jit(solution)/shard_map/ppermute | solution.py:42
  21.2 10.8 %collective-permute-start.4 = (bf16[1552,128]{1,0:T(8,128)(2,1)S(1)}, bf16[1552,128]{1,0:T(8,128)(2,1)S(1)}, u32[]{:S(2)}, u32[]{:S(2)}) collective-permute-start(bf16[1552,128]{1,0:T(8,128)(2,1)S(1)} %collective-permute-done.1.refs_1_), channel_id=1, source_target_pairs={{0,1},{1,0},{2,3},{3,2},{4,5},{5,4},{6,7},{7,6},{8,9},{9,8},{10,11... | collective-permute-start | bytes 1191944 | tf_op jit(solution)/shard_map/ppermute | solution.py:42
  32.0 13.9 %collective-permute-start.6 = (bf16[1552,128]{1,0:T(8,128)(2,1)S(1)}, bf16[1552,128]{1,0:T(8,128)(2,1)S(1)}, u32[]{:S(2)}, u32[]{:S(2)}) collective-permute-start(bf16[1552,128]{1,0:T(8,128)(2,1)S(1)} %collective-permute-done.3.refs_0_), channel_id=1, source_target_pairs={{0,4},{1,5},{2,6},{3,7},{4,8},{5,9},{6,10},{7,11},{8,12},{9,13},{1... | collective-permute-start | bytes 1191944 | tf_op jit(solution)/shard_map/ppermute | solution.py:42
  32.0 13.9 %collective-permute-start.8 = (bf16[1552,128]{1,0:T(8,128)(2,1)S(1)}, bf16[1552,128]{1,0:T(8,128)(2,1)S(1)}, u32[]{:S(2)}, u32[]{:S(2)}) collective-permute-start(bf16[1552,128]{1,0:T(8,128)(2,1)S(1)} %collective-permute-done.3.refs_0_), channel_id=1, source_target_pairs={{0,2},{1,3},{2,0},{3,1},{4,6},{5,7},{6,4},{7,5},{8,10},{9,11},{10,... | collective-permute-start | bytes 1191944 | tf_op jit(solution)/shard_map/ppermute | solution.py:42
  32.9 13.1 %collective-permute-start.7 = (bf16[1552,128]{1,0:T(8,128)(2,1)S(1)}, bf16[1552,128]{1,0:T(8,128)(2,1)S(1)}, u32[]{:S(2)}, u32[]{:S(2)}) collective-permute-start(bf16[1552,128]{1,0:T(8,128)(2,1)S(1)} %collective-permute-done.5.refs_2_), channel_id=1, source_target_pairs={{0,1},{1,0},{2,3},{3,2},{4,5},{5,4},{6,7},{7,6},{8,9},{9,8},{10,11... | collective-permute-start | bytes 1191944 | tf_op jit(solution)/shard_map/ppermute | solution.py:42
  33.4 24.2 %collective-permute-start.15 = (bf16[2,1024,256]{2,1,0:T(8,128)(2,1)}, bf16[2,1024,256]{2,1,0:T(8,128)(2,1)S(1)}, u32[]{:S(2)}, u32[]{:S(2)}) collective-permute-start(bf16[2,1024,256]{2,1,0:T(8,128)(2,1)} %refs_0_.1), channel_id=1, source_target_pairs={{0,16},{16,0},{1,17},{17,1},{2,18},{18,2},{3,19},{19,3},{4,20},{20... | collective-permute-start | bytes 3145736 | tf_op jit(solution)/shard_map/ppermute | solution.py:235
  33.4 17.5 %collective-permute-start.12 = (bf16[1552,128]{1,0:T(8,128)(2,1)S(1)}, bf16[1552,128]{1,0:T(8,128)(2,1)S(1)}, u32[]{:S(2)}, u32[]{:S(2)}) collective-permute-start(bf16[1552,128]{1,0:T(8,128)(2,1)S(1)} %collective-permute-done.refs_0_), channel_id=1, source_target_pairs={{0,4},{1,5},{2,6},{3,7},{4,8},{5,9},{6,10},{7,11},{8,12},{9,13},{1... | collective-permute-start | bytes 1191944 | tf_op jit(solution)/shard_map/ppermute | solution.py:42
  45.9 8.4 %collective-permute-start.10 = (bf16[1552,128]{1,0:T(8,128)(2,1)S(1)}, bf16[1552,128]{1,0:T(8,128)(2,1)S(1)}, u32[]{:S(2)}, u32[]{:S(2)}) collective-permute-start(bf16[1552,128]{1,0:T(8,128)(2,1)S(1)} %collective-permute-done.6.refs_0_), channel_id=1, source_target_pairs={{0,1},{1,0},{2,3},{3,2},{4,5},{5,4},{6,7},{7,6},{8,9},{9,8},{10,11... | collective-permute-start | bytes 1191944 | tf_op jit(solution)/shard_map/ppermute | solution.py:42
  46.0 11.7 %collective-permute-start.11 = (bf16[1552,128]{1,0:T(8,128)(2,1)S(1)}, bf16[1552,128]{1,0:T(8,128)(2,1)S(1)}, u32[]{:S(2)}, u32[]{:S(2)}) collective-permute-start(bf16[1552,128]{1,0:T(8,128)(2,1)S(1)} %collective-permute-done.6.refs_0_), channel_id=1, source_target_pairs={{0,2},{1,3},{2,0},{3,1},{4,6},{5,7},{6,4},{7,5},{8,10},{9,11},{10,... | collective-permute-start | bytes 1191944 | tf_op jit(solution)/shard_map/ppermute | solution.py:42
  46.5 20.3 %collective-permute-start.9 = (bf16[1552,128]{1,0:T(8,128)(2,1)S(1)}, bf16[1552,128]{1,0:T(8,128)(2,1)S(1)}, u32[]{:S(2)}, u32[]{:S(2)}) collective-permute-start(bf16[1552,128]{1,0:T(8,128)(2,1)S(1)} %collective-permute-done.8.refs_2_), channel_id=1, source_target_pairs={{0,1},{1,0},{2,3},{3,2},{4,5},{5,4},{6,7},{7,6},{8,9},{9,8},{10,11... | collective-permute-start | bytes 1191944 | tf_op jit(solution)/shard_map/ppermute | solution.py:42
  57.7 9.1 %collective-permute-start.13 = (bf16[1552,128]{1,0:T(8,128)(2,1)S(1)}, bf16[1552,128]{1,0:T(8,128)(2,1)S(1)}, u32[]{:S(2)}, u32[]{:S(2)}) collective-permute-start(bf16[1552,128]{1,0:T(8,128)(2,1)S(1)} %collective-permute-done.10.refs_0_), channel_id=1, source_target_pairs={{0,2},{1,3},{2,0},{3,1},{4,6},{5,7},{6,4},{7,5},{8,10},{9,11},{10,... | collective-permute-start | bytes 1191944 | tf_op jit(solution)/shard_map/ppermute | solution.py:42
  57.7 9.6 %collective-permute-start.14 = (bf16[1552,128]{1,0:T(8,128)(2,1)S(1)}, bf16[1552,128]{1,0:T(8,128)(2,1)S(1)}, u32[]{:S(2)}, u32[]{:S(2)}) collective-permute-start(bf16[1552,128]{1,0:T(8,128)(2,1)S(1)} %collective-permute-done.12.refs_2_), channel_id=1, source_target_pairs={{0,4},{1,5},{2,6},{3,7},{4,8},{5,9},{6,10},{7,11},{8,12},{9,13},{1... | collective-permute-start | bytes 1191944 | tf_op jit(solution)/shard_map/ppermute | solution.py:42
  57.7 1.2 %copy-start = (bf16[2,1024,256]{2,1,0:T(8,128)(2,1)S(1)}, bf16[2,1024,256]{2,1,0:T(8,128)(2,1)}, u32[]{:S(2)}) copy-start(bf16[2,1024,256]{2,1,0:T(8,128)(2,1)} %refs_0_.1) | copy-start | bytes 3145732

commit v2 on v1

--- a/solution.py
+++ b/solution.py
@@ -30,84 +30,113 @@
     return tuple(reversed(parts))
 
 
-def hop(dims, axis, unit):
+def hop(dims, axis, sign, unit):
     n_col = 1
     for size in dims:
         n_col *= size
+    size = dims[axis]
     pairs = []
     for index in range(n_col):
         at = list(unflat(dims, index))
-        at[axis] += 1
+        at[axis] = (at[axis] + sign) % size
         pairs.append((index, flat(dims, at)))
     return lax.ppermute(unit, "col", pairs)
 
 
-def back(dims, axis, offset):
+def source(dims, offset, axis, sign):
     at = list(offset)
-    at[axis] = (at[axis] - 1) % dims[axis]
+    at[axis] = (at[axis] - sign) % dims[axis]
     return tuple(at)
 
 
 def gather_plan(dims):
     if dims == (4, 2, 2):
         return [
-            [((0, 0, 1), 2), ((0, 1, 0), 1), ((1, 0, 0), 0)],
-            [((2, 0, 0), 0), ((0, 1, 1), 2), ((1, 1, 0), 1)],
-            [((3, 0, 0), 0), ((1, 1, 1), 2), ((2, 1, 0), 1)],
-            [((3, 0, 1), 2), ((3, 1, 0), 1), ((1, 0, 1), 0)],
-            [((2, 1, 1), 2), ((3, 1, 1), 1), ((2, 0, 1), 0)],
+            ((1, 0, 0), 0, 1),
+            ((0, 1, 0), 1, 1),
+            ((0, 0, 1), 2, 1),
+            [(0, 0, 0)],
+            ((3, 0, 0), 0, -1),
+            ((1, 0, 1), 2, 1),
+            ((1, 1, 0), 1, 1),
+            ((2, 0, 0), 0, 1),
+            [(1, 0, 0), (0, 1, 0), (0, 0, 1)],
+            ((3, 0, 1), 2, 1),
+            ((3, 1, 0), 1, 1),
+            ((2, 0, 1), 0, 1),
+            ((1, 1, 1), 2, 1),
+            ((0, 1, 1), 1, 1),
+            ((2, 1, 0), 0, 1),
+            [(3, 0, 0), (1, 0, 1), (1, 1, 0)],
+            ((3, 1, 1), 2, 1),
+            [(2, 0, 0), (3, 0, 1), (3, 1, 0)],
+            ((2, 1, 1), 1, 1),
+            [(2, 0, 1), (1, 1, 1), (0, 1, 1)],
         ]
     total = 1
     for size in dims:
         total *= size
     held = {(0,) * len(dims)}
-    slots = []
+    plan = []
+    ready = list(held)
     while len(held) < total:
-        slot = []
-        taken = set()
+        taken = []
         for axis in range(len(dims)):
             for index in range(1, total):
                 offset = unflat(dims, index)
-                if offset not in held and offset not in taken and back(dims, axis, offset) in held:
-                    slot.append((offset, axis))
-                    taken.add(offset)
+                if offset not in held and offset not in taken and source(dims, offset, axis, 1) in held:
+                    plan.append((offset, axis, 1))
+                    taken.append(offset)
                     break
-        held |= taken
-        slots.append(slot)
-    return slots
-
-
-def pack_kernel(rows_ref, cols_ref, counts_ref, tiles_ref, unit_ref, sem):
+        plan.append(ready)
+        held.update(taken)
+        ready = taken
+    return plan
+
+
+def pack_kernel(rows_hbm, cols_hbm, counts_hbm, tiles_ref, unit_ref, rows_ref, cols_ref, counts_ref, sem):
     steps, _, per_dev = rows_ref.shape
     body = tiles_ref.shape[0]
-    copy = pltpu.make_async_copy(tiles_ref, unit_ref.at[pl.ds(0, body)], sem)
-    copy.start()
+    copies = [
+        pltpu.make_async_copy(tiles_ref, unit_ref.at[pl.ds(0, body)], sem.at[0]),
+        pltpu.make_async_copy(rows_hbm, rows_ref, sem.at[1]),
+        pltpu.make_async_copy(cols_hbm, cols_ref, sem.at[2]),
+        pltpu.make_async_copy(counts_hbm, counts_ref, sem.at[3]),
+    ]
+    for copy in copies:
+        copy.start()
+    for copy in copies[1:]:
+        copy.wait()
     lane = lax.broadcasted_iota(jnp.int32, (META, 128), 1)
     meta = jnp.zeros((META, 128), jnp.int32)
     n_slots = steps * per_dev
     for step in range(steps):
         for q in range(per_dev):
             at = step * per_dev + q
-            row = jnp.where(q < counts_ref[step, 0, 0], rows_ref[step, 0, q], RB_DEV)
+            row = jnp.where(q < counts_ref[step], rows_ref[step, 0, q], RB_DEV)
             meta = jnp.where(lane == at, row, meta)
             meta = jnp.where(lane == n_slots + at, cols_ref[step, 0, q], meta)
     unit_ref[pl.ds(body, META), :] = meta.astype(jnp.float32).astype(jnp.bfloat16)
-    copy.wait()
+    copies[0].wait()
 
 
 def pack(rows, cols, counts, tiles):
     steps, _, per_dev, size, _ = tiles.shape
     body = steps * per_dev * size
-    smem = pl.BlockSpec(memory_space=pltpu.SMEM)
     return pl.pallas_call(
         pack_kernel,
         out_shape=jax.ShapeDtypeStruct((body + META, size), jnp.bfloat16),
-        in_specs=[smem, smem, smem, pl.BlockSpec(memory_space=pl.ANY)],
+        in_specs=[pl.BlockSpec(memory_space=pltpu.HBM)] * 4,
         out_specs=pl.BlockSpec(memory_space=pltpu.VMEM),
-        scratch_shapes=[pltpu.SemaphoreType.DMA],
+        scratch_shapes=[
+            pltpu.SMEM(rows.shape, jnp.int32),
+            pltpu.SMEM(cols.shape, jnp.int32),
+            pltpu.SMEM((steps,), jnp.int32),
+            pltpu.SemaphoreType.DMA((4,)),
+        ],
         compiler_params=pltpu.CompilerParams(vmem_limit_bytes=2 << 20),
         name="pack",
-    )(rows, cols, counts, tiles.reshape(body, size))
+    )(*(pltpu.with_memory_space_constraint(x, pltpu.HBM) for x in (rows, cols, counts.reshape(steps), tiles.reshape(body, size))))
 
 
 def panel_kernel(*refs, n_row):
@@ -141,12 +170,12 @@
             pltpu.VMEM((steps, n_row * depth, scen), jnp.bfloat16),
             pltpu.VMEM(((RB_DEV + 1) * size, scen), jnp.float32),
         ),
-        in_specs=[pl.BlockSpec(memory_space=pl.ANY)] * n_row,
+        in_specs=[pl.BlockSpec(memory_space=pltpu.HBM)] + [pl.BlockSpec(memory_space=pl.ANY)] * (n_row - 1),
         out_specs=(pl.BlockSpec(memory_space=pltpu.VMEM),) * 2,
         scratch_shapes=[pltpu.SemaphoreType.DMA((n_row * steps,))],
         compiler_params=pltpu.CompilerParams(vmem_limit_bytes=2 << 20),
         name="panels",
-    )(*pieces)
+    )(pltpu.with_memory_space_constraint(pieces[0], pltpu.HBM), *pieces[1:])
 
 
 def add_units(n, steps, size, unit_refs, panel_ref, acc_ref, meta_ref, index_ref, sem):
@@ -235,18 +264,23 @@
         pieces.append(lax.ppermute(pieces[-1], "row", ring))
     own = pack(block_rows, block_cols, live_counts, tiles)
     held = {(0,) * len(dims): own}
-    waiting = [own]
-    acc = None
-    for slot in gather_plan(dims):
-        arrived = tuple(hop(dims, axis, held[back(dims, axis, offset)]) for offset, axis in slot)
-        if acc is None:
-            whole, acc = whole_panels(pieces, size)
-        acc = fold(waiting, whole, acc, False)
-        arrived = lax.optimization_barrier(arrived)
-        for (offset, _), unit in zip(slot, arrived):
-            held[offset] = unit
-        waiting = list(arrived)
-    return fold(waiting, whole, acc, True)
+    seen = set(held)
+    folded = set()
+    whole, acc = whole_panels(pieces, size)
+    for step in gather_plan(dims):
+        if isinstance(step, list):
+            acc = fold([held[key] for key in step], whole, acc, False)
+            folded.update(step)
+            continue
+        offset, axis, sign = step
+        origin = source(dims, offset, axis, sign)
+        seen.add(origin)
+        keys = [key for key in held if key in seen]
+        if folded:
+            *tied, acc = lax.optimization_barrier((*(held[key] for key in keys), acc))
+            held.update(zip(keys, tied))
+        held[offset] = hop(dims, axis, sign, held[origin])
+    return fold([held[key] for key in held if key not in folded], whole, acc, True)
 
 
 def solution(mesh):

time: 71.1 us -> 61.7 us (0.87)
  waiting for transfers between devices: 42 us -> 19.3 us
  starting transfers between devices: 12.2 us -> 28.9 us
  local copies, waits for them, and re-layouts: 4.31 us -> 0 us
  Pallas kernels: 12.2 us -> 13.2 us
    ppermute x15, waiting for transfers between devices: 42 us -> 19.3 us  [hop(): return lax.ppermute(unit, 'col', pairs)]
    ppermute x15, starting transfers between devices: 12.2 us -> 28.5 us  [hop(): return lax.ppermute(unit, 'col', pairs)]
    unnamed x9 -> x0, local copies, waits for them, and re-layouts: 4.31 us -> none
    pallas_call x1, Pallas kernels: 0.46 us -> 1.24 us  [whole_panels(): pl.pallas_call(functools.partial(panel_kernel, n_row=n_row), out_shape=(p...]
  transfers between devices with their start and end apart: 16 -> 16, of which waited for: 9 -> 7; matrix products, arithmetic and copies ran while one was open for 0% -> 0% of each run, Pallas kernels for 11% -> 16%
where the time goes in v2:
time: 61.7 us; the launch traced here: 61.5 us
  starting transfers between devices  28.9 us (47%)
  waiting for transfers between devices  19.3 us (31%)
  Pallas kernels  13.2 us (21%)
    ppermute x15, starting transfers between devices, hop(): return lax.ppermute(unit, 'col', pairs)  28.5 us
    ppermute x15, waiting for transfers between devices, hop(): return lax.ppermute(unit, 'col', pairs)  19.3 us
    pallas_call x5, Pallas kernels, fold(): pl.pallas_call(functools.partial(fold_kernel, n=n, steps=steps, size=size...  7.35 us
    pallas_call x1, Pallas kernels, fold(): pl.pallas_call(functools.partial(last_kernel, n=n, steps=steps, size=size...  3.58 us
    pallas_call x1, Pallas kernels, whole_panels(): pl.pallas_call(functools.partial(panel_kernel, n_row=n_row), out_shape=(p...  1.24 us
  transfers between devices with their start and end apart: 16, of which 7 were waited for; matrix products, arithmetic and copies ran while one was open for 0% of the time, Pallas kernels for 16%

profile of v2, /device:TPU:0, one launch (start us, length us, event | category | flops | bytes accessed | tf_op | source)
XLA Modules:
  0.0 61.5 jit_solution(5232933756060518396)
XLA Ops:
  0.0 0.5 collective-permute-start.1
  0.5 1.0 %pack.1.refs_0_ = bf16[1552,128]{1,0:T(8,128)(2,1)S(1)} custom-call(s32[2,1,6]{2,1,0:T(1,128)} %rows_hbm.1, s32[2,1,6]{2,1,0:T(1,128)} %cols_hbm.1, s32[2]{0:T(128)} %bitcast.3, bf16[1536,128]{1,0:T(8,128)(2,1)} %bitcast.2), custom_call_target="tpu_custom_call" | custom-call | tf_op jit(solution)/shard_map/pack/pallas_call | solution.py:126
  1.5 2.6 %collective-permute-start.2 = (bf16[1552,128]{1,0:T(8,128)(2,1)S(1)}, bf16[1552,128]{1,0:T(8,128)(2,1)S(1)}, u32[]{:S(2)}, u32[]{:S(2)}) collective-permute-start(bf16[1552,128]{1,0:T(8,128)(2,1)S(1)} %pack.1.refs_0_), channel_id=1, source_target_pairs={{0,4},{1,5},{2,6},{3,7},{4,8},{5,9},{6,10},{7,11},{8,12},{9,13},{1... | collective-permute-start | bytes 1191944 | tf_op jit(solution)/shard_map/ppermute | solution.py:43
  4.1 1.5 %collective-permute-start.4 = (bf16[1552,128]{1,0:T(8,128)(2,1)S(1)}, bf16[1552,128]{1,0:T(8,128)(2,1)S(1)}, u32[]{:S(2)}, u32[]{:S(2)}) collective-permute-start(bf16[1552,128]{1,0:T(8,128)(2,1)S(1)} %pack.1.refs_0_), channel_id=1, source_target_pairs={{0,2},{1,3},{2,0},{3,1},{4,6},{5,7},{6,4},{7,5},{8,10},{9,11},{10,... | collective-permute-start | bytes 1191944 | tf_op jit(solution)/shard_map/ppermute | solution.py:43
  5.6 1.5 %collective-permute-start = (bf16[1552,128]{1,0:T(8,128)(2,1)S(1)}, bf16[1552,128]{1,0:T(8,128)(2,1)S(1)}, u32[]{:S(2)}, u32[]{:S(2)}) collective-permute-start(bf16[1552,128]{1,0:T(8,128)(2,1)S(1)} %pack.1.refs_0_), channel_id=1, source_target_pairs={{0,1},{1,0},{2,3},{3,2},{4,5},{5,4},{6,7},{7,6},{8,9},{9,8},{10,11... | collective-permute-start | bytes 1191944 | tf_op jit(solution)/shard_map/ppermute | solution.py:43
  7.1 0.0 collective-permute-done.1.refs_1_
  7.1 1.2 %panels.1 = (bf16[2,2048,256]{2,1,0:T(8,128)(2,1)S(1)}, f32[4224,256]{1,0:T(8,128)S(1)}) custom-call(bf16[2,1024,256]{2,1,0:T(8,128)(2,1)} %refs_0_.1, bf16[2,1024,256]{2,1,0:T(8,128)(2,1)S(1)} %collective-permute-done.1.refs_1_), custom_call_target="tpu_custom_call" | custom-call | tf_op jit(solution)/shard_map/panels/pallas_call | solution.py:167
  8.4 1.0 %fold.5.refs_4_ = f32[4224,256]{1,0:T(8,128)S(1)} custom-call(bf16[1552,128]{1,0:T(8,128)(2,1)S(1)} %pack.1.refs_0_, bf16[2,2048,256]{2,1,0:T(8,128)(2,1)S(1)} %get-tuple-element.49.refs_1_.refs_3_, f32[4224,256]{1,0:T(8,128)S(1)} %get-tuple-element.50.refs_2_), custom_call_target="tpu_custom_call", output_to_operand_aliasing={{}: (2, {})} | custom-call | flops 100663296 | bytes 397312 | tf_op jit(solution)/shard_map/fold/pallas_call | solution.py:245
  9.4 2.3 %collective-permute-start.3 = (bf16[1552,128]{1,0:T(8,128)(2,1)S(1)}, bf16[1552,128]{1,0:T(8,128)(2,1)S(1)}, u32[]{:S(2)}, u32[]{:S(2)}) collective-permute-start(bf16[1552,128]{1,0:T(8,128)(2,1)S(1)} %pack.1.refs_0_), channel_id=1, source_target_pairs={{0,12},{1,13},{2,14},{3,15},{4,0},{5,1},{6,2},{7,3},{8,4},{9,5},{1... | collective-permute-start | bytes 1191944 | tf_op jit(solution)/shard_map/ppermute | solution.py:43
  11.7 4.5 %collective-permute-done.2.refs_0_ = bf16[1552,128]{1,0:T(8,128)(2,1)S(1)} collective-permute-done((bf16[1552,128]{1,0:T(8,128)(2,1)S(1)}, bf16[1552,128]{1,0:T(8,128)(2,1)S(1)}, u32[]{:S(2)}, u32[]{:S(2)}) %collective-permute-start.2) | collective-permute-done | bytes 397344 | tf_op jit(solution)/shard_map/ppermute | solution.py:43
  16.2 1.6 %collective-permute-start.5 = (bf16[1552,128]{1,0:T(8,128)(2,1)S(1)}, bf16[1552,128]{1,0:T(8,128)(2,1)S(1)}, u32[]{:S(2)}, u32[]{:S(2)}) collective-permute-start(bf16[1552,128]{1,0:T(8,128)(2,1)S(1)} %collective-permute-done.2.refs_0_), channel_id=1, source_target_pairs={{0,1},{1,0},{2,3},{3,2},{4,5},{5,4},{6,7},{7,6},{8,9},{9,8},{10,11... | collective-permute-start | bytes 1191944 | tf_op jit(solution)/shard_map/ppermute | solution.py:43
  17.9 1.5 %collective-permute-start.6 = (bf16[1552,128]{1,0:T(8,128)(2,1)S(1)}, bf16[1552,128]{1,0:T(8,128)(2,1)S(1)}, u32[]{:S(2)}, u32[]{:S(2)}) collective-permute-start(bf16[1552,128]{1,0:T(8,128)(2,1)S(1)} %collective-permute-done.2.refs_0_), channel_id=1, source_target_pairs={{0,2},{1,3},{2,0},{3,1},{4,6},{5,7},{6,4},{7,5},{8,10},{9,11},{10,... | collective-permute-start | bytes 1191944 | tf_op jit(solution)/shard_map/ppermute | solution.py:43
  19.4 0.0 collective-permute-done.4.refs_1_
  19.4 0.0 collective-permute-done.refs_2_
  19.4 1.6 %fold.6.refs_4_ = f32[4224,256]{1,0:T(8,128)S(1)} custom-call(bf16[1552,128]{1,0:T(8,128)(2,1)S(1)} %collective-permute-done.2.refs_0_, bf16[1552,128]{1,0:T(8,128)(2,1)S(1)} %collective-permute-done.4.refs_1_, bf16[1552,128]{1,0:T(8,128)(2,1)S(1)} %collective-permute-done.refs_2_, ...), custom_call_target="tpu_custom_call", output_to_operand_aliasing={{}: (4, {})} | custom-call | flops 301989888 | bytes 1191936 | tf_op jit(solution)/shard_map/fold/pallas_call | solution.py:245
  21.0 3.5 %collective-permute-done.3.refs_0_ = bf16[1552,128]{1,0:T(8,128)(2,1)S(1)} collective-permute-done((bf16[1552,128]{1,0:T(8,128)(2,1)S(1)}, bf16[1552,128]{1,0:T(8,128)(2,1)S(1)}, u32[]{:S(2)}, u32[]{:S(2)}) %collective-permute-start.3) | collective-permute-done | bytes 397344 | tf_op jit(solution)/shard_map/ppermute | solution.py:43
  24.5 1.5 %collective-permute-start.8 = (bf16[1552,128]{1,0:T(8,128)(2,1)S(1)}, bf16[1552,128]{1,0:T(8,128)(2,1)S(1)}, u32[]{:S(2)}, u32[]{:S(2)}) collective-permute-start(bf16[1552,128]{1,0:T(8,128)(2,1)S(1)} %collective-permute-done.3.refs_0_), channel_id=1, source_target_pairs={{0,2},{1,3},{2,0},{3,1},{4,6},{5,7},{6,4},{7,5},{8,10},{9,11},{10,... | collective-permute-start | bytes 1191944 | tf_op jit(solution)/shard_map/ppermute | solution.py:43
  26.1 0.6 collective-permute-start.11
  26.6 1.5 %collective-permute-start.12 = (bf16[1552,128]{1,0:T(8,128)(2,1)S(1)}, bf16[1552,128]{1,0:T(8,128)(2,1)S(1)}, u32[]{:S(2)}, u32[]{:S(2)}) collective-permute-start(bf16[1552,128]{1,0:T(8,128)(2,1)S(1)} %collective-permute-done.3.refs_0_), channel_id=1, source_target_pairs={{0,1},{1,0},{2,3},{3,2},{4,5},{5,4},{6,7},{7,6},{8,9},{9,8},{10,11... | collective-permute-start | bytes 1191944 | tf_op jit(solution)/shard_map/ppermute | solution.py:43
  28.1 0.0 collective-permute-done.5.refs_1_
  28.1 3.5 %collective-permute-start.10 = (bf16[1552,128]{1,0:T(8,128)(2,1)S(1)}, bf16[1552,128]{1,0:T(8,128)(2,1)S(1)}, u32[]{:S(2)}, u32[]{:S(2)}) collective-permute-start(bf16[1552,128]{1,0:T(8,128)(2,1)S(1)} %collective-permute-done.5.refs_1_), channel_id=1, source_target_pairs={{0,4},{1,5},{2,6},{3,7},{4,8},{5,9},{6,10},{7,11},{8,12},{9,13},{1... | collective-permute-start | bytes 1191944 | tf_op jit(solution)/shard_map/ppermute | solution.py:43
  31.6 0.0 collective-permute-done.6.refs_2_
  31.6 5.2 %collective-permute-start.7 = (bf16[1552,128]{1,0:T(8,128)(2,1)S(1)}, bf16[1552,128]{1,0:T(8,128)(2,1)S(1)}, u32[]{:S(2)}, u32[]{:S(2)}) collective-permute-start(bf16[1552,128]{1,0:T(8,128)(2,1)S(1)} %collective-permute-done.6.refs_2_), channel_id=1, source_target_pairs={{0,4},{1,5},{2,6},{3,7},{4,8},{5,9},{6,10},{7,11},{8,12},{9,13},{1... | collective-permute-start | bytes 1191944 | tf_op jit(solution)/shard_map/ppermute | solution.py:43
  36.8 1.6 %fold.7.refs_4_ = f32[4224,256]{1,0:T(8,128)S(1)} custom-call(bf16[1552,128]{1,0:T(8,128)(2,1)S(1)} %collective-permute-done.3.refs_0_, bf16[1552,128]{1,0:T(8,128)(2,1)S(1)} %collective-permute-done.5.refs_1_, bf16[1552,128]{1,0:T(8,128)(2,1)S(1)} %collective-permute-done.6.refs_2_, ...), custom_call_target="tpu_custom_call", output_to_operand_aliasing={{}: (4, {})} | custom-call | flops 301989888 | bytes 1191936 | tf_op jit(solution)/shard_map/fold/pallas_call | solution.py:245
  38.4 0.0 collective-permute-done.8.refs_2_
  38.4 1.6 %collective-permute-start.14 = (bf16[1552,128]{1,0:T(8,128)(2,1)S(1)}, bf16[1552,128]{1,0:T(8,128)(2,1)S(1)}, u32[]{:S(2)}, u32[]{:S(2)}) collective-permute-start(bf16[1552,128]{1,0:T(8,128)(2,1)S(1)} %collective-permute-done.6.refs_2_), channel_id=1, source_target_pairs={{0,1},{1,0},{2,3},{3,2},{4,5},{5,4},{6,7},{7,6},{8,9},{9,8},{10,11... | collective-permute-start | bytes 1191944 | tf_op jit(solution)/shard_map/ppermute | solution.py:43
  39.9 1.6 %collective-permute-done.11.refs_0_ = bf16[1552,128]{1,0:T(8,128)(2,1)S(1)} collective-permute-done((bf16[1552,128]{1,0:T(8,128)(2,1)S(1)}, bf16[1552,128]{1,0:T(8,128)(2,1)S(1)}, u32[]{:S(2)}, u32[]{:S(2)}) %collective-permute-start.11) | collective-permute-done | bytes 397344 | tf_op jit(solution)/shard_map/ppermute | solution.py:43
  41.6 1.5 %collective-permute-start.15 = (bf16[1552,128]{1,0:T(8,128)(2,1)S(1)}, bf16[1552,128]{1,0:T(8,128)(2,1)S(1)}, u32[]{:S(2)}, u32[]{:S(2)}) collective-permute-start(bf16[1552,128]{1,0:T(8,128)(2,1)S(1)} %collective-permute-done.refs_2_), channel_id=1, source_target_pairs={{0,2},{1,3},{2,0},{3,1},{4,6},{5,7},{6,4},{7,5},{8,10},{9,11},{10,... | collective-permute-start | bytes 1191944 | tf_op jit(solution)/shard_map/ppermute | solution.py:43
  43.1 0.0 collective-permute-done.12.refs_1_
  43.1 0.5 collective-permute-start.9
  43.6 1.6 %fold.8.refs_4_ = f32[4224,256]{1,0:T(8,128)S(1)} custom-call(bf16[1552,128]{1,0:T(8,128)(2,1)S(1)} %collective-permute-done.11.refs_0_, bf16[1552,128]{1,0:T(8,128)(2,1)S(1)} %collective-permute-done.12.refs_1_, bf16[1552,128]{1,0:T(8,128)(2,1)S(1)} %collective-permute-done.8.refs_2_, ...), custom_call_target="tpu_custom_call", output_to_operand_aliasing={{}: (4, {})} | custom-call | flops 301989888 | bytes 1191936 | tf_op jit(solution)/shard_map/fold/pallas_call | solution.py:245
  45.2 4.9 %collective-permute-done.10.refs_0_ = bf16[1552,128]{1,0:T(8,128)(2,1)S(1)} collective-permute-done((bf16[1552,128]{1,0:T(8,128)(2,1)S(1)}, bf16[1552,128]{1,0:T(8,128)(2,1)S(1)}, u32[]{:S(2)}, u32[]{:S(2)}) %collective-permute-start.10) | collective-permute-done | bytes 397344 | tf_op jit(solution)/shard_map/ppermute | solution.py:43
  50.1 1.5 %collective-permute-start.13 = (bf16[1552,128]{1,0:T(8,128)(2,1)S(1)}, bf16[1552,128]{1,0:T(8,128)(2,1)S(1)}, u32[]{:S(2)}, u32[]{:S(2)}) collective-permute-start(bf16[1552,128]{1,0:T(8,128)(2,1)S(1)} %collective-permute-done.10.refs_0_), channel_id=1, source_target_pairs={{0,2},{1,3},{2,0},{3,1},{4,6},{5,7},{6,4},{7,5},{8,10},{9,11},{10,... | collective-permute-start | bytes 1191944 | tf_op jit(solution)/shard_map/ppermute | solution.py:43
  51.6 0.5 collective-permute-done.15.refs_2_
  52.1 0.0 collective-permute-done.14.refs_1_
  52.1 1.6 %fold.9.refs_4_ = f32[4224,256]{1,0:T(8,128)S(1)} custom-call(bf16[1552,128]{1,0:T(8,128)(2,1)S(1)} %collective-permute-done.10.refs_0_, bf16[1552,128]{1,0:T(8,128)(2,1)S(1)} %collective-permute-done.14.refs_1_, bf16[1552,128]{1,0:T(8,128)(2,1)S(1)} %collective-permute-done.15.refs_2_, ...), custom_call_target="tpu_custom_call", output_to_operand_aliasing={{}: (4, {})} | custom-call | flops 301989888 | bytes 1191936 | tf_op jit(solution)/shard_map/fold/pallas_call | solution.py:245
  53.7 2.0 %collective-permute-done.7.refs_0_ = bf16[1552,128]{1,0:T(8,128)(2,1)S(1)} collective-permute-done((bf16[1552,128]{1,0:T(8,128)(2,1)S(1)}, bf16[1552,128]{1,0:T(8,128)(2,1)S(1)}, u32[]{:S(2)}, u32[]{:S(2)}) %collective-permute-start.7) | collective-permute-done | bytes 397344 | tf_op jit(solution)/shard_map/ppermute | solution.py:43
  55.7 0.0 collective-permute-done.9.refs_1_
  55.7 2.2 %collective-permute-done.13.refs_2_ = bf16[1552,128]{1,0:T(8,128)(2,1)S(1)} collective-permute-done((bf16[1552,128]{1,0:T(8,128)(2,1)S(1)}, bf16[1552,128]{1,0:T(8,128)(2,1)S(1)}, u32[]{:S(2)}, u32[]{:S(2)}) %collective-permute-start.13) | collective-permute-done | bytes 397344 | tf_op jit(solution)/shard_map/ppermute | solution.py:43
  57.9 3.6 %last.1 = (f32[4224,256]{1,0:T(8,128)S(1)}, f32[4096,256]{1,0:T(8,128)}) custom-call(bf16[1552,128]{1,0:T(8,128)(2,1)S(1)} %collective-permute-done.7.refs_0_, bf16[1552,128]{1,0:T(8,128)(2,1)S(1)} %collective-permute-done.9.refs_1_, bf16[1552,128]{1,0:T(8,128)(2,1)S(1)} %collective-permute-done.13.refs_2_, ...), custom_call_target="tpu_custom_call", output_to_operand_aliasing={{0}: (4, {})} | custom-call | flops 301989888 | bytes 1191936 | tf_op jit(solution)/shard_map/last/pallas_call | solution.py:233
Async XLA Ops:
  0.0 7.1 %collective-permute-start.1 = (bf16[2,1024,256]{2,1,0:T(8,128)(2,1)}, bf16[2,1024,256]{2,1,0:T(8,128)(2,1)S(1)}, u32[]{:S(2)}, u32[]{:S(2)}) collective-permute-start(bf16[2,1024,256]{2,1,0:T(8,128)(2,1)} %refs_0_.1), channel_id=1, source_target_pairs={{0,16},{16,0},{1,17},{17,1},{2,18},{18,2},{3,19},{19,3},{4,20},{20... | collective-permute-start | bytes 3145736 | tf_op jit(solution)/shard_map/ppermute | solution.py:264
  1.5 14.8 %collective-permute-start.2 = (bf16[1552,128]{1,0:T(8,128)(2,1)S(1)}, bf16[1552,128]{1,0:T(8,128)(2,1)S(1)}, u32[]{:S(2)}, u32[]{:S(2)}) collective-permute-start(bf16[1552,128]{1,0:T(8,128)(2,1)S(1)} %pack.1.refs_0_), channel_id=1, source_target_pairs={{0,4},{1,5},{2,6},{3,7},{4,8},{5,9},{6,10},{7,11},{8,12},{9,13},{1... | collective-permute-start | bytes 1191944 | tf_op jit(solution)/shard_map/ppermute | solution.py:43
  4.1 15.3 %collective-permute-start.4 = (bf16[1552,128]{1,0:T(8,128)(2,1)S(1)}, bf16[1552,128]{1,0:T(8,128)(2,1)S(1)}, u32[]{:S(2)}, u32[]{:S(2)}) collective-permute-start(bf16[1552,128]{1,0:T(8,128)(2,1)S(1)} %pack.1.refs_0_), channel_id=1, source_target_pairs={{0,2},{1,3},{2,0},{3,1},{4,6},{5,7},{6,4},{7,5},{8,10},{9,11},{10,... | collective-permute-start | bytes 1191944 | tf_op jit(solution)/shard_map/ppermute | solution.py:43
  5.6 13.7 %collective-permute-start = (bf16[1552,128]{1,0:T(8,128)(2,1)S(1)}, bf16[1552,128]{1,0:T(8,128)(2,1)S(1)}, u32[]{:S(2)}, u32[]{:S(2)}) collective-permute-start(bf16[1552,128]{1,0:T(8,128)(2,1)S(1)} %pack.1.refs_0_), channel_id=1, source_target_pairs={{0,1},{1,0},{2,3},{3,2},{4,5},{5,4},{6,7},{7,6},{8,9},{9,8},{10,11... | collective-permute-start | bytes 1191944 | tf_op jit(solution)/shard_map/ppermute | solution.py:43
  9.4 15.2 %collective-permute-start.3 = (bf16[1552,128]{1,0:T(8,128)(2,1)S(1)}, bf16[1552,128]{1,0:T(8,128)(2,1)S(1)}, u32[]{:S(2)}, u32[]{:S(2)}) collective-permute-start(bf16[1552,128]{1,0:T(8,128)(2,1)S(1)} %pack.1.refs_0_), channel_id=1, source_target_pairs={{0,12},{1,13},{2,14},{3,15},{4,0},{5,1},{6,2},{7,3},{8,4},{9,5},{1... | collective-permute-start | bytes 1191944 | tf_op jit(solution)/shard_map/ppermute | solution.py:43
  16.2 11.9 %collective-permute-start.5 = (bf16[1552,128]{1,0:T(8,128)(2,1)S(1)}, bf16[1552,128]{1,0:T(8,128)(2,1)S(1)}, u32[]{:S(2)}, u32[]{:S(2)}) collective-permute-start(bf16[1552,128]{1,0:T(8,128)(2,1)S(1)} %collective-permute-done.2.refs_0_), channel_id=1, source_target_pairs={{0,1},{1,0},{2,3},{3,2},{4,5},{5,4},{6,7},{7,6},{8,9},{9,8},{10,11... | collective-permute-start | bytes 1191944 | tf_op jit(solution)/shard_map/ppermute | solution.py:43
  17.9 13.7 %collective-permute-start.6 = (bf16[1552,128]{1,0:T(8,128)(2,1)S(1)}, bf16[1552,128]{1,0:T(8,128)(2,1)S(1)}, u32[]{:S(2)}, u32[]{:S(2)}) collective-permute-start(bf16[1552,128]{1,0:T(8,128)(2,1)S(1)} %collective-permute-done.2.refs_0_), channel_id=1, source_target_pairs={{0,2},{1,3},{2,0},{3,1},{4,6},{5,7},{6,4},{7,5},{8,10},{9,11},{10,... | collective-permute-start | bytes 1191944 | tf_op jit(solution)/shard_map/ppermute | solution.py:43
  24.5 13.8 %collective-permute-start.8 = (bf16[1552,128]{1,0:T(8,128)(2,1)S(1)}, bf16[1552,128]{1,0:T(8,128)(2,1)S(1)}, u32[]{:S(2)}, u32[]{:S(2)}) collective-permute-start(bf16[1552,128]{1,0:T(8,128)(2,1)S(1)} %collective-permute-done.3.refs_0_), channel_id=1, source_target_pairs={{0,2},{1,3},{2,0},{3,1},{4,6},{5,7},{6,4},{7,5},{8,10},{9,11},{10,... | collective-permute-start | bytes 1191944 | tf_op jit(solution)/shard_map/ppermute | solution.py:43
  26.1 15.5 %collective-permute-start.11 = (bf16[1552,128]{1,0:T(8,128)(2,1)S(1)}, bf16[1552,128]{1,0:T(8,128)(2,1)S(1)}, u32[]{:S(2)}, u32[]{:S(2)}) collective-permute-start(bf16[1552,128]{1,0:T(8,128)(2,1)S(1)} %collective-permute-done.2.refs_0_), channel_id=1, source_target_pairs={{0,4},{1,5},{2,6},{3,7},{4,8},{5,9},{6,10},{7,11},{8,12},{9,13},{1... | collective-permute-start | bytes 1191944 | tf_op jit(solution)/shard_map/ppermute | solution.py:43
  26.6 16.5 %collective-permute-start.12 = (bf16[1552,128]{1,0:T(8,128)(2,1)S(1)}, bf16[1552,128]{1,0:T(8,128)(2,1)S(1)}, u32[]{:S(2)}, u32[]{:S(2)}) collective-permute-start(bf16[1552,128]{1,0:T(8,128)(2,1)S(1)} %collective-permute-done.3.refs_0_), channel_id=1, source_target_pairs={{0,1},{1,0},{2,3},{3,2},{4,5},{5,4},{6,7},{7,6},{8,9},{9,8},{10,11... | collective-permute-start | bytes 1191944 | tf_op jit(solution)/shard_map/ppermute | solution.py:43
  28.1 22.0 %collective-permute-start.10 = (bf16[1552,128]{1,0:T(8,128)(2,1)S(1)}, bf16[1552,128]{1,0:T(8,128)(2,1)S(1)}, u32[]{:S(2)}, u32[]{:S(2)}) collective-permute-start(bf16[1552,128]{1,0:T(8,128)(2,1)S(1)} %collective-permute-done.5.refs_1_), channel_id=1, source_target_pairs={{0,4},{1,5},{2,6},{3,7},{4,8},{5,9},{6,10},{7,11},{8,12},{9,13},{1... | collective-permute-start | bytes 1191944 | tf_op jit(solution)/shard_map/ppermute | solution.py:43
  31.6 24.1 %collective-permute-start.7 = (bf16[1552,128]{1,0:T(8,128)(2,1)S(1)}, bf16[1552,128]{1,0:T(8,128)(2,1)S(1)}, u32[]{:S(2)}, u32[]{:S(2)}) collective-permute-start(bf16[1552,128]{1,0:T(8,128)(2,1)S(1)} %collective-permute-done.6.refs_2_), channel_id=1, source_target_pairs={{0,4},{1,5},{2,6},{3,7},{4,8},{5,9},{6,10},{7,11},{8,12},{9,13},{1... | collective-permute-start | bytes 1191944 | tf_op jit(solution)/shard_map/ppermute | solution.py:43
  38.4 13.7 %collective-permute-start.14 = (bf16[1552,128]{1,0:T(8,128)(2,1)S(1)}, bf16[1552,128]{1,0:T(8,128)(2,1)S(1)}, u32[]{:S(2)}, u32[]{:S(2)}) collective-permute-start(bf16[1552,128]{1,0:T(8,128)(2,1)S(1)} %collective-permute-done.6.refs_2_), channel_id=1, source_target_pairs={{0,1},{1,0},{2,3},{3,2},{4,5},{5,4},{6,7},{7,6},{8,9},{9,8},{10,11... | collective-permute-start | bytes 1191944 | tf_op jit(solution)/shard_map/ppermute | solution.py:43
  41.6 10.5 %collective-permute-start.15 = (bf16[1552,128]{1,0:T(8,128)(2,1)S(1)}, bf16[1552,128]{1,0:T(8,128)(2,1)S(1)}, u32[]{:S(2)}, u32[]{:S(2)}) collective-permute-start(bf16[1552,128]{1,0:T(8,128)(2,1)S(1)} %collective-permute-done.refs_2_), channel_id=1, source_target_pairs={{0,2},{1,3},{2,0},{3,1},{4,6},{5,7},{6,4},{7,5},{8,10},{9,11},{10,... | collective-permute-start | bytes 1191944 | tf_op jit(solution)/shard_map/ppermute | solution.py:43
  43.1 12.6 %collective-permute-start.9 = (bf16[1552,128]{1,0:T(8,128)(2,1)S(1)}, bf16[1552,128]{1,0:T(8,128)(2,1)S(1)}, u32[]{:S(2)}, u32[]{:S(2)}) collective-permute-start(bf16[1552,128]{1,0:T(8,128)(2,1)S(1)} %collective-permute-done.8.refs_2_), channel_id=1, source_target_pairs={{0,1},{1,0},{2,3},{3,2},{4,5},{5,4},{6,7},{7,6},{8,9},{9,8},{10,11... | collective-permute-start | bytes 1191944 | tf_op jit(solution)/shard_map/ppermute | solution.py:43
  50.1 7.8 %collective-permute-start.13 = (bf16[1552,128]{1,0:T(8,128)(2,1)S(1)}, bf16[1552,128]{1,0:T(8,128)(2,1)S(1)}, u32[]{:S(2)}, u32[]{:S(2)}) collective-permute-start(bf16[1552,128]{1,0:T(8,128)(2,1)S(1)} %collective-permute-done.10.refs_0_), channel_id=1, source_target_pairs={{0,2},{1,3},{2,0},{3,1},{4,6},{5,7},{6,4},{7,5},{8,10},{9,11},{10,... | collective-permute-start | bytes 1191944 | tf_op jit(solution)/shard_map/ppermute | solution.py:43

commit v3 on v0

v3 whole, which is shorter than its diff:
```python
import functools

import jax
import jax.numpy as jnp
from jax import lax
from jax.experimental import pallas as pl
from jax.experimental.pallas import tpu as pltpu
from jax.sharding import PartitionSpec as P

RB_DEV = 32
META = 16


PARTS = ((0, 12),)
PLAN = [
    (0, 1, 0),
    (0, 12, 3),
    (0, 2, 1),
    [(0, 0)],
    (0, 5, 2),
    (0, 13, 0),
    (0, 14, 1),
    (0, 6, 2),
    [(0, 1), (0, 12), (0, 2)],
    (0, 3, 0),
    (0, 7, 1),
    (0, 9, 2),
    [(0, 5), (0, 13)],
    (0, 4, 0),
    (0, 15, 1),
    (0, 10, 2),
    [(0, 14), (0, 6), (0, 3)],
    (0, 8, 0),
    (0, 11, 1),
    [(0, 9), (0, 7)],
    [(0, 4)],
    [(0, 15)],
]


def ring_of(n_col):
    return (0, 1, 3, 2) if n_col == 16 else tuple(range(n_col // 4))


def moved(n_col, index, direction):
    if direction < 2:
        return index ^ (1 + direction)
    ring = ring_of(n_col)
    at = ring.index(index // 4) + (1 if direction == 2 else -1)
    return ring[at % len(ring)] * 4 + index % 4


def hop(n_row, n_col, direction, unit):
    pairs = []
    for row in range(n_row):
        way = direction ^ 1 if row % 2 and direction < 2 else direction
        pairs += [(row * n_col + i, row * n_col + moved(n_col, i, way)) for i in range(n_col)]
    return lax.ppermute(unit, ("row", "col"), pairs)


def origin(n_col, key, direction):
    return (key ^ 1, key ^ 2, (key - 4) % n_col, (key + 4) % n_col)[direction]


def gather_plan(n_col, n_slots):
    if n_col == 16 and n_slots == PARTS[-1][1]:
        return PARTS, PLAN
    steps = []
    held = [0]
    ready = [(0, 0)]
    while len(held) < n_col:
        taken = []
        for direction in range(3):
            for key in range(1, n_col):
                if key not in held and key not in taken and origin(n_col, key, direction) in held:
                    steps.append((0, key, direction))
                    taken.append(key)
                    break
        steps.append(ready)
        held += taken
        ready = [(0, key) for key in taken]
    return ((0, n_slots),), steps


def pack_kernel(rows_hbm, cols_hbm, counts_hbm, tiles_ref, *refs, parts, size):
    unit_refs, (rows_ref, cols_ref, counts_ref, sem) = refs[: len(parts)], refs[len(parts) :]
    per_dev = rows_ref.shape[2]
    copies = [
        pltpu.make_async_copy(rows_hbm, rows_ref, sem.at[0]),
        pltpu.make_async_copy(cols_hbm, cols_ref, sem.at[1]),
        pltpu.make_async_copy(counts_hbm, counts_ref, sem.at[2]),
    ]
    for p, (low, high) in enumerate(parts):
        here = tiles_ref.at[pl.ds(low * size, (high - low) * size)]
        copies.append(pltpu.make_async_copy(here, unit_refs[p].at[pl.ds(0, (high - low) * size)], sem.at[3 + p]))
    for copy in copies:
        copy.start()
    for copy in copies[:3]:
        copy.wait()
    lane = lax.broadcasted_iota(jnp.int32, (META, 128), 1)
    for p, (low, high) in enumerate(parts):
        meta = jnp.zeros((META, 128), jnp.int32)
        for slot in range(low, high):
            step, q = slot // per_dev, slot % per_dev
            row = jnp.where(q < counts_ref[step], rows_ref[step, 0, q], RB_DEV)
            meta = jnp.where(lane == slot - low, row, meta)
            meta = jnp.where(lane == high - 2 * low + slot, cols_ref[step, 0, q], meta)
        unit_refs[p][pl.ds((high - low) * size, META), :] = meta.astype(jnp.float32).astype(jnp.bfloat16)
    for copy in copies[3:]:
        copy.wait()


def pack(rows, cols, counts, tiles, parts):
    steps, _, per_dev, size, _ = tiles.shape
    args = rows, cols, counts.reshape(steps), tiles.reshape(steps * per_dev * size, size)
    return pl.pallas_call(
        functools.partial(pack_kernel, parts=parts, size=size),
        out_shape=tuple(jax.ShapeDtypeStruct(((high - low) * size + META, size), jnp.bfloat16) for low, high in parts),
        in_specs=[pl.BlockSpec(memory_space=pltpu.HBM)] * 4,
        out_specs=(pl.BlockSpec(memory_space=pltpu.VMEM),) * len(parts),
        scratch_shapes=[
            pltpu.SMEM(rows.shape, jnp.int32),
            pltpu.SMEM(cols.shape, jnp.int32),
            pltpu.SMEM((steps,), jnp.int32),
            pltpu.SemaphoreType.DMA((3 + len(parts),)),
        ],
        compiler_params=pltpu.CompilerParams(vmem_limit_bytes=2 << 20),
        name="pack",
    )(*(pltpu.with_memory_space_constraint(x, pltpu.HBM) for x in args))


def panel_kernel(*refs, n_row):
    pieces, whole_ref, acc_ref, sem = refs[:n_row], refs[n_row], refs[n_row + 1], refs[n_row + 2]
    steps, depth, _ = pieces[0].shape
    me = lax.axis_index("row")
    copies = []
    for back_by, piece in enumerate(pieces):
        owner = lax.rem(me - back_by + n_row, n_row)
        for step in range(steps):
            copies.append(
                pltpu.make_async_copy(
                    piece.at[step],
                    whole_ref.at[step, pl.ds(owner * depth, depth)],
                    sem.at[back_by * steps + step],
                )
            )
    for copy in copies:
        copy.start()
    acc_ref[...] = jnp.zeros_like(acc_ref)
    for copy in copies:
        copy.wait()


def whole_panels(pieces, size):
    n_row = len(pieces)
    steps, depth, scen = pieces[0].shape
    return pl.pallas_call(
        functools.partial(panel_kernel, n_row=n_row),
        out_shape=(
            pltpu.VMEM((steps, n_row * depth, scen), jnp.bfloat16),
            pltpu.VMEM(((RB_DEV + 1) * size, scen), jnp.float32),
        ),
        in_specs=[pl.BlockSpec(memory_space=pltpu.HBM)] + [pl.BlockSpec(memory_space=pl.ANY)] * (n_row - 1),
        out_specs=(pl.BlockSpec(memory_space=pltpu.VMEM),) * 2,
        scratch_shapes=[pltpu.SemaphoreType.DMA((n_row * steps,))],
        compiler_params=pltpu.CompilerParams(vmem_limit_bytes=2 << 20),
        name="panels",
    )(pltpu.with_memory_space_constraint(pieces[0], pltpu.HBM), *pieces[1:])


def add_units(slots, size, unit_refs, panel_ref, acc_ref, meta_ref, index_ref, sem):
    for k, unit_ref in enumerate(unit_refs):
        meta = unit_ref[pl.ds(len(slots[k]) * size, META), :].astype(jnp.float32).astype(jnp.int32)
        meta_ref[pl.ds(8 * k, 8), :] = meta[:8]
    copy = pltpu.make_async_copy(meta_ref, index_ref, sem)
    copy.start()
    copy.wait()
    for k, unit_ref in enumerate(unit_refs):
        for q, step in enumerate(slots[k]):
            row = index_ref[8 * k, q]
            col = index_ref[8 * k, len(slots[k]) + q]
            product = jnp.dot(
                unit_ref[pl.ds(q * size, size), :],
                panel_ref[step, pl.ds(pl.multiple_of(col * size, size), size), :],
                preferred_element_type=jnp.float32,
            )
            at = pl.ds(pl.multiple_of(row * size, size), size)
            acc_ref[at, :] = acc_ref[at, :] + product


def fold_kernel(*refs, slots, size):
    n = len(slots)
    unit_refs, (panel_ref, _, acc_ref, meta_ref, index_ref, sem) = refs[:n], refs[n:]
    add_units(slots, size, unit_refs, panel_ref, acc_ref, meta_ref, index_ref, sem)


def last_kernel(*refs, slots, size):
    n = len(slots)
    unit_refs, (panel_ref, _, acc_ref, out_ref, meta_ref, index_ref, sem, out_sem) = refs[:n], refs[n:]
    add_units(slots, size, unit_refs, panel_ref, acc_ref, meta_ref, index_ref, sem)
    copy = pltpu.make_async_copy(acc_ref.at[pl.ds(0, out_ref.shape[0])], out_ref, out_sem)
    copy.start()
    copy.wait()


def fold(units, slots, panels, acc, last):
    n = len(units)
    size = units[0].shape[1]
    scen = panels.shape[2]
    vmem = pl.BlockSpec(memory_space=pltpu.VMEM)
    out_shape = [pltpu.VMEM(acc.shape, jnp.float32)]
    out_specs = [vmem]
    scratch = [pltpu.VMEM((8 * n, 128), jnp.int32), pltpu.SMEM((8 * n, 128), jnp.int32), pltpu.SemaphoreType.DMA]
    if last:
        out_shape.append(jax.ShapeDtypeStruct((RB_DEV * size, scen), jnp.float32))
        out_specs.append(pl.BlockSpec(memory_space=pltpu.HBM))
        scratch.append(pltpu.SemaphoreType.DMA)
    tiles = sum(len(held) for held in slots)
    return pl.pallas_call(
        functools.partial(last_kernel if last else fold_kernel, slots=slots, size=size),
        out_shape=tuple(out_shape),
        in_specs=[vmem] * (n + 2),
        out_specs=tuple(out_specs),
        input_output_aliases={n + 1: 0},
        scratch_shapes=scratch,
        compiler_params=pltpu.CompilerParams(vmem_limit_bytes=8 << 20),
        cost_estimate=pl.CostEstimate(
            flops=2 * tiles * size * size * scen, bytes_accessed=2 * tiles * size * size, transcendentals=0
        ),
        name="last" if last else "fold",
    )(*units, panels, acc)[-1]


def per_device(tiles, block_rows, block_cols, live_counts, panels, n_row, n_col):
    steps, _, per_dev, size, _ = tiles.shape
    parts, plan = gather_plan(n_col, steps * per_dev)
    slots = [[slot // per_dev for slot in range(low, high)] for low, high in parts]
    ring = [(i, (i + 1) % n_row) for i in range(n_row)]
    pieces = [panels]
    for _ in range(n_row - 1):
        pieces.append(lax.ppermute(pieces[-1], "row", ring))
    held = {(p, 0): unit for p, unit in enumerate(pack(block_rows, block_cols, live_counts, tiles, parts))}
    seen = set(held)
    folded = set()
    whole, acc = whole_panels(pieces, size)
    for step in plan:
        if isinstance(step, list):
            acc = fold([held[name] for name in step], [slots[p] for p, _ in step], whole, acc, False)
            folded.update(step)
            continue
        p, key, direction = step
        source = (p, origin(n_col, key, direction))
        seen.add(source)
        if folded:
            names = [name for name in held if name in seen]
            *tied, acc = lax.optimization_barrier((*(held[name] for name in names), acc))
            held.update(zip(names, tied))
        held[p, key] = hop(n_row, n_col, direction, held[source])
    rest = [name for name in held if name not in folded]
    return fold([held[name] for name in rest], [slots[p] for p, _ in rest], whole, acc, True)


def solution(mesh):
    placed = (
        P(None, "row", "col", None, None),
        P(None, "row", "col"),
        P(None, "row", "col"),
        P(None, "row", "col"),
        P(None, "row", "col"),
    )
    body = functools.partial(per_device, n_row=mesh.shape["row"], n_col=mesh.shape["col"])
    return jax.shard_map(body, mesh=mesh, in_specs=placed, out_specs=P("row", "col"), check_vma=False)
```

time: 228 us -> 58.7 us (0.26)
  local copies, waits for them, and re-layouts: 60.4 us -> 0 us
  waiting for transfers between devices: 71.3 us -> 13.3 us
  other arithmetic: 41.2 us -> 0 us
  starting transfers between devices: 0.08 us -> 30.5 us
  matrix products: 23.6 us -> 0 us
  blocking collectives: 16.2 us -> 0 us
  Pallas kernels: 0 us -> 14.6 us
  between operations: 13.8 us -> 0.1 us
    all_gather x3 -> x0, waiting for transfers between devices: 69.9 us -> none  [the longest x2 69.9 us: per_device(): lax.all_gather(tiles[step:step + 1], 'col', axis=2, tiled=True)]
    scatter-add x2 -> x0, local copies, waits for them, and re-layouts: 37.1 us -> none  [place_blocks(): return dense.at[rows_idx, :, cols_idx, :].add(masked)]
    scatter-add x2 -> x0, other arithmetic: 36.8 us -> none  [place_blocks(): return dense.at[rows_idx, :, cols_idx, :].add(masked)]
    ppermute x0 -> x16, starting transfers between devices: none -> 30.5 us  [the longest x15 30.1 us: hop(): return lax.ppermute(unit, ('row', 'col'), pairs)]
    dot_general x2 -> x0, matrix products: 23.6 us -> none  [per_device(): jnp.dot(matrix, whole[step], preferred_element_type=jnp.float32)]
    unnamed x1 -> x0, blocking collectives: 16.2 us -> none
    pallas_call x0 -> x10, Pallas kernels: none -> 14.6 us  [the longest x8 12.3 us: fold(): pl.pallas_call(functools.partial(last_kernel if last else fold_kernel, sl...]
    ppermute x0 -> x16, waiting for transfers between devices: none -> 13.3 us  [the longest x15 13.3 us: hop(): return lax.ppermute(unit, ('row', 'col'), pairs)]
  transfers between devices with their start and end apart: 3 -> 16, of which waited for: 2 -> 7; matrix products, arithmetic and copies ran while one was open for 44% -> 0% of each run, Pallas kernels for 0% -> 19%
where the time goes in v3:
time: 58.7 us; the launch traced here: 58.6 us
  starting transfers between devices  30.5 us (52%)
  Pallas kernels  14.6 us (25%)
  waiting for transfers between devices  13.3 us (23%)
    ppermute x15, starting transfers between devices, hop(): return lax.ppermute(unit, ('row', 'col'), pairs)  30.1 us
    ppermute x15, waiting for transfers between devices, hop(): return lax.ppermute(unit, ('row', 'col'), pairs)  13.3 us
    pallas_call x8, Pallas kernels, fold(): pl.pallas_call(functools.partial(last_kernel if last else fold_kernel, sl...  12.3 us
    pallas_call x1, Pallas kernels, whole_panels(): pl.pallas_call(functools.partial(panel_kernel, n_row=n_row), out_shape=(p...  1.24 us
  transfers between devices with their start and end apart: 16, of which 7 were waited for; matrix products, arithmetic and copies ran while one was open for 0% of the time, Pallas kernels for 19%

profile of v3, /device:TPU:0, one launch (start us, length us, event | category | flops | bytes accessed | tf_op | source)
XLA Modules:
  0.0 58.6 jit_solution(18088256527928519495)
XLA Ops:
  0.0 0.5 collective-permute-start.1
  0.5 1.0 %pack.1.refs_0_ = bf16[1552,128]{1,0:T(8,128)(2,1)S(1)} custom-call(s32[2,1,6]{2,1,0:T(1,128)} %rows_hbm.1, s32[2,1,6]{2,1,0:T(1,128)} %cols_hbm.1, s32[2]{0:T(128)} %bitcast.3, bf16[1536,128]{1,0:T(8,128)(2,1)} %bitcast.2), custom_call_target="tpu_custom_call" | custom-call | tf_op jit(solution)/shard_map/pack/pallas_call | solution.py:116
  1.5 2.6 %collective-permute-start = (bf16[1552,128]{1,0:T(8,128)(2,1)S(1)}, bf16[1552,128]{1,0:T(8,128)(2,1)S(1)}, u32[]{:S(2)}, u32[]{:S(2)}) collective-permute-start(bf16[1552,128]{1,0:T(8,128)(2,1)S(1)} %pack.1.refs_0_), channel_id=1, source_target_pairs={{0,1},{1,0},{2,3},{3,2},{4,5},{5,4},{6,7},{7,6},{8,9},{9,8},{10,11... | collective-permute-start | bytes 1191944 | tf_op jit(solution)/shard_map/ppermute | solution.py:58
  4.0 2.6 %collective-permute-start.2 = (bf16[1552,128]{1,0:T(8,128)(2,1)S(1)}, bf16[1552,128]{1,0:T(8,128)(2,1)S(1)}, u32[]{:S(2)}, u32[]{:S(2)}) collective-permute-start(bf16[1552,128]{1,0:T(8,128)(2,1)S(1)} %pack.1.refs_0_), channel_id=1, source_target_pairs={{0,8},{1,9},{2,10},{3,11},{4,0},{5,1},{6,2},{7,3},{8,12},{9,13},{1... | collective-permute-start | bytes 1191944 | tf_op jit(solution)/shard_map/ppermute | solution.py:58
  6.6 1.5 %collective-permute-start.3 = (bf16[1552,128]{1,0:T(8,128)(2,1)S(1)}, bf16[1552,128]{1,0:T(8,128)(2,1)S(1)}, u32[]{:S(2)}, u32[]{:S(2)}) collective-permute-start(bf16[1552,128]{1,0:T(8,128)(2,1)S(1)} %pack.1.refs_0_), channel_id=1, source_target_pairs={{0,2},{1,3},{2,0},{3,1},{4,6},{5,7},{6,4},{7,5},{8,10},{9,11},{10,... | collective-permute-start | bytes 1191944 | tf_op jit(solution)/shard_map/ppermute | solution.py:58
  8.2 0.0 collective-permute-done.1.refs_1_
  8.2 1.2 %panels.1 = (bf16[2,2048,256]{2,1,0:T(8,128)(2,1)S(1)}, f32[4224,256]{1,0:T(8,128)S(1)}) custom-call(bf16[2,1024,256]{2,1,0:T(8,128)(2,1)} %refs_0_.1, bf16[2,1024,256]{2,1,0:T(8,128)(2,1)S(1)} %collective-permute-done.1.refs_1_), custom_call_target="tpu_custom_call" | custom-call | tf_op jit(solution)/shard_map/panels/pallas_call | solution.py:157
  9.4 1.0 %fold.7.refs_4_ = f32[4224,256]{1,0:T(8,128)S(1)} custom-call(bf16[1552,128]{1,0:T(8,128)(2,1)S(1)} %pack.1.refs_0_, bf16[2,2048,256]{2,1,0:T(8,128)(2,1)S(1)} %get-tuple-element.41.refs_1_.refs_3_.refs_2_, f32[4224,256]{1,0:T(8,128)S(1)} %get-tuple-element.42.refs_2_), custom_call_target="tpu_custom_call", output_to_operand_aliasing={{}: (2, {})} | custom-call | flops 100663296 | bytes 393216 | tf_op jit(solution)/shard_map/fold/pallas_call | solution.py:219
  10.4 0.1 collective-permute-done.refs_0_
  10.5 4.8 %collective-permute-start.4 = (bf16[1552,128]{1,0:T(8,128)(2,1)S(1)}, bf16[1552,128]{1,0:T(8,128)(2,1)S(1)}, u32[]{:S(2)}, u32[]{:S(2)}) collective-permute-start(bf16[1552,128]{1,0:T(8,128)(2,1)S(1)} %collective-permute-done.refs_0_), channel_id=1, source_target_pairs={{0,4},{1,5},{2,6},{3,7},{4,12},{5,13},{6,14},{7,15},{8,0},{9,1},{1... | collective-permute-start | bytes 1191944 | tf_op jit(solution)/shard_map/ppermute | solution.py:58
  15.3 0.9 %collective-permute-done.2.refs_1_ = bf16[1552,128]{1,0:T(8,128)(2,1)S(1)} collective-permute-done((bf16[1552,128]{1,0:T(8,128)(2,1)S(1)}, bf16[1552,128]{1,0:T(8,128)(2,1)S(1)}, u32[]{:S(2)}, u32[]{:S(2)}) %collective-permute-start.2) | collective-permute-done | bytes 397344 | tf_op jit(solution)/shard_map/ppermute | solution.py:58
  16.2 0.6 collective-permute-start.5
  16.8 0.0 collective-permute-done.3.refs_2_
  16.8 2.7 %collective-permute-start.6 = (bf16[1552,128]{1,0:T(8,128)(2,1)S(1)}, bf16[1552,128]{1,0:T(8,128)(2,1)S(1)}, u32[]{:S(2)}, u32[]{:S(2)}) collective-permute-start(bf16[1552,128]{1,0:T(8,128)(2,1)S(1)} %collective-permute-done.3.refs_2_), channel_id=1, source_target_pairs={{0,4},{1,5},{2,6},{3,7},{4,12},{5,13},{6,14},{7,15},{8,0},{9,1},{1... | collective-permute-start | bytes 1191944 | tf_op jit(solution)/shard_map/ppermute | solution.py:58
  19.5 1.6 %fold.8.refs_3_ = f32[4224,256]{1,0:T(8,128)S(1)} custom-call(bf16[1552,128]{1,0:T(8,128)(2,1)S(1)} %collective-permute-done.refs_0_, bf16[1552,128]{1,0:T(8,128)(2,1)S(1)} %collective-permute-done.2.refs_1_, bf16[1552,128]{1,0:T(8,128)(2,1)S(1)} %collective-permute-done.3.refs_2_, ...), custom_call_target="tpu_custom_call", output_to_operand_aliasing={{}: (4, {})} | custom-call | flops 301989888 | bytes 1179648 | tf_op jit(solution)/shard_map/fold/pallas_call | solution.py:219
  21.1 1.2 %collective-permute-start.10 = (bf16[1552,128]{1,0:T(8,128)(2,1)S(1)}, bf16[1552,128]{1,0:T(8,128)(2,1)S(1)}, u32[]{:S(2)}, u32[]{:S(2)}) collective-permute-start(bf16[1552,128]{1,0:T(8,128)(2,1)S(1)} %collective-permute-done.3.refs_2_), channel_id=1, source_target_pairs={{0,1},{1,0},{2,3},{3,2},{4,5},{5,4},{6,7},{7,6},{8,9},{9,8},{10,11... | collective-permute-start | bytes 1191944 | tf_op jit(solution)/shard_map/ppermute | solution.py:58
  22.3 1.5 %collective-permute-start.9 = (bf16[1552,128]{1,0:T(8,128)(2,1)S(1)}, bf16[1552,128]{1,0:T(8,128)(2,1)S(1)}, u32[]{:S(2)}, u32[]{:S(2)}) collective-permute-start(bf16[1552,128]{1,0:T(8,128)(2,1)S(1)} %collective-permute-done.2.refs_1_), channel_id=1, source_target_pairs={{0,2},{1,3},{2,0},{3,1},{4,6},{5,7},{6,4},{7,5},{8,10},{9,11},{10,... | collective-permute-start | bytes 1191944 | tf_op jit(solution)/shard_map/ppermute | solution.py:58
  23.8 2.1 %collective-permute-done.4.refs_0_ = bf16[1552,128]{1,0:T(8,128)(2,1)S(1)} collective-permute-done((bf16[1552,128]{1,0:T(8,128)(2,1)S(1)}, bf16[1552,128]{1,0:T(8,128)(2,1)S(1)}, u32[]{:S(2)}, u32[]{:S(2)}) %collective-permute-start.4) | collective-permute-done | bytes 397344 | tf_op jit(solution)/shard_map/ppermute | solution.py:58
  25.9 1.7 %collective-permute-start.8 = (bf16[1552,128]{1,0:T(8,128)(2,1)S(1)}, bf16[1552,128]{1,0:T(8,128)(2,1)S(1)}, u32[]{:S(2)}, u32[]{:S(2)}) collective-permute-start(bf16[1552,128]{1,0:T(8,128)(2,1)S(1)} %collective-permute-done.4.refs_0_), channel_id=1, source_target_pairs={{0,4},{1,5},{2,6},{3,7},{4,12},{5,13},{6,14},{7,15},{8,0},{9,1},{1... | collective-permute-start | bytes 1191944 | tf_op jit(solution)/shard_map/ppermute | solution.py:58
  27.7 0.0 collective-permute-done.5.refs_1_
  27.7 2.1 %collective-permute-start.15 = (bf16[1552,128]{1,0:T(8,128)(2,1)S(1)}, bf16[1552,128]{1,0:T(8,128)(2,1)S(1)}, u32[]{:S(2)}, u32[]{:S(2)}) collective-permute-start(bf16[1552,128]{1,0:T(8,128)(2,1)S(1)} %collective-permute-done.4.refs_0_), channel_id=1, source_target_pairs={{0,2},{1,3},{2,0},{3,1},{4,6},{5,7},{6,4},{7,5},{8,10},{9,11},{10,... | collective-permute-start | bytes 1191944 | tf_op jit(solution)/shard_map/ppermute | solution.py:58
  29.8 1.3 %fold.9.refs_4_ = f32[4224,256]{1,0:T(8,128)S(1)} custom-call(bf16[1552,128]{1,0:T(8,128)(2,1)S(1)} %collective-permute-done.4.refs_0_, bf16[1552,128]{1,0:T(8,128)(2,1)S(1)} %collective-permute-done.5.refs_1_, bf16[2,2048,256]{2,1,0:T(8,128)(2,1)S(1)} %get-tuple-element.41.refs_1_.refs_3_.refs_2_, ...), custom_call_target="tpu_custom_call", output_to_operand_aliasing={{}: (3, {})} | custom-call | flops 201326592 | bytes 786432 | tf_op jit(solution)/shard_map/fold/pallas_call | solution.py:219
  31.1 3.3 %collective-permute-done.6.refs_1_ = bf16[1552,128]{1,0:T(8,128)(2,1)S(1)} collective-permute-done((bf16[1552,128]{1,0:T(8,128)(2,1)S(1)}, bf16[1552,128]{1,0:T(8,128)(2,1)S(1)}, u32[]{:S(2)}, u32[]{:S(2)}) %collective-permute-start.6) | collective-permute-done | bytes 397344 | tf_op jit(solution)/shard_map/ppermute | solution.py:58
  34.4 1.9 %collective-permute-start.13 = (bf16[1552,128]{1,0:T(8,128)(2,1)S(1)}, bf16[1552,128]{1,0:T(8,128)(2,1)S(1)}, u32[]{:S(2)}, u32[]{:S(2)}) collective-permute-start(bf16[1552,128]{1,0:T(8,128)(2,1)S(1)} %collective-permute-done.5.refs_1_), channel_id=1, source_target_pairs={{0,2},{1,3},{2,0},{3,1},{4,6},{5,7},{6,4},{7,5},{8,10},{9,11},{10,... | collective-permute-start | bytes 1191944 | tf_op jit(solution)/shard_map/ppermute | solution.py:58
  36.3 0.0 collective-permute-done.10.refs_2_
  36.3 1.5 %collective-permute-start.14 = (bf16[1552,128]{1,0:T(8,128)(2,1)S(1)}, bf16[1552,128]{1,0:T(8,128)(2,1)S(1)}, u32[]{:S(2)}, u32[]{:S(2)}) collective-permute-start(bf16[1552,128]{1,0:T(8,128)(2,1)S(1)} %collective-permute-done.4.refs_0_), channel_id=1, source_target_pairs={{0,1},{1,0},{2,3},{3,2},{4,5},{5,4},{6,7},{7,6},{8,9},{9,8},{10,11... | collective-permute-start | bytes 1191944 | tf_op jit(solution)/shard_map/ppermute | solution.py:58
  37.8 0.0 collective-permute-done.9.refs_0_
  37.8 2.0 %collective-permute-start.7 = (bf16[1552,128]{1,0:T(8,128)(2,1)S(1)}, bf16[1552,128]{1,0:T(8,128)(2,1)S(1)}, u32[]{:S(2)}, u32[]{:S(2)}) collective-permute-start(bf16[1552,128]{1,0:T(8,128)(2,1)S(1)} %collective-permute-done.6.refs_1_), channel_id=1, source_target_pairs={{0,4},{1,5},{2,6},{3,7},{4,12},{5,13},{6,14},{7,15},{8,0},{9,1},{1... | collective-permute-start | bytes 1191944 | tf_op jit(solution)/shard_map/ppermute | solution.py:58
  39.8 1.6 %fold.10.refs_3_ = f32[4224,256]{1,0:T(8,128)S(1)} custom-call(bf16[1552,128]{1,0:T(8,128)(2,1)S(1)} %collective-permute-done.9.refs_0_, bf16[1552,128]{1,0:T(8,128)(2,1)S(1)} %collective-permute-done.6.refs_1_, bf16[1552,128]{1,0:T(8,128)(2,1)S(1)} %collective-permute-done.10.refs_2_, ...), custom_call_target="tpu_custom_call", output_to_operand_aliasing={{}: (4, {})} | custom-call | flops 301989888 | bytes 1179648 | tf_op jit(solution)/shard_map/fold/pallas_call | solution.py:219
  41.4 1.5 %collective-permute-done.8.refs_0_ = bf16[1552,128]{1,0:T(8,128)(2,1)S(1)} collective-permute-done((bf16[1552,128]{1,0:T(8,128)(2,1)S(1)}, bf16[1552,128]{1,0:T(8,128)(2,1)S(1)}, u32[]{:S(2)}, u32[]{:S(2)}) %collective-permute-start.8) | collective-permute-done | bytes 397344 | tf_op jit(solution)/shard_map/ppermute | solution.py:58
  43.0 1.9 %collective-permute-start.12 = (bf16[1552,128]{1,0:T(8,128)(2,1)S(1)}, bf16[1552,128]{1,0:T(8,128)(2,1)S(1)}, u32[]{:S(2)}, u32[]{:S(2)}) collective-permute-start(bf16[1552,128]{1,0:T(8,128)(2,1)S(1)} %collective-permute-done.8.refs_0_), channel_id=1, source_target_pairs={{0,2},{1,3},{2,0},{3,1},{4,6},{5,7},{6,4},{7,5},{8,10},{9,11},{10,... | collective-permute-start | bytes 1191944 | tf_op jit(solution)/shard_map/ppermute | solution.py:58
  44.8 0.0 collective-permute-done.15.refs_1_
  44.8 1.5 %collective-permute-start.11 = (bf16[1552,128]{1,0:T(8,128)(2,1)S(1)}, bf16[1552,128]{1,0:T(8,128)(2,1)S(1)}, u32[]{:S(2)}, u32[]{:S(2)}) collective-permute-start(bf16[1552,128]{1,0:T(8,128)(2,1)S(1)} %collective-permute-done.8.refs_0_), channel_id=1, source_target_pairs={{0,1},{1,0},{2,3},{3,2},{4,5},{5,4},{6,7},{7,6},{8,9},{9,8},{10,11... | collective-permute-start | bytes 1191944 | tf_op jit(solution)/shard_map/ppermute | solution.py:58
  46.3 1.3 %fold.11.refs_2_ = f32[4224,256]{1,0:T(8,128)S(1)} custom-call(bf16[1552,128]{1,0:T(8,128)(2,1)S(1)} %collective-permute-done.8.refs_0_, bf16[1552,128]{1,0:T(8,128)(2,1)S(1)} %collective-permute-done.15.refs_1_, bf16[2,2048,256]{2,1,0:T(8,128)(2,1)S(1)} %get-tuple-element.41.refs_1_.refs_3_.refs_2_, ...), custom_call_target="tpu_custom_call", output_to_operand_aliasing={{}: (3, {})} | custom-call | flops 201326592 | bytes 786432 | tf_op jit(solution)/shard_map/fold/pallas_call | solution.py:219
  47.6 0.0 collective-permute-done.14.refs_0_
  47.6 1.0 %fold.12.refs_2_ = f32[4224,256]{1,0:T(8,128)S(1)} custom-call(bf16[1552,128]{1,0:T(8,128)(2,1)S(1)} %collective-permute-done.14.refs_0_, bf16[2,2048,256]{2,1,0:T(8,128)(2,1)S(1)} %get-tuple-element.41.refs_1_.refs_3_.refs_2_, f32[4224,256]{1,0:T(8,128)S(1)} %fold.11.refs_2_), custom_call_target="tpu_custom_call", output_to_operand_aliasing={{}: (2, {})} | custom-call | flops 100663296 | bytes 393216 | tf_op jit(solution)/shard_map/fold/pallas_call | solution.py:219
  48.6 0.0 collective-permute-done.13.refs_0_
  48.6 1.0 %fold.13.refs_4_ = f32[4224,256]{1,0:T(8,128)S(1)} custom-call(bf16[1552,128]{1,0:T(8,128)(2,1)S(1)} %collective-permute-done.13.refs_0_, bf16[2,2048,256]{2,1,0:T(8,128)(2,1)S(1)} %get-tuple-element.41.refs_1_.refs_3_.refs_2_, f32[4224,256]{1,0:T(8,128)S(1)} %fold.12.refs_2_), custom_call_target="tpu_custom_call", output_to_operand_aliasing={{}: (2, {})} | custom-call | flops 100663296 | bytes 393216 | tf_op jit(solution)/shard_map/fold/pallas_call | solution.py:219
  49.6 1.7 %collective-permute-done.7.refs_0_ = bf16[1552,128]{1,0:T(8,128)(2,1)S(1)} collective-permute-done((bf16[1552,128]{1,0:T(8,128)(2,1)S(1)}, bf16[1552,128]{1,0:T(8,128)(2,1)S(1)}, u32[]{:S(2)}, u32[]{:S(2)}) %collective-permute-start.7) | collective-permute-done | bytes 397344 | tf_op jit(solution)/shard_map/ppermute | solution.py:58
  51.4 3.6 %collective-permute-done.12.refs_2_ = bf16[1552,128]{1,0:T(8,128)(2,1)S(1)} collective-permute-done((bf16[1552,128]{1,0:T(8,128)(2,1)S(1)}, bf16[1552,128]{1,0:T(8,128)(2,1)S(1)}, u32[]{:S(2)}, u32[]{:S(2)}) %collective-permute-start.12) | collective-permute-done | bytes 397344 | tf_op jit(solution)/shard_map/ppermute | solution.py:58
  55.0 0.0 collective-permute-done.11.refs_1_
  55.0 3.6 %last.1 = (f32[4224,256]{1,0:T(8,128)S(1)}, f32[4096,256]{1,0:T(8,128)}) custom-call(bf16[1552,128]{1,0:T(8,128)(2,1)S(1)} %collective-permute-done.7.refs_0_, bf16[1552,128]{1,0:T(8,128)(2,1)S(1)} %collective-permute-done.11.refs_1_, bf16[1552,128]{1,0:T(8,128)(2,1)S(1)} %collective-permute-done.12.refs_2_, ...), custom_call_target="tpu_custom_call", output_to_operand_aliasing={{0}: (4, {})} | custom-call | flops 301989888 | bytes 1179648 | tf_op jit(solution)/shard_map/last/pallas_call | solution.py:219
Async XLA Ops:
  0.0 8.2 %collective-permute-start.1 = (bf16[2,1024,256]{2,1,0:T(8,128)(2,1)}, bf16[2,1024,256]{2,1,0:T(8,128)(2,1)S(1)}, u32[]{:S(2)}, u32[]{:S(2)}) collective-permute-start(bf16[2,1024,256]{2,1,0:T(8,128)(2,1)} %refs_0_.1), channel_id=1, source_target_pairs={{0,16},{16,0},{1,17},{17,1},{2,18},{18,2},{3,19},{19,3},{4,20},{20... | collective-permute-start | bytes 3145736 | tf_op jit(solution)/shard_map/ppermute | solution.py:241
  1.5 9.0 %collective-permute-start = (bf16[1552,128]{1,0:T(8,128)(2,1)S(1)}, bf16[1552,128]{1,0:T(8,128)(2,1)S(1)}, u32[]{:S(2)}, u32[]{:S(2)}) collective-permute-start(bf16[1552,128]{1,0:T(8,128)(2,1)S(1)} %pack.1.refs_0_), channel_id=1, source_target_pairs={{0,1},{1,0},{2,3},{3,2},{4,5},{5,4},{6,7},{7,6},{8,9},{9,8},{10,11... | collective-permute-start | bytes 1191944 | tf_op jit(solution)/shard_map/ppermute | solution.py:58
  4.0 12.1 %collective-permute-start.2 = (bf16[1552,128]{1,0:T(8,128)(2,1)S(1)}, bf16[1552,128]{1,0:T(8,128)(2,1)S(1)}, u32[]{:S(2)}, u32[]{:S(2)}) collective-permute-start(bf16[1552,128]{1,0:T(8,128)(2,1)S(1)} %pack.1.refs_0_), channel_id=1, source_target_pairs={{0,8},{1,9},{2,10},{3,11},{4,0},{5,1},{6,2},{7,3},{8,12},{9,13},{1... | collective-permute-start | bytes 1191944 | tf_op jit(solution)/shard_map/ppermute | solution.py:58
  6.6 10.1 %collective-permute-start.3 = (bf16[1552,128]{1,0:T(8,128)(2,1)S(1)}, bf16[1552,128]{1,0:T(8,128)(2,1)S(1)}, u32[]{:S(2)}, u32[]{:S(2)}) collective-permute-start(bf16[1552,128]{1,0:T(8,128)(2,1)S(1)} %pack.1.refs_0_), channel_id=1, source_target_pairs={{0,2},{1,3},{2,0},{3,1},{4,6},{5,7},{6,4},{7,5},{8,10},{9,11},{10,... | collective-permute-start | bytes 1191944 | tf_op jit(solution)/shard_map/ppermute | solution.py:58
  10.5 15.4 %collective-permute-start.4 = (bf16[1552,128]{1,0:T(8,128)(2,1)S(1)}, bf16[1552,128]{1,0:T(8,128)(2,1)S(1)}, u32[]{:S(2)}, u32[]{:S(2)}) collective-permute-start(bf16[1552,128]{1,0:T(8,128)(2,1)S(1)} %collective-permute-done.refs_0_), channel_id=1, source_target_pairs={{0,4},{1,5},{2,6},{3,7},{4,12},{5,13},{6,14},{7,15},{8,0},{9,1},{1... | collective-permute-start | bytes 1191944 | tf_op jit(solution)/shard_map/ppermute | solution.py:58
  16.2 11.5 %collective-permute-start.5 = (bf16[1552,128]{1,0:T(8,128)(2,1)S(1)}, bf16[1552,128]{1,0:T(8,128)(2,1)S(1)}, u32[]{:S(2)}, u32[]{:S(2)}) collective-permute-start(bf16[1552,128]{1,0:T(8,128)(2,1)S(1)} %collective-permute-done.2.refs_1_), channel_id=1, source_target_pairs={{0,1},{1,0},{2,3},{3,2},{4,5},{5,4},{6,7},{7,6},{8,9},{9,8},{10,11... | collective-permute-start | bytes 1191944 | tf_op jit(solution)/shard_map/ppermute | solution.py:58
  16.8 17.7 %collective-permute-start.6 = (bf16[1552,128]{1,0:T(8,128)(2,1)S(1)}, bf16[1552,128]{1,0:T(8,128)(2,1)S(1)}, u32[]{:S(2)}, u32[]{:S(2)}) collective-permute-start(bf16[1552,128]{1,0:T(8,128)(2,1)S(1)} %collective-permute-done.3.refs_2_), channel_id=1, source_target_pairs={{0,4},{1,5},{2,6},{3,7},{4,12},{5,13},{6,14},{7,15},{8,0},{9,1},{1... | collective-permute-start | bytes 1191944 | tf_op jit(solution)/shard_map/ppermute | solution.py:58
  21.1 15.2 %collective-permute-start.10 = (bf16[1552,128]{1,0:T(8,128)(2,1)S(1)}, bf16[1552,128]{1,0:T(8,128)(2,1)S(1)}, u32[]{:S(2)}, u32[]{:S(2)}) collective-permute-start(bf16[1552,128]{1,0:T(8,128)(2,1)S(1)} %collective-permute-done.3.refs_2_), channel_id=1, source_target_pairs={{0,1},{1,0},{2,3},{3,2},{4,5},{5,4},{6,7},{7,6},{8,9},{9,8},{10,11... | collective-permute-start | bytes 1191944 | tf_op jit(solution)/shard_map/ppermute | solution.py:58
  22.3 15.5 %collective-permute-start.9 = (bf16[1552,128]{1,0:T(8,128)(2,1)S(1)}, bf16[1552,128]{1,0:T(8,128)(2,1)S(1)}, u32[]{:S(2)}, u32[]{:S(2)}) collective-permute-start(bf16[1552,128]{1,0:T(8,128)(2,1)S(1)} %collective-permute-done.2.refs_1_), channel_id=1, source_target_pairs={{0,2},{1,3},{2,0},{3,1},{4,6},{5,7},{6,4},{7,5},{8,10},{9,11},{10,... | collective-permute-start | bytes 1191944 | tf_op jit(solution)/shard_map/ppermute | solution.py:58
  25.9 17.0 %collective-permute-start.8 = (bf16[1552,128]{1,0:T(8,128)(2,1)S(1)}, bf16[1552,128]{1,0:T(8,128)(2,1)S(1)}, u32[]{:S(2)}, u32[]{:S(2)}) collective-permute-start(bf16[1552,128]{1,0:T(8,128)(2,1)S(1)} %collective-permute-done.4.refs_0_), channel_id=1, source_target_pairs={{0,4},{1,5},{2,6},{3,7},{4,12},{5,13},{6,14},{7,15},{8,0},{9,1},{1... | collective-permute-start | bytes 1191944 | tf_op jit(solution)/shard_map/ppermute | solution.py:58
  27.7 17.2 %collective-permute-start.15 = (bf16[1552,128]{1,0:T(8,128)(2,1)S(1)}, bf16[1552,128]{1,0:T(8,128)(2,1)S(1)}, u32[]{:S(2)}, u32[]{:S(2)}) collective-permute-start(bf16[1552,128]{1,0:T(8,128)(2,1)S(1)} %collective-permute-done.4.refs_0_), channel_id=1, source_target_pairs={{0,2},{1,3},{2,0},{3,1},{4,6},{5,7},{6,4},{7,5},{8,10},{9,11},{10,... | collective-permute-start | bytes 1191944 | tf_op jit(solution)/shard_map/ppermute | solution.py:58
  34.4 14.2 %collective-permute-start.13 = (bf16[1552,128]{1,0:T(8,128)(2,1)S(1)}, bf16[1552,128]{1,0:T(8,128)(2,1)S(1)}, u32[]{:S(2)}, u32[]{:S(2)}) collective-permute-start(bf16[1552,128]{1,0:T(8,128)(2,1)S(1)} %collective-permute-done.5.refs_1_), channel_id=1, source_target_pairs={{0,2},{1,3},{2,0},{3,1},{4,6},{5,7},{6,4},{7,5},{8,10},{9,11},{10,... | collective-permute-start | bytes 1191944 | tf_op jit(solution)/shard_map/ppermute | solution.py:58
  36.3 11.3 %collective-permute-start.14 = (bf16[1552,128]{1,0:T(8,128)(2,1)S(1)}, bf16[1552,128]{1,0:T(8,128)(2,1)S(1)}, u32[]{:S(2)}, u32[]{:S(2)}) collective-permute-start(bf16[1552,128]{1,0:T(8,128)(2,1)S(1)} %collective-permute-done.4.refs_0_), channel_id=1, source_target_pairs={{0,1},{1,0},{2,3},{3,2},{4,5},{5,4},{6,7},{7,6},{8,9},{9,8},{10,11... | collective-permute-start | bytes 1191944 | tf_op jit(solution)/shard_map/ppermute | solution.py:58
  37.8 13.6 %collective-permute-start.7 = (bf16[1552,128]{1,0:T(8,128)(2,1)S(1)}, bf16[1552,128]{1,0:T(8,128)(2,1)S(1)}, u32[]{:S(2)}, u32[]{:S(2)}) collective-permute-start(bf16[1552,128]{1,0:T(8,128)(2,1)S(1)} %collective-permute-done.6.refs_1_), channel_id=1, source_target_pairs={{0,4},{1,5},{2,6},{3,7},{4,12},{5,13},{6,14},{7,15},{8,0},{9,1},{1... | collective-permute-start | bytes 1191944 | tf_op jit(solution)/shard_map/ppermute | solution.py:58
  43.0 12.0 %collective-permute-start.12 = (bf16[1552,128]{1,0:T(8,128)(2,1)S(1)}, bf16[1552,128]{1,0:T(8,128)(2,1)S(1)}, u32[]{:S(2)}, u32[]{:S(2)}) collective-permute-start(bf16[1552,128]{1,0:T(8,128)(2,1)S(1)} %collective-permute-done.8.refs_0_), channel_id=1, source_target_pairs={{0,2},{1,3},{2,0},{3,1},{4,6},{5,7},{6,4},{7,5},{8,10},{9,11},{10,... | collective-permute-start | bytes 1191944 | tf_op jit(solution)/shard_map/ppermute | solution.py:58
  44.8 10.1 %collective-permute-start.11 = (bf16[1552,128]{1,0:T(8,128)(2,1)S(1)}, bf16[1552,128]{1,0:T(8,128)(2,1)S(1)}, u32[]{:S(2)}, u32[]{:S(2)}) collective-permute-start(bf16[1552,128]{1,0:T(8,128)(2,1)S(1)} %collective-permute-done.8.refs_0_), channel_id=1, source_target_pairs={{0,1},{1,0},{2,3},{3,2},{4,5},{5,4},{6,7},{7,6},{8,9},{9,8},{10,11... | collective-permute-start | bytes 1191944 | tf_op jit(solution)/shard_map/ppermute | solution.py:58

commit v4 on v3

--- a/solution.py
+++ b/solution.py
@@ -18,22 +18,24 @@
     (0, 2, 1),
     [(0, 0)],
     (0, 5, 2),
+    (0, 14, 1),
     (0, 13, 0),
-    (0, 14, 1),
     (0, 6, 2),
     [(0, 1), (0, 12), (0, 2)],
-    (0, 3, 0),
+    (0, 3, 1),
+    (0, 4, 0),
+    [(0, 5)],
+    (0, 9, 2),
+    [(0, 14)],
     (0, 7, 1),
-    (0, 9, 2),
-    [(0, 5), (0, 13)],
-    (0, 4, 0),
-    (0, 15, 1),
+    [(0, 13)],
+    (0, 15, 0),
     (0, 10, 2),
-    [(0, 14), (0, 6), (0, 3)],
+    [(0, 6), (0, 3)],
+    (0, 11, 1),
     (0, 8, 0),
-    (0, 11, 1),
-    [(0, 9), (0, 7)],
-    [(0, 4)],
+    [(0, 9), (0, 4)],
+    [(0, 7)],
     [(0, 15)],
 ]
 
@@ -168,39 +170,61 @@
     )(pltpu.with_memory_space_constraint(pieces[0], pltpu.HBM), *pieces[1:])
 
 
-def add_units(slots, size, unit_refs, panel_ref, acc_ref, meta_ref, index_ref, sem):
+def read_index(slots, size, unit_refs, meta_ref, index_ref, sem):
     for k, unit_ref in enumerate(unit_refs):
         meta = unit_ref[pl.ds(len(slots[k]) * size, META), :].astype(jnp.float32).astype(jnp.int32)
         meta_ref[pl.ds(8 * k, 8), :] = meta[:8]
     copy = pltpu.make_async_copy(meta_ref, index_ref, sem)
     copy.start()
     copy.wait()
-    for k, unit_ref in enumerate(unit_refs):
-        for q, step in enumerate(slots[k]):
-            row = index_ref[8 * k, q]
-            col = index_ref[8 * k, len(slots[k]) + q]
-            product = jnp.dot(
-                unit_ref[pl.ds(q * size, size), :],
-                panel_ref[step, pl.ds(pl.multiple_of(col * size, size), size), :],
-                preferred_element_type=jnp.float32,
-            )
-            at = pl.ds(pl.multiple_of(row * size, size), size)
-            acc_ref[at, :] = acc_ref[at, :] + product
+
+
+def add_unit(k, slots, size, unit_ref, panel_ref, acc_ref, index_ref):
+    for q, step in enumerate(slots[k]):
+        row = index_ref[8 * k, q]
+        col = index_ref[8 * k, len(slots[k]) + q]
+        product = jnp.dot(
+            unit_ref[pl.ds(q * size, size), :],
+            panel_ref[step, pl.ds(pl.multiple_of(col * size, size), size), :],
+            preferred_element_type=jnp.float32,
+        )
+        at = pl.ds(pl.multiple_of(row * size, size), size)
+        acc_ref[at, :] = acc_ref[at, :] + product
 
 
 def fold_kernel(*refs, slots, size):
     n = len(slots)
     unit_refs, (panel_ref, _, acc_ref, meta_ref, index_ref, sem) = refs[:n], refs[n:]
-    add_units(slots, size, unit_refs, panel_ref, acc_ref, meta_ref, index_ref, sem)
+    read_index(slots, size, unit_refs, meta_ref, index_ref, sem)
+    for k, unit_ref in enumerate(unit_refs):
+        add_unit(k, slots, size, unit_ref, panel_ref, acc_ref, index_ref)
 
 
 def last_kernel(*refs, slots, size):
     n = len(slots)
     unit_refs, (panel_ref, _, acc_ref, out_ref, meta_ref, index_ref, sem, out_sem) = refs[:n], refs[n:]
-    add_units(slots, size, unit_refs, panel_ref, acc_ref, meta_ref, index_ref, sem)
-    copy = pltpu.make_async_copy(acc_ref.at[pl.ds(0, out_ref.shape[0])], out_ref, out_sem)
-    copy.start()
-    copy.wait()
+    read_index(slots, size, unit_refs, meta_ref, index_ref, sem)
+    touched = [jnp.int32(0)]
+    for k in reversed(range(n)):
+        mask = touched[0]
+        for q in range(len(slots[k])):
+            row = index_ref[8 * k, q]
+            mask = mask | jnp.where(row < RB_DEV, lax.shift_left(jnp.int32(1), row), 0)
+        touched.insert(0, mask)
+
+    def write(ready):
+        for row in range(RB_DEV):
+            at = pl.ds(row * size, size)
+
+            @pl.when((lax.shift_right_logical(ready, jnp.int32(row)) & 1) == 1)
+            def _():
+                pltpu.make_async_copy(acc_ref.at[at], out_ref.at[at], out_sem).start()
+
+    write(~touched[0])
+    for k, unit_ref in enumerate(unit_refs):
+        add_unit(k, slots, size, unit_ref, panel_ref, acc_ref, index_ref)
+        write(touched[k] & ~touched[k + 1])
+    pltpu.make_async_copy(acc_ref.at[pl.ds(0, out_ref.shape[0])], out_ref, out_sem).wait()
 
 
 def fold(units, slots, panels, acc, last):

time: 58.7 us -> 57 us (0.971)
  waiting for transfers between devices: 13.3 us -> 11.3 us
  Pallas kernels: 14.6 us -> 15.2 us
    ppermute x15, waiting for transfers between devices: 13.3 us -> 11.3 us  [hop(): return lax.ppermute(unit, ('row', 'col'), pairs)]
    pallas_call x8 -> x10, Pallas kernels: 12.3 us -> 12.9 us  [fold(): pl.pallas_call(functools.partial(last_kernel if last else fold_kernel, sl...]
  transfers between devices with their start and end apart: 16 -> 16, of which waited for: 7 -> 6; matrix products, arithmetic and copies ran while one was open for 0% -> 0% of each run, Pallas kernels for 19% -> 22%
where the time goes in v4:
time: 57 us; the launch traced here: 56.8 us
  starting transfers between devices  30.2 us (53%)
  Pallas kernels  15.2 us (27%)
  waiting for transfers between devices  11.3 us (20%)
    ppermute x15, starting transfers between devices, hop(): return lax.ppermute(unit, ('row', 'col'), pairs)  29.8 us
    pallas_call x10, Pallas kernels, fold(): pl.pallas_call(functools.partial(last_kernel if last else fold_kernel, sl...  12.9 us
    ppermute x15, waiting for transfers between devices, hop(): return lax.ppermute(unit, ('row', 'col'), pairs)  11.3 us
    pallas_call x1, Pallas kernels, whole_panels(): pl.pallas_call(functools.partial(panel_kernel, n_row=n_row), out_shape=(p...  1.24 us
  transfers between devices with their start and end apart: 16, of which 6 were waited for; matrix products, arithmetic and copies ran while one was open for 0% of the time, Pallas kernels for 22%

profile of v4, /device:TPU:0, one launch (start us, length us, event | category | flops | bytes accessed | tf_op | source)
XLA Modules:
  0.0 56.8 jit_solution(11039061873199193365)
XLA Ops:
  0.0 0.5 collective-permute-start.1
  0.5 1.0 %pack.1.refs_0_ = bf16[1552,128]{1,0:T(8,128)(2,1)S(1)} custom-call(s32[2,1,6]{2,1,0:T(1,128)} %rows_hbm.1, s32[2,1,6]{2,1,0:T(1,128)} %cols_hbm.1, s32[2]{0:T(128)} %bitcast.3, bf16[1536,128]{1,0:T(8,128)(2,1)} %bitcast.2), custom_call_target="tpu_custom_call" | custom-call | tf_op jit(solution)/shard_map/pack/pallas_call | solution.py:118
  1.5 2.6 %collective-permute-start = (bf16[1552,128]{1,0:T(8,128)(2,1)S(1)}, bf16[1552,128]{1,0:T(8,128)(2,1)S(1)}, u32[]{:S(2)}, u32[]{:S(2)}) collective-permute-start(bf16[1552,128]{1,0:T(8,128)(2,1)S(1)} %pack.1.refs_0_), channel_id=1, source_target_pairs={{0,1},{1,0},{2,3},{3,2},{4,5},{5,4},{6,7},{7,6},{8,9},{9,8},{10,11... | collective-permute-start | bytes 1191944 | tf_op jit(solution)/shard_map/ppermute | solution.py:60
  4.0 2.6 %collective-permute-start.2 = (bf16[1552,128]{1,0:T(8,128)(2,1)S(1)}, bf16[1552,128]{1,0:T(8,128)(2,1)S(1)}, u32[]{:S(2)}, u32[]{:S(2)}) collective-permute-start(bf16[1552,128]{1,0:T(8,128)(2,1)S(1)} %pack.1.refs_0_), channel_id=1, source_target_pairs={{0,8},{1,9},{2,10},{3,11},{4,0},{5,1},{6,2},{7,3},{8,12},{9,13},{1... | collective-permute-start | bytes 1191944 | tf_op jit(solution)/shard_map/ppermute | solution.py:60
  6.6 1.5 %collective-permute-start.3 = (bf16[1552,128]{1,0:T(8,128)(2,1)S(1)}, bf16[1552,128]{1,0:T(8,128)(2,1)S(1)}, u32[]{:S(2)}, u32[]{:S(2)}) collective-permute-start(bf16[1552,128]{1,0:T(8,128)(2,1)S(1)} %pack.1.refs_0_), channel_id=1, source_target_pairs={{0,2},{1,3},{2,0},{3,1},{4,6},{5,7},{6,4},{7,5},{8,10},{9,11},{10,... | collective-permute-start | bytes 1191944 | tf_op jit(solution)/shard_map/ppermute | solution.py:60
  8.2 0.0 collective-permute-done.1.refs_1_
  8.2 1.2 %panels.1 = (bf16[2,2048,256]{2,1,0:T(8,128)(2,1)S(1)}, f32[4224,256]{1,0:T(8,128)S(1)}) custom-call(bf16[2,1024,256]{2,1,0:T(8,128)(2,1)} %refs_0_.1, bf16[2,1024,256]{2,1,0:T(8,128)(2,1)S(1)} %collective-permute-done.1.refs_1_), custom_call_target="tpu_custom_call" | custom-call | tf_op jit(solution)/shard_map/panels/pallas_call | solution.py:159
  9.4 1.0 %fold.9.refs_4_ = f32[4224,256]{1,0:T(8,128)S(1)} custom-call(bf16[1552,128]{1,0:T(8,128)(2,1)S(1)} %pack.1.refs_0_, bf16[2,2048,256]{2,1,0:T(8,128)(2,1)S(1)} %get-tuple-element.39.refs_1_.refs_3_.refs_2_, f32[4224,256]{1,0:T(8,128)S(1)} %get-tuple-element.40.refs_2_), custom_call_target="tpu_custom_call", output_to_operand_aliasing={{}: (2, {})} | custom-call | flops 100663296 | bytes 393216 | tf_op jit(solution)/shard_map/fold/pallas_call | solution.py:243
  10.4 0.1 collective-permute-done.refs_0_
  10.5 4.8 %collective-permute-start.4 = (bf16[1552,128]{1,0:T(8,128)(2,1)S(1)}, bf16[1552,128]{1,0:T(8,128)(2,1)S(1)}, u32[]{:S(2)}, u32[]{:S(2)}) collective-permute-start(bf16[1552,128]{1,0:T(8,128)(2,1)S(1)} %collective-permute-done.refs_0_), channel_id=1, source_target_pairs={{0,4},{1,5},{2,6},{3,7},{4,12},{5,13},{6,14},{7,15},{8,0},{9,1},{1... | collective-permute-start | bytes 1191944 | tf_op jit(solution)/shard_map/ppermute | solution.py:60
  15.3 0.9 %collective-permute-done.2.refs_1_ = bf16[1552,128]{1,0:T(8,128)(2,1)S(1)} collective-permute-done((bf16[1552,128]{1,0:T(8,128)(2,1)S(1)}, bf16[1552,128]{1,0:T(8,128)(2,1)S(1)}, u32[]{:S(2)}, u32[]{:S(2)}) %collective-permute-start.2) | collective-permute-done | bytes 397344 | tf_op jit(solution)/shard_map/ppermute | solution.py:60
  16.2 1.3 %collective-permute-start.5 = (bf16[1552,128]{1,0:T(8,128)(2,1)S(1)}, bf16[1552,128]{1,0:T(8,128)(2,1)S(1)}, u32[]{:S(2)}, u32[]{:S(2)}) collective-permute-start(bf16[1552,128]{1,0:T(8,128)(2,1)S(1)} %collective-permute-done.2.refs_1_), channel_id=1, source_target_pairs={{0,2},{1,3},{2,0},{3,1},{4,6},{5,7},{6,4},{7,5},{8,10},{9,11},{10,... | collective-permute-start | bytes 1191944 | tf_op jit(solution)/shard_map/ppermute | solution.py:60
  17.5 1.7 %collective-permute-start.6 = (bf16[1552,128]{1,0:T(8,128)(2,1)S(1)}, bf16[1552,128]{1,0:T(8,128)(2,1)S(1)}, u32[]{:S(2)}, u32[]{:S(2)}) collective-permute-start(bf16[1552,128]{1,0:T(8,128)(2,1)S(1)} %collective-permute-done.2.refs_1_), channel_id=1, source_target_pairs={{0,1},{1,0},{2,3},{3,2},{4,5},{5,4},{6,7},{7,6},{8,9},{9,8},{10,11... | collective-permute-start | bytes 1191944 | tf_op jit(solution)/shard_map/ppermute | solution.py:60
  19.2 0.0 collective-permute-done.3.refs_2_
  19.2 2.5 %collective-permute-start.7 = (bf16[1552,128]{1,0:T(8,128)(2,1)S(1)}, bf16[1552,128]{1,0:T(8,128)(2,1)S(1)}, u32[]{:S(2)}, u32[]{:S(2)}) collective-permute-start(bf16[1552,128]{1,0:T(8,128)(2,1)S(1)} %collective-permute-done.3.refs_2_), channel_id=1, source_target_pairs={{0,4},{1,5},{2,6},{3,7},{4,12},{5,13},{6,14},{7,15},{8,0},{9,1},{1... | collective-permute-start | bytes 1191944 | tf_op jit(solution)/shard_map/ppermute | solution.py:60
  21.6 1.6 %fold.10.refs_2_ = f32[4224,256]{1,0:T(8,128)S(1)} custom-call(bf16[1552,128]{1,0:T(8,128)(2,1)S(1)} %collective-permute-done.refs_0_, bf16[1552,128]{1,0:T(8,128)(2,1)S(1)} %collective-permute-done.2.refs_1_, bf16[1552,128]{1,0:T(8,128)(2,1)S(1)} %collective-permute-done.3.refs_2_, ...), custom_call_target="tpu_custom_call", output_to_operand_aliasing={{}: (4, {})} | custom-call | flops 301989888 | bytes 1179648 | tf_op jit(solution)/shard_map/fold/pallas_call | solution.py:243
  23.2 0.1 collective-permute-start.10
  23.3 2.6 %collective-permute-done.4.refs_0_ = bf16[1552,128]{1,0:T(8,128)(2,1)S(1)} collective-permute-done((bf16[1552,128]{1,0:T(8,128)(2,1)S(1)}, bf16[1552,128]{1,0:T(8,128)(2,1)S(1)}, u32[]{:S(2)}, u32[]{:S(2)}) %collective-permute-start.4) | collective-permute-done | bytes 397344 | tf_op jit(solution)/shard_map/ppermute | solution.py:60
  25.9 1.0 %fold.11.refs_2_ = f32[4224,256]{1,0:T(8,128)S(1)} custom-call(bf16[1552,128]{1,0:T(8,128)(2,1)S(1)} %collective-permute-done.4.refs_0_, bf16[2,2048,256]{2,1,0:T(8,128)(2,1)S(1)} %get-tuple-element.39.refs_1_.refs_3_.refs_2_, f32[4224,256]{1,0:T(8,128)S(1)} %fold.10.refs_2_), custom_call_target="tpu_custom_call", output_to_operand_aliasing={{}: (2, {})} | custom-call | flops 100663296 | bytes 393216 | tf_op jit(solution)/shard_map/fold/pallas_call | solution.py:243
  26.9 1.8 %collective-permute-start.9 = (bf16[1552,128]{1,0:T(8,128)(2,1)S(1)}, bf16[1552,128]{1,0:T(8,128)(2,1)S(1)}, u32[]{:S(2)}, u32[]{:S(2)}) collective-permute-start(bf16[1552,128]{1,0:T(8,128)(2,1)S(1)} %collective-permute-done.4.refs_0_), channel_id=1, source_target_pairs={{0,4},{1,5},{2,6},{3,7},{4,12},{5,13},{6,14},{7,15},{8,0},{9,1},{1... | collective-permute-start | bytes 1191944 | tf_op jit(solution)/shard_map/ppermute | solution.py:60
  28.7 0.0 collective-permute-done.5.refs_0_
  28.7 1.5 %collective-permute-start.15 = (bf16[1552,128]{1,0:T(8,128)(2,1)S(1)}, bf16[1552,128]{1,0:T(8,128)(2,1)S(1)}, u32[]{:S(2)}, u32[]{:S(2)}) collective-permute-start(bf16[1552,128]{1,0:T(8,128)(2,1)S(1)} %collective-permute-done.4.refs_0_), channel_id=1, source_target_pairs={{0,1},{1,0},{2,3},{3,2},{4,5},{5,4},{6,7},{7,6},{8,9},{9,8},{10,11... | collective-permute-start | bytes 1191944 | tf_op jit(solution)/shard_map/ppermute | solution.py:60
  30.2 1.0 %fold.12.refs_2_ = f32[4224,256]{1,0:T(8,128)S(1)} custom-call(bf16[1552,128]{1,0:T(8,128)(2,1)S(1)} %collective-permute-done.5.refs_0_, bf16[2,2048,256]{2,1,0:T(8,128)(2,1)S(1)} %get-tuple-element.39.refs_1_.refs_3_.refs_2_, f32[4224,256]{1,0:T(8,128)S(1)} %fold.11.refs_2_), custom_call_target="tpu_custom_call", output_to_operand_aliasing={{}: (2, {})} | custom-call | flops 100663296 | bytes 393216 | tf_op jit(solution)/shard_map/fold/pallas_call | solution.py:243
  31.2 0.0 collective-permute-done.6.refs_0_
  31.2 2.2 %collective-permute-start.14 = (bf16[1552,128]{1,0:T(8,128)(2,1)S(1)}, bf16[1552,128]{1,0:T(8,128)(2,1)S(1)}, u32[]{:S(2)}, u32[]{:S(2)}) collective-permute-start(bf16[1552,128]{1,0:T(8,128)(2,1)S(1)} %collective-permute-done.4.refs_0_), channel_id=1, source_target_pairs={{0,2},{1,3},{2,0},{3,1},{4,6},{5,7},{6,4},{7,5},{8,10},{9,11},{10,... | collective-permute-start | bytes 1191944 | tf_op jit(solution)/shard_map/ppermute | solution.py:60
  33.4 1.0 %fold.13.refs_3_ = f32[4224,256]{1,0:T(8,128)S(1)} custom-call(bf16[1552,128]{1,0:T(8,128)(2,1)S(1)} %collective-permute-done.6.refs_0_, bf16[2,2048,256]{2,1,0:T(8,128)(2,1)S(1)} %get-tuple-element.39.refs_1_.refs_3_.refs_2_, f32[4224,256]{1,0:T(8,128)S(1)} %fold.12.refs_2_), custom_call_target="tpu_custom_call", output_to_operand_aliasing={{}: (2, {})} | custom-call | flops 100663296 | bytes 393216 | tf_op jit(solution)/shard_map/fold/pallas_call | solution.py:243
  34.4 0.0 collective-permute-done.7.refs_0_
  34.4 1.2 %collective-permute-start.13 = (bf16[1552,128]{1,0:T(8,128)(2,1)S(1)}, bf16[1552,128]{1,0:T(8,128)(2,1)S(1)}, u32[]{:S(2)}, u32[]{:S(2)}) collective-permute-start(bf16[1552,128]{1,0:T(8,128)(2,1)S(1)} %collective-permute-done.5.refs_0_), channel_id=1, source_target_pairs={{0,1},{1,0},{2,3},{3,2},{4,5},{5,4},{6,7},{7,6},{8,9},{9,8},{10,11... | collective-permute-start | bytes 1191944 | tf_op jit(solution)/shard_map/ppermute | solution.py:60
  35.7 0.0 collective-permute-done.10.refs_1_
  35.7 2.7 %collective-permute-start.8 = (bf16[1552,128]{1,0:T(8,128)(2,1)S(1)}, bf16[1552,128]{1,0:T(8,128)(2,1)S(1)}, u32[]{:S(2)}, u32[]{:S(2)}) collective-permute-start(bf16[1552,128]{1,0:T(8,128)(2,1)S(1)} %collective-permute-done.7.refs_0_), channel_id=1, source_target_pairs={{0,4},{1,5},{2,6},{3,7},{4,12},{5,13},{6,14},{7,15},{8,0},{9,1},{1... | collective-permute-start | bytes 1191944 | tf_op jit(solution)/shard_map/ppermute | solution.py:60
  38.4 1.3 %fold.14.refs_3_ = f32[4224,256]{1,0:T(8,128)S(1)} custom-call(bf16[1552,128]{1,0:T(8,128)(2,1)S(1)} %collective-permute-done.7.refs_0_, bf16[1552,128]{1,0:T(8,128)(2,1)S(1)} %collective-permute-done.10.refs_1_, bf16[2,2048,256]{2,1,0:T(8,128)(2,1)S(1)} %get-tuple-element.39.refs_1_.refs_3_.refs_2_, ...), custom_call_target="tpu_custom_call", output_to_operand_aliasing={{}: (3, {})} | custom-call | flops 201326592 | bytes 786432 | tf_op jit(solution)/shard_map/fold/pallas_call | solution.py:243
  39.7 3.3 %collective-permute-done.9.refs_0_ = bf16[1552,128]{1,0:T(8,128)(2,1)S(1)} collective-permute-done((bf16[1552,128]{1,0:T(8,128)(2,1)S(1)}, bf16[1552,128]{1,0:T(8,128)(2,1)S(1)}, u32[]{:S(2)}, u32[]{:S(2)}) %collective-permute-start.9) | collective-permute-done | bytes 397344 | tf_op jit(solution)/shard_map/ppermute | solution.py:60
  43.0 1.2 %collective-permute-start.12 = (bf16[1552,128]{1,0:T(8,128)(2,1)S(1)}, bf16[1552,128]{1,0:T(8,128)(2,1)S(1)}, u32[]{:S(2)}, u32[]{:S(2)}) collective-permute-start(bf16[1552,128]{1,0:T(8,128)(2,1)S(1)} %collective-permute-done.9.refs_0_), channel_id=1, source_target_pairs={{0,1},{1,0},{2,3},{3,2},{4,5},{5,4},{6,7},{7,6},{8,9},{9,8},{10,11... | collective-permute-start | bytes 1191944 | tf_op jit(solution)/shard_map/ppermute | solution.py:60
  44.2 0.0 collective-permute-done.15.refs_1_
  44.2 2.1 %collective-permute-start.11 = (bf16[1552,128]{1,0:T(8,128)(2,1)S(1)}, bf16[1552,128]{1,0:T(8,128)(2,1)S(1)}, u32[]{:S(2)}, u32[]{:S(2)}) collective-permute-start(bf16[1552,128]{1,0:T(8,128)(2,1)S(1)} %collective-permute-done.9.refs_0_), channel_id=1, source_target_pairs={{0,2},{1,3},{2,0},{3,1},{4,6},{5,7},{6,4},{7,5},{8,10},{9,11},{10,... | collective-permute-start | bytes 1191944 | tf_op jit(solution)/shard_map/ppermute | solution.py:60
  46.3 1.3 %fold.15.refs_2_ = f32[4224,256]{1,0:T(8,128)S(1)} custom-call(bf16[1552,128]{1,0:T(8,128)(2,1)S(1)} %collective-permute-done.9.refs_0_, bf16[1552,128]{1,0:T(8,128)(2,1)S(1)} %collective-permute-done.15.refs_1_, bf16[2,2048,256]{2,1,0:T(8,128)(2,1)S(1)} %get-tuple-element.39.refs_1_.refs_3_.refs_2_, ...), custom_call_target="tpu_custom_call", output_to_operand_aliasing={{}: (3, {})} | custom-call | flops 201326592 | bytes 786432 | tf_op jit(solution)/shard_map/fold/pallas_call | solution.py:243
  47.6 0.0 collective-permute-done.14.refs_0_
  47.6 1.0 %fold.16.refs_2_ = f32[4224,256]{1,0:T(8,128)S(1)} custom-call(bf16[1552,128]{1,0:T(8,128)(2,1)S(1)} %collective-permute-done.14.refs_0_, bf16[2,2048,256]{2,1,0:T(8,128)(2,1)S(1)} %get-tuple-element.39.refs_1_.refs_3_.refs_2_, f32[4224,256]{1,0:T(8,128)S(1)} %fold.15.refs_2_), custom_call_target="tpu_custom_call", output_to_operand_aliasing={{}: (2, {})} | custom-call | flops 100663296 | bytes 393216 | tf_op jit(solution)/shard_map/fold/pallas_call | solution.py:243
  48.6 0.0 collective-permute-done.13.refs_0_
  48.6 1.0 %fold.17.refs_4_ = f32[4224,256]{1,0:T(8,128)S(1)} custom-call(bf16[1552,128]{1,0:T(8,128)(2,1)S(1)} %collective-permute-done.13.refs_0_, bf16[2,2048,256]{2,1,0:T(8,128)(2,1)S(1)} %get-tuple-element.39.refs_1_.refs_3_.refs_2_, f32[4224,256]{1,0:T(8,128)S(1)} %fold.16.refs_2_), custom_call_target="tpu_custom_call", output_to_operand_aliasing={{}: (2, {})} | custom-call | flops 100663296 | bytes 393216 | tf_op jit(solution)/shard_map/fold/pallas_call | solution.py:243
  49.6 1.8 %collective-permute-done.8.refs_0_ = bf16[1552,128]{1,0:T(8,128)(2,1)S(1)} collective-permute-done((bf16[1552,128]{1,0:T(8,128)(2,1)S(1)}, bf16[1552,128]{1,0:T(8,128)(2,1)S(1)}, u32[]{:S(2)}, u32[]{:S(2)}) %collective-permute-start.8) | collective-permute-done | bytes 397344 | tf_op jit(solution)/shard_map/ppermute | solution.py:60
  51.4 2.6 %collective-permute-done.12.refs_2_ = bf16[1552,128]{1,0:T(8,128)(2,1)S(1)} collective-permute-done((bf16[1552,128]{1,0:T(8,128)(2,1)S(1)}, bf16[1552,128]{1,0:T(8,128)(2,1)S(1)}, u32[]{:S(2)}, u32[]{:S(2)}) %collective-permute-start.12) | collective-permute-done | bytes 397344 | tf_op jit(solution)/shard_map/ppermute | solution.py:60
  54.0 0.0 collective-permute-done.11.refs_1_
  54.0 2.8 %last.1 = (f32[4224,256]{1,0:T(8,128)S(1)}, f32[4096,256]{1,0:T(8,128)}) custom-call(bf16[1552,128]{1,0:T(8,128)(2,1)S(1)} %collective-permute-done.8.refs_0_, bf16[1552,128]{1,0:T(8,128)(2,1)S(1)} %collective-permute-done.11.refs_1_, bf16[1552,128]{1,0:T(8,128)(2,1)S(1)} %collective-permute-done.12.refs_2_, ...), custom_call_target="tpu_custom_call", output_to_operand_aliasing={{0}: (4, {})} | custom-call | flops 301989888 | bytes 1179648 | tf_op jit(solution)/shard_map/last/pallas_call | solution.py:243
Async XLA Ops:
  0.0 8.2 %collective-permute-start.1 = (bf16[2,1024,256]{2,1,0:T(8,128)(2,1)}, bf16[2,1024,256]{2,1,0:T(8,128)(2,1)S(1)}, u32[]{:S(2)}, u32[]{:S(2)}) collective-permute-start(bf16[2,1024,256]{2,1,0:T(8,128)(2,1)} %refs_0_.1), channel_id=1, source_target_pairs={{0,16},{16,0},{1,17},{17,1},{2,18},{18,2},{3,19},{19,3},{4,20},{20... | collective-permute-start | bytes 3145736 | tf_op jit(solution)/shard_map/ppermute | solution.py:265
  1.5 9.0 %collective-permute-start = (bf16[1552,128]{1,0:T(8,128)(2,1)S(1)}, bf16[1552,128]{1,0:T(8,128)(2,1)S(1)}, u32[]{:S(2)}, u32[]{:S(2)}) collective-permute-start(bf16[1552,128]{1,0:T(8,128)(2,1)S(1)} %pack.1.refs_0_), channel_id=1, source_target_pairs={{0,1},{1,0},{2,3},{3,2},{4,5},{5,4},{6,7},{7,6},{8,9},{9,8},{10,11... | collective-permute-start | bytes 1191944 | tf_op jit(solution)/shard_map/ppermute | solution.py:60
  4.0 12.1 %collective-permute-start.2 = (bf16[1552,128]{1,0:T(8,128)(2,1)S(1)}, bf16[1552,128]{1,0:T(8,128)(2,1)S(1)}, u32[]{:S(2)}, u32[]{:S(2)}) collective-permute-start(bf16[1552,128]{1,0:T(8,128)(2,1)S(1)} %pack.1.refs_0_), channel_id=1, source_target_pairs={{0,8},{1,9},{2,10},{3,11},{4,0},{5,1},{6,2},{7,3},{8,12},{9,13},{1... | collective-permute-start | bytes 1191944 | tf_op jit(solution)/shard_map/ppermute | solution.py:60
  6.6 12.5 %collective-permute-start.3 = (bf16[1552,128]{1,0:T(8,128)(2,1)S(1)}, bf16[1552,128]{1,0:T(8,128)(2,1)S(1)}, u32[]{:S(2)}, u32[]{:S(2)}) collective-permute-start(bf16[1552,128]{1,0:T(8,128)(2,1)S(1)} %pack.1.refs_0_), channel_id=1, source_target_pairs={{0,2},{1,3},{2,0},{3,1},{4,6},{5,7},{6,4},{7,5},{8,10},{9,11},{10,... | collective-permute-start | bytes 1191944 | tf_op jit(solution)/shard_map/ppermute | solution.py:60
  10.5 15.4 %collective-permute-start.4 = (bf16[1552,128]{1,0:T(8,128)(2,1)S(1)}, bf16[1552,128]{1,0:T(8,128)(2,1)S(1)}, u32[]{:S(2)}, u32[]{:S(2)}) collective-permute-start(bf16[1552,128]{1,0:T(8,128)(2,1)S(1)} %collective-permute-done.refs_0_), channel_id=1, source_target_pairs={{0,4},{1,5},{2,6},{3,7},{4,12},{5,13},{6,14},{7,15},{8,0},{9,1},{1... | collective-permute-start | bytes 1191944 | tf_op jit(solution)/shard_map/ppermute | solution.py:60
  16.2 12.5 %collective-permute-start.5 = (bf16[1552,128]{1,0:T(8,128)(2,1)S(1)}, bf16[1552,128]{1,0:T(8,128)(2,1)S(1)}, u32[]{:S(2)}, u32[]{:S(2)}) collective-permute-start(bf16[1552,128]{1,0:T(8,128)(2,1)S(1)} %collective-permute-done.2.refs_1_), channel_id=1, source_target_pairs={{0,2},{1,3},{2,0},{3,1},{4,6},{5,7},{6,4},{7,5},{8,10},{9,11},{10,... | collective-permute-start | bytes 1191944 | tf_op jit(solution)/shard_map/ppermute | solution.py:60
  17.5 13.7 %collective-permute-start.6 = (bf16[1552,128]{1,0:T(8,128)(2,1)S(1)}, bf16[1552,128]{1,0:T(8,128)(2,1)S(1)}, u32[]{:S(2)}, u32[]{:S(2)}) collective-permute-start(bf16[1552,128]{1,0:T(8,128)(2,1)S(1)} %collective-permute-done.2.refs_1_), channel_id=1, source_target_pairs={{0,1},{1,0},{2,3},{3,2},{4,5},{5,4},{6,7},{7,6},{8,9},{9,8},{10,11... | collective-permute-start | bytes 1191944 | tf_op jit(solution)/shard_map/ppermute | solution.py:60
  19.2 15.3 %collective-permute-start.7 = (bf16[1552,128]{1,0:T(8,128)(2,1)S(1)}, bf16[1552,128]{1,0:T(8,128)(2,1)S(1)}, u32[]{:S(2)}, u32[]{:S(2)}) collective-permute-start(bf16[1552,128]{1,0:T(8,128)(2,1)S(1)} %collective-permute-done.3.refs_2_), channel_id=1, source_target_pairs={{0,4},{1,5},{2,6},{3,7},{4,12},{5,13},{6,14},{7,15},{8,0},{9,1},{1... | collective-permute-start | bytes 1191944 | tf_op jit(solution)/shard_map/ppermute | solution.py:60
  23.2 12.5 %collective-permute-start.10 = (bf16[1552,128]{1,0:T(8,128)(2,1)S(1)}, bf16[1552,128]{1,0:T(8,128)(2,1)S(1)}, u32[]{:S(2)}, u32[]{:S(2)}) collective-permute-start(bf16[1552,128]{1,0:T(8,128)(2,1)S(1)} %collective-permute-done.refs_0_), channel_id=1, source_target_pairs={{0,2},{1,3},{2,0},{3,1},{4,6},{5,7},{6,4},{7,5},{8,10},{9,11},{10,... | collective-permute-start | bytes 1191944 | tf_op jit(solution)/shard_map/ppermute | solution.py:60
  26.9 16.0 %collective-permute-start.9 = (bf16[1552,128]{1,0:T(8,128)(2,1)S(1)}, bf16[1552,128]{1,0:T(8,128)(2,1)S(1)}, u32[]{:S(2)}, u32[]{:S(2)}) collective-permute-start(bf16[1552,128]{1,0:T(8,128)(2,1)S(1)} %collective-permute-done.4.refs_0_), channel_id=1, source_target_pairs={{0,4},{1,5},{2,6},{3,7},{4,12},{5,13},{6,14},{7,15},{8,0},{9,1},{1... | collective-permute-start | bytes 1191944 | tf_op jit(solution)/shard_map/ppermute | solution.py:60
  28.7 15.5 %collective-permute-start.15 = (bf16[1552,128]{1,0:T(8,128)(2,1)S(1)}, bf16[1552,128]{1,0:T(8,128)(2,1)S(1)}, u32[]{:S(2)}, u32[]{:S(2)}) collective-permute-start(bf16[1552,128]{1,0:T(8,128)(2,1)S(1)} %collective-permute-done.4.refs_0_), channel_id=1, source_target_pairs={{0,1},{1,0},{2,3},{3,2},{4,5},{5,4},{6,7},{7,6},{8,9},{9,8},{10,11... | collective-permute-start | bytes 1191944 | tf_op jit(solution)/shard_map/ppermute | solution.py:60
  31.2 16.4 %collective-permute-start.14 = (bf16[1552,128]{1,0:T(8,128)(2,1)S(1)}, bf16[1552,128]{1,0:T(8,128)(2,1)S(1)}, u32[]{:S(2)}, u32[]{:S(2)}) collective-permute-start(bf16[1552,128]{1,0:T(8,128)(2,1)S(1)} %collective-permute-done.4.refs_0_), channel_id=1, source_target_pairs={{0,2},{1,3},{2,0},{3,1},{4,6},{5,7},{6,4},{7,5},{8,10},{9,11},{10,... | collective-permute-start | bytes 1191944 | tf_op jit(solution)/shard_map/ppermute | solution.py:60
  34.4 14.2 %collective-permute-start.13 = (bf16[1552,128]{1,0:T(8,128)(2,1)S(1)}, bf16[1552,128]{1,0:T(8,128)(2,1)S(1)}, u32[]{:S(2)}, u32[]{:S(2)}) collective-permute-start(bf16[1552,128]{1,0:T(8,128)(2,1)S(1)} %collective-permute-done.5.refs_0_), channel_id=1, source_target_pairs={{0,1},{1,0},{2,3},{3,2},{4,5},{5,4},{6,7},{7,6},{8,9},{9,8},{10,11... | collective-permute-start | bytes 1191944 | tf_op jit(solution)/shard_map/ppermute | solution.py:60
  35.7 15.7 %collective-permute-start.8 = (bf16[1552,128]{1,0:T(8,128)(2,1)S(1)}, bf16[1552,128]{1,0:T(8,128)(2,1)S(1)}, u32[]{:S(2)}, u32[]{:S(2)}) collective-permute-start(bf16[1552,128]{1,0:T(8,128)(2,1)S(1)} %collective-permute-done.7.refs_0_), channel_id=1, source_target_pairs={{0,4},{1,5},{2,6},{3,7},{4,12},{5,13},{6,14},{7,15},{8,0},{9,1},{1... | collective-permute-start | bytes 1191944 | tf_op jit(solution)/shard_map/ppermute | solution.py:60
  43.0 11.0 %collective-permute-start.12 = (bf16[1552,128]{1,0:T(8,128)(2,1)S(1)}, bf16[1552,128]{1,0:T(8,128)(2,1)S(1)}, u32[]{:S(2)}, u32[]{:S(2)}) collective-permute-start(bf16[1552,128]{1,0:T(8,128)(2,1)S(1)} %collective-permute-done.9.refs_0_), channel_id=1, source_target_pairs={{0,1},{1,0},{2,3},{3,2},{4,5},{5,4},{6,7},{7,6},{8,9},{9,8},{10,11... | collective-permute-start | bytes 1191944 | tf_op jit(solution)/shard_map/ppermute | solution.py:60
  44.2 9.8 %collective-permute-start.11 = (bf16[1552,128]{1,0:T(8,128)(2,1)S(1)}, bf16[1552,128]{1,0:T(8,128)(2,1)S(1)}, u32[]{:S(2)}, u32[]{:S(2)}) collective-permute-start(bf16[1552,128]{1,0:T(8,128)(2,1)S(1)} %collective-permute-done.9.refs_0_), channel_id=1, source_target_pairs={{0,2},{1,3},{2,0},{3,1},{4,6},{5,7},{6,4},{7,5},{8,10},{9,11},{10,... | collective-permute-start | bytes 1191944 | tf_op jit(solution)/shard_map/ppermute | solution.py:60

commit v5 on v4

--- a/solution.py
+++ b/solution.py
@@ -34,7 +34,8 @@
     [(0, 6), (0, 3)],
     (0, 11, 1),
     (0, 8, 0),
-    [(0, 9), (0, 4)],
+    [(0, 9)],
+    [(0, 4)],
     [(0, 7)],
     [(0, 15)],
 ]

time: 57 us -> 57 us (level)
  Pallas kernels: 15.2 us -> 15.9 us
  waiting for transfers between devices: 11.3 us -> 10.6 us
    ppermute x15, waiting for transfers between devices: 11.3 us -> 10.6 us  [hop(): return lax.ppermute(unit, ('row', 'col'), pairs)]
    pallas_call x10 -> x11, Pallas kernels: 12.9 us -> 13.6 us  [fold(): pl.pallas_call(functools.partial(last_kernel if last else fold_kernel, sl...]
  transfers between devices with their start and end apart: 16 -> 16, of which waited for: 6 -> 6; matrix products, arithmetic and copies ran while one was open for 0% -> 0% of each run, Pallas kernels for 22% -> 23%
where the time goes in v5:
time: 57 us; the launch traced here: 56.8 us
  starting transfers between devices  30.2 us (53%)
  Pallas kernels  15.9 us (28%)
  waiting for transfers between devices  10.6 us (19%)
    ppermute x15, starting transfers between devices, hop(): return lax.ppermute(unit, ('row', 'col'), pairs)  29.8 us
    pallas_call x11, Pallas kernels, fold(): pl.pallas_call(functools.partial(last_kernel if last else fold_kernel, sl...  13.6 us
    ppermute x15, waiting for transfers between devices, hop(): return lax.ppermute(unit, ('row', 'col'), pairs)  10.6 us
    pallas_call x1, Pallas kernels, whole_panels(): pl.pallas_call(functools.partial(panel_kernel, n_row=n_row), out_shape=(p...  1.24 us
  transfers between devices with their start and end apart: 16, of which 6 were waited for; matrix products, arithmetic and copies ran while one was open for 0% of the time, Pallas kernels for 23%

profile of v5, /device:TPU:0, one launch (start us, length us, event | category | flops | bytes accessed | tf_op | source)
XLA Modules:
  0.0 56.8 jit_solution(16145872391774952803)
XLA Ops:
  0.0 0.5 collective-permute-start.1
  0.5 1.0 %pack.1.refs_0_ = bf16[1552,128]{1,0:T(8,128)(2,1)S(1)} custom-call(s32[2,1,6]{2,1,0:T(1,128)} %rows_hbm.1, s32[2,1,6]{2,1,0:T(1,128)} %cols_hbm.1, s32[2]{0:T(128)} %bitcast.3, bf16[1536,128]{1,0:T(8,128)(2,1)} %bitcast.2), custom_call_target="tpu_custom_call" | custom-call | tf_op jit(solution)/shard_map/pack/pallas_call | solution.py:119
  1.5 2.6 %collective-permute-start = (bf16[1552,128]{1,0:T(8,128)(2,1)S(1)}, bf16[1552,128]{1,0:T(8,128)(2,1)S(1)}, u32[]{:S(2)}, u32[]{:S(2)}) collective-permute-start(bf16[1552,128]{1,0:T(8,128)(2,1)S(1)} %pack.1.refs_0_), channel_id=1, source_target_pairs={{0,1},{1,0},{2,3},{3,2},{4,5},{5,4},{6,7},{7,6},{8,9},{9,8},{10,11... | collective-permute-start | bytes 1191944 | tf_op jit(solution)/shard_map/ppermute | solution.py:61
  4.0 2.6 %collective-permute-start.2 = (bf16[1552,128]{1,0:T(8,128)(2,1)S(1)}, bf16[1552,128]{1,0:T(8,128)(2,1)S(1)}, u32[]{:S(2)}, u32[]{:S(2)}) collective-permute-start(bf16[1552,128]{1,0:T(8,128)(2,1)S(1)} %pack.1.refs_0_), channel_id=1, source_target_pairs={{0,8},{1,9},{2,10},{3,11},{4,0},{5,1},{6,2},{7,3},{8,12},{9,13},{1... | collective-permute-start | bytes 1191944 | tf_op jit(solution)/shard_map/ppermute | solution.py:61
  6.6 1.5 %collective-permute-start.3 = (bf16[1552,128]{1,0:T(8,128)(2,1)S(1)}, bf16[1552,128]{1,0:T(8,128)(2,1)S(1)}, u32[]{:S(2)}, u32[]{:S(2)}) collective-permute-start(bf16[1552,128]{1,0:T(8,128)(2,1)S(1)} %pack.1.refs_0_), channel_id=1, source_target_pairs={{0,2},{1,3},{2,0},{3,1},{4,6},{5,7},{6,4},{7,5},{8,10},{9,11},{10,... | collective-permute-start | bytes 1191944 | tf_op jit(solution)/shard_map/ppermute | solution.py:61
  8.2 0.0 collective-permute-done.1.refs_1_
  8.2 1.2 %panels.1 = (bf16[2,2048,256]{2,1,0:T(8,128)(2,1)S(1)}, f32[4224,256]{1,0:T(8,128)S(1)}) custom-call(bf16[2,1024,256]{2,1,0:T(8,128)(2,1)} %refs_0_.1, bf16[2,1024,256]{2,1,0:T(8,128)(2,1)S(1)} %collective-permute-done.1.refs_1_), custom_call_target="tpu_custom_call" | custom-call | tf_op jit(solution)/shard_map/panels/pallas_call | solution.py:160
  9.4 1.0 %fold.10.refs_4_ = f32[4224,256]{1,0:T(8,128)S(1)} custom-call(bf16[1552,128]{1,0:T(8,128)(2,1)S(1)} %pack.1.refs_0_, bf16[2,2048,256]{2,1,0:T(8,128)(2,1)S(1)} %get-tuple-element.39.refs_1_.refs_3_.refs_2_, f32[4224,256]{1,0:T(8,128)S(1)} %get-tuple-element.40.refs_2_), custom_call_target="tpu_custom_call", output_to_operand_aliasing={{}: (2, {})} | custom-call | flops 100663296 | bytes 393216 | tf_op jit(solution)/shard_map/fold/pallas_call | solution.py:244
  10.4 0.1 collective-permute-done.refs_0_
  10.5 4.8 %collective-permute-start.4 = (bf16[1552,128]{1,0:T(8,128)(2,1)S(1)}, bf16[1552,128]{1,0:T(8,128)(2,1)S(1)}, u32[]{:S(2)}, u32[]{:S(2)}) collective-permute-start(bf16[1552,128]{1,0:T(8,128)(2,1)S(1)} %collective-permute-done.refs_0_), channel_id=1, source_target_pairs={{0,4},{1,5},{2,6},{3,7},{4,12},{5,13},{6,14},{7,15},{8,0},{9,1},{1... | collective-permute-start | bytes 1191944 | tf_op jit(solution)/shard_map/ppermute | solution.py:61
  15.3 0.9 %collective-permute-done.2.refs_1_ = bf16[1552,128]{1,0:T(8,128)(2,1)S(1)} collective-permute-done((bf16[1552,128]{1,0:T(8,128)(2,1)S(1)}, bf16[1552,128]{1,0:T(8,128)(2,1)S(1)}, u32[]{:S(2)}, u32[]{:S(2)}) %collective-permute-start.2) | collective-permute-done | bytes 397344 | tf_op jit(solution)/shard_map/ppermute | solution.py:61
  16.2 1.3 %collective-permute-start.5 = (bf16[1552,128]{1,0:T(8,128)(2,1)S(1)}, bf16[1552,128]{1,0:T(8,128)(2,1)S(1)}, u32[]{:S(2)}, u32[]{:S(2)}) collective-permute-start(bf16[1552,128]{1,0:T(8,128)(2,1)S(1)} %collective-permute-done.2.refs_1_), channel_id=1, source_target_pairs={{0,2},{1,3},{2,0},{3,1},{4,6},{5,7},{6,4},{7,5},{8,10},{9,11},{10,... | collective-permute-start | bytes 1191944 | tf_op jit(solution)/shard_map/ppermute | solution.py:61
  17.5 1.7 %collective-permute-start.6 = (bf16[1552,128]{1,0:T(8,128)(2,1)S(1)}, bf16[1552,128]{1,0:T(8,128)(2,1)S(1)}, u32[]{:S(2)}, u32[]{:S(2)}) collective-permute-start(bf16[1552,128]{1,0:T(8,128)(2,1)S(1)} %collective-permute-done.2.refs_1_), channel_id=1, source_target_pairs={{0,1},{1,0},{2,3},{3,2},{4,5},{5,4},{6,7},{7,6},{8,9},{9,8},{10,11... | collective-permute-start | bytes 1191944 | tf_op jit(solution)/shard_map/ppermute | solution.py:61
  19.2 0.0 collective-permute-done.3.refs_2_
  19.2 2.5 %collective-permute-start.7 = (bf16[1552,128]{1,0:T(8,128)(2,1)S(1)}, bf16[1552,128]{1,0:T(8,128)(2,1)S(1)}, u32[]{:S(2)}, u32[]{:S(2)}) collective-permute-start(bf16[1552,128]{1,0:T(8,128)(2,1)S(1)} %collective-permute-done.3.refs_2_), channel_id=1, source_target_pairs={{0,4},{1,5},{2,6},{3,7},{4,12},{5,13},{6,14},{7,15},{8,0},{9,1},{1... | collective-permute-start | bytes 1191944 | tf_op jit(solution)/shard_map/ppermute | solution.py:61
  21.6 1.6 %fold.11.refs_2_ = f32[4224,256]{1,0:T(8,128)S(1)} custom-call(bf16[1552,128]{1,0:T(8,128)(2,1)S(1)} %collective-permute-done.refs_0_, bf16[1552,128]{1,0:T(8,128)(2,1)S(1)} %collective-permute-done.2.refs_1_, bf16[1552,128]{1,0:T(8,128)(2,1)S(1)} %collective-permute-done.3.refs_2_, ...), custom_call_target="tpu_custom_call", output_to_operand_aliasing={{}: (4, {})} | custom-call | flops 301989888 | bytes 1179648 | tf_op jit(solution)/shard_map/fold/pallas_call | solution.py:244
  23.2 0.1 collective-permute-start.10
  23.3 2.6 %collective-permute-done.4.refs_0_ = bf16[1552,128]{1,0:T(8,128)(2,1)S(1)} collective-permute-done((bf16[1552,128]{1,0:T(8,128)(2,1)S(1)}, bf16[1552,128]{1,0:T(8,128)(2,1)S(1)}, u32[]{:S(2)}, u32[]{:S(2)}) %collective-permute-start.4) | collective-permute-done | bytes 397344 | tf_op jit(solution)/shard_map/ppermute | solution.py:61
  25.9 1.0 %fold.12.refs_2_ = f32[4224,256]{1,0:T(8,128)S(1)} custom-call(bf16[1552,128]{1,0:T(8,128)(2,1)S(1)} %collective-permute-done.4.refs_0_, bf16[2,2048,256]{2,1,0:T(8,128)(2,1)S(1)} %get-tuple-element.39.refs_1_.refs_3_.refs_2_, f32[4224,256]{1,0:T(8,128)S(1)} %fold.11.refs_2_), custom_call_target="tpu_custom_call", output_to_operand_aliasing={{}: (2, {})} | custom-call | flops 100663296 | bytes 393216 | tf_op jit(solution)/shard_map/fold/pallas_call | solution.py:244
  26.9 1.8 %collective-permute-start.9 = (bf16[1552,128]{1,0:T(8,128)(2,1)S(1)}, bf16[1552,128]{1,0:T(8,128)(2,1)S(1)}, u32[]{:S(2)}, u32[]{:S(2)}) collective-permute-start(bf16[1552,128]{1,0:T(8,128)(2,1)S(1)} %collective-permute-done.4.refs_0_), channel_id=1, source_target_pairs={{0,4},{1,5},{2,6},{3,7},{4,12},{5,13},{6,14},{7,15},{8,0},{9,1},{1... | collective-permute-start | bytes 1191944 | tf_op jit(solution)/shard_map/ppermute | solution.py:61
  28.7 0.0 collective-permute-done.5.refs_0_
  28.7 1.5 %collective-permute-start.15 = (bf16[1552,128]{1,0:T(8,128)(2,1)S(1)}, bf16[1552,128]{1,0:T(8,128)(2,1)S(1)}, u32[]{:S(2)}, u32[]{:S(2)}) collective-permute-start(bf16[1552,128]{1,0:T(8,128)(2,1)S(1)} %collective-permute-done.4.refs_0_), channel_id=1, source_target_pairs={{0,1},{1,0},{2,3},{3,2},{4,5},{5,4},{6,7},{7,6},{8,9},{9,8},{10,11... | collective-permute-start | bytes 1191944 | tf_op jit(solution)/shard_map/ppermute | solution.py:61
  30.2 1.0 %fold.13.refs_2_ = f32[4224,256]{1,0:T(8,128)S(1)} custom-call(bf16[1552,128]{1,0:T(8,128)(2,1)S(1)} %collective-permute-done.5.refs_0_, bf16[2,2048,256]{2,1,0:T(8,128)(2,1)S(1)} %get-tuple-element.39.refs_1_.refs_3_.refs_2_, f32[4224,256]{1,0:T(8,128)S(1)} %fold.12.refs_2_), custom_call_target="tpu_custom_call", output_to_operand_aliasing={{}: (2, {})} | custom-call | flops 100663296 | bytes 393216 | tf_op jit(solution)/shard_map/fold/pallas_call | solution.py:244
  31.2 0.0 collective-permute-done.6.refs_0_
  31.2 2.2 %collective-permute-start.14 = (bf16[1552,128]{1,0:T(8,128)(2,1)S(1)}, bf16[1552,128]{1,0:T(8,128)(2,1)S(1)}, u32[]{:S(2)}, u32[]{:S(2)}) collective-permute-start(bf16[1552,128]{1,0:T(8,128)(2,1)S(1)} %collective-permute-done.4.refs_0_), channel_id=1, source_target_pairs={{0,2},{1,3},{2,0},{3,1},{4,6},{5,7},{6,4},{7,5},{8,10},{9,11},{10,... | collective-permute-start | bytes 1191944 | tf_op jit(solution)/shard_map/ppermute | solution.py:61
  33.4 1.0 %fold.14.refs_3_ = f32[4224,256]{1,0:T(8,128)S(1)} custom-call(bf16[1552,128]{1,0:T(8,128)(2,1)S(1)} %collective-permute-done.6.refs_0_, bf16[2,2048,256]{2,1,0:T(8,128)(2,1)S(1)} %get-tuple-element.39.refs_1_.refs_3_.refs_2_, f32[4224,256]{1,0:T(8,128)S(1)} %fold.13.refs_2_), custom_call_target="tpu_custom_call", output_to_operand_aliasing={{}: (2, {})} | custom-call | flops 100663296 | bytes 393216 | tf_op jit(solution)/shard_map/fold/pallas_call | solution.py:244
  34.4 0.0 collective-permute-done.7.refs_0_
  34.4 1.2 %collective-permute-start.13 = (bf16[1552,128]{1,0:T(8,128)(2,1)S(1)}, bf16[1552,128]{1,0:T(8,128)(2,1)S(1)}, u32[]{:S(2)}, u32[]{:S(2)}) collective-permute-start(bf16[1552,128]{1,0:T(8,128)(2,1)S(1)} %collective-permute-done.5.refs_0_), channel_id=1, source_target_pairs={{0,1},{1,0},{2,3},{3,2},{4,5},{5,4},{6,7},{7,6},{8,9},{9,8},{10,11... | collective-permute-start | bytes 1191944 | tf_op jit(solution)/shard_map/ppermute | solution.py:61
  35.7 0.0 collective-permute-done.10.refs_1_
  35.7 2.7 %collective-permute-start.8 = (bf16[1552,128]{1,0:T(8,128)(2,1)S(1)}, bf16[1552,128]{1,0:T(8,128)(2,1)S(1)}, u32[]{:S(2)}, u32[]{:S(2)}) collective-permute-start(bf16[1552,128]{1,0:T(8,128)(2,1)S(1)} %collective-permute-done.7.refs_0_), channel_id=1, source_target_pairs={{0,4},{1,5},{2,6},{3,7},{4,12},{5,13},{6,14},{7,15},{8,0},{9,1},{1... | collective-permute-start | bytes 1191944 | tf_op jit(solution)/shard_map/ppermute | solution.py:61
  38.4 1.3 %fold.15.refs_2_ = f32[4224,256]{1,0:T(8,128)S(1)} custom-call(bf16[1552,128]{1,0:T(8,128)(2,1)S(1)} %collective-permute-done.7.refs_0_, bf16[1552,128]{1,0:T(8,128)(2,1)S(1)} %collective-permute-done.10.refs_1_, bf16[2,2048,256]{2,1,0:T(8,128)(2,1)S(1)} %get-tuple-element.39.refs_1_.refs_3_.refs_2_, ...), custom_call_target="tpu_custom_call", output_to_operand_aliasing={{}: (3, {})} | custom-call | flops 201326592 | bytes 786432 | tf_op jit(solution)/shard_map/fold/pallas_call | solution.py:244
  39.7 3.3 %collective-permute-done.9.refs_0_ = bf16[1552,128]{1,0:T(8,128)(2,1)S(1)} collective-permute-done((bf16[1552,128]{1,0:T(8,128)(2,1)S(1)}, bf16[1552,128]{1,0:T(8,128)(2,1)S(1)}, u32[]{:S(2)}, u32[]{:S(2)}) %collective-permute-start.9) | collective-permute-done | bytes 397344 | tf_op jit(solution)/shard_map/ppermute | solution.py:61
  43.0 1.2 %collective-permute-start.12 = (bf16[1552,128]{1,0:T(8,128)(2,1)S(1)}, bf16[1552,128]{1,0:T(8,128)(2,1)S(1)}, u32[]{:S(2)}, u32[]{:S(2)}) collective-permute-start(bf16[1552,128]{1,0:T(8,128)(2,1)S(1)} %collective-permute-done.9.refs_0_), channel_id=1, source_target_pairs={{0,1},{1,0},{2,3},{3,2},{4,5},{5,4},{6,7},{7,6},{8,9},{9,8},{10,11... | collective-permute-start | bytes 1191944 | tf_op jit(solution)/shard_map/ppermute | solution.py:61
  44.2 0.0 collective-permute-done.15.refs_0_
  44.2 2.1 %collective-permute-start.11 = (bf16[1552,128]{1,0:T(8,128)(2,1)S(1)}, bf16[1552,128]{1,0:T(8,128)(2,1)S(1)}, u32[]{:S(2)}, u32[]{:S(2)}) collective-permute-start(bf16[1552,128]{1,0:T(8,128)(2,1)S(1)} %collective-permute-done.9.refs_0_), channel_id=1, source_target_pairs={{0,2},{1,3},{2,0},{3,1},{4,6},{5,7},{6,4},{7,5},{8,10},{9,11},{10,... | collective-permute-start | bytes 1191944 | tf_op jit(solution)/shard_map/ppermute | solution.py:61
  46.3 1.0 %fold.16.refs_2_ = f32[4224,256]{1,0:T(8,128)S(1)} custom-call(bf16[1552,128]{1,0:T(8,128)(2,1)S(1)} %collective-permute-done.9.refs_0_, bf16[2,2048,256]{2,1,0:T(8,128)(2,1)S(1)} %get-tuple-element.39.refs_1_.refs_3_.refs_2_, f32[4224,256]{1,0:T(8,128)S(1)} %fold.15.refs_2_), custom_call_target="tpu_custom_call", output_to_operand_aliasing={{}: (2, {})} | custom-call | flops 100663296 | bytes 393216 | tf_op jit(solution)/shard_map/fold/pallas_call | solution.py:244
  47.3 1.0 %fold.17.refs_2_ = f32[4224,256]{1,0:T(8,128)S(1)} custom-call(bf16[1552,128]{1,0:T(8,128)(2,1)S(1)} %collective-permute-done.15.refs_0_, bf16[2,2048,256]{2,1,0:T(8,128)(2,1)S(1)} %get-tuple-element.39.refs_1_.refs_3_.refs_2_, f32[4224,256]{1,0:T(8,128)S(1)} %fold.16.refs_2_), custom_call_target="tpu_custom_call", output_to_operand_aliasing={{}: (2, {})} | custom-call | flops 100663296 | bytes 393216 | tf_op jit(solution)/shard_map/fold/pallas_call | solution.py:244
  48.3 0.0 collective-permute-done.14.refs_0_
  48.3 1.0 %fold.18.refs_2_ = f32[4224,256]{1,0:T(8,128)S(1)} custom-call(bf16[1552,128]{1,0:T(8,128)(2,1)S(1)} %collective-permute-done.14.refs_0_, bf16[2,2048,256]{2,1,0:T(8,128)(2,1)S(1)} %get-tuple-element.39.refs_1_.refs_3_.refs_2_, f32[4224,256]{1,0:T(8,128)S(1)} %fold.17.refs_2_), custom_call_target="tpu_custom_call", output_to_operand_aliasing={{}: (2, {})} | custom-call | flops 100663296 | bytes 393216 | tf_op jit(solution)/shard_map/fold/pallas_call | solution.py:244
  49.3 0.0 collective-permute-done.13.refs_0_
  49.3 1.0 %fold.19.refs_4_ = f32[4224,256]{1,0:T(8,128)S(1)} custom-call(bf16[1552,128]{1,0:T(8,128)(2,1)S(1)} %collective-permute-done.13.refs_0_, bf16[2,2048,256]{2,1,0:T(8,128)(2,1)S(1)} %get-tuple-element.39.refs_1_.refs_3_.refs_2_, f32[4224,256]{1,0:T(8,128)S(1)} %fold.18.refs_2_), custom_call_target="tpu_custom_call", output_to_operand_aliasing={{}: (2, {})} | custom-call | flops 100663296 | bytes 393216 | tf_op jit(solution)/shard_map/fold/pallas_call | solution.py:244
  50.3 1.1 %collective-permute-done.8.refs_0_ = bf16[1552,128]{1,0:T(8,128)(2,1)S(1)} collective-permute-done((bf16[1552,128]{1,0:T(8,128)(2,1)S(1)}, bf16[1552,128]{1,0:T(8,128)(2,1)S(1)}, u32[]{:S(2)}, u32[]{:S(2)}) %collective-permute-start.8) | collective-permute-done | bytes 397344 | tf_op jit(solution)/shard_map/ppermute | solution.py:61
  51.4 2.6 %collective-permute-done.12.refs_2_ = bf16[1552,128]{1,0:T(8,128)(2,1)S(1)} collective-permute-done((bf16[1552,128]{1,0:T(8,128)(2,1)S(1)}, bf16[1552,128]{1,0:T(8,128)(2,1)S(1)}, u32[]{:S(2)}, u32[]{:S(2)}) %collective-permute-start.12) | collective-permute-done | bytes 397344 | tf_op jit(solution)/shard_map/ppermute | solution.py:61
  54.0 0.0 collective-permute-done.11.refs_1_
  54.0 2.8 %last.1 = (f32[4224,256]{1,0:T(8,128)S(1)}, f32[4096,256]{1,0:T(8,128)}) custom-call(bf16[1552,128]{1,0:T(8,128)(2,1)S(1)} %collective-permute-done.8.refs_0_, bf16[1552,128]{1,0:T(8,128)(2,1)S(1)} %collective-permute-done.11.refs_1_, bf16[1552,128]{1,0:T(8,128)(2,1)S(1)} %collective-permute-done.12.refs_2_, ...), custom_call_target="tpu_custom_call", output_to_operand_aliasing={{0}: (4, {})} | custom-call | flops 301989888 | bytes 1179648 | tf_op jit(solution)/shard_map/last/pallas_call | solution.py:244
Async XLA Ops:
  0.0 8.2 %collective-permute-start.1 = (bf16[2,1024,256]{2,1,0:T(8,128)(2,1)}, bf16[2,1024,256]{2,1,0:T(8,128)(2,1)S(1)}, u32[]{:S(2)}, u32[]{:S(2)}) collective-permute-start(bf16[2,1024,256]{2,1,0:T(8,128)(2,1)} %refs_0_.1), channel_id=1, source_target_pairs={{0,16},{16,0},{1,17},{17,1},{2,18},{18,2},{3,19},{19,3},{4,20},{20... | collective-permute-start | bytes 3145736 | tf_op jit(solution)/shard_map/ppermute | solution.py:266
  1.5 9.0 %collective-permute-start = (bf16[1552,128]{1,0:T(8,128)(2,1)S(1)}, bf16[1552,128]{1,0:T(8,128)(2,1)S(1)}, u32[]{:S(2)}, u32[]{:S(2)}) collective-permute-start(bf16[1552,128]{1,0:T(8,128)(2,1)S(1)} %pack.1.refs_0_), channel_id=1, source_target_pairs={{0,1},{1,0},{2,3},{3,2},{4,5},{5,4},{6,7},{7,6},{8,9},{9,8},{10,11... | collective-permute-start | bytes 1191944 | tf_op jit(solution)/shard_map/ppermute | solution.py:61
  4.0 12.1 %collective-permute-start.2 = (bf16[1552,128]{1,0:T(8,128)(2,1)S(1)}, bf16[1552,128]{1,0:T(8,128)(2,1)S(1)}, u32[]{:S(2)}, u32[]{:S(2)}) collective-permute-start(bf16[1552,128]{1,0:T(8,128)(2,1)S(1)} %pack.1.refs_0_), channel_id=1, source_target_pairs={{0,8},{1,9},{2,10},{3,11},{4,0},{5,1},{6,2},{7,3},{8,12},{9,13},{1... | collective-permute-start | bytes 1191944 | tf_op jit(solution)/shard_map/ppermute | solution.py:61
  6.6 12.5 %collective-permute-start.3 = (bf16[1552,128]{1,0:T(8,128)(2,1)S(1)}, bf16[1552,128]{1,0:T(8,128)(2,1)S(1)}, u32[]{:S(2)}, u32[]{:S(2)}) collective-permute-start(bf16[1552,128]{1,0:T(8,128)(2,1)S(1)} %pack.1.refs_0_), channel_id=1, source_target_pairs={{0,2},{1,3},{2,0},{3,1},{4,6},{5,7},{6,4},{7,5},{8,10},{9,11},{10,... | collective-permute-start | bytes 1191944 | tf_op jit(solution)/shard_map/ppermute | solution.py:61
  10.5 15.4 %collective-permute-start.4 = (bf16[1552,128]{1,0:T(8,128)(2,1)S(1)}, bf16[1552,128]{1,0:T(8,128)(2,1)S(1)}, u32[]{:S(2)}, u32[]{:S(2)}) collective-permute-start(bf16[1552,128]{1,0:T(8,128)(2,1)S(1)} %collective-permute-done.refs_0_), channel_id=1, source_target_pairs={{0,4},{1,5},{2,6},{3,7},{4,12},{5,13},{6,14},{7,15},{8,0},{9,1},{1... | collective-permute-start | bytes 1191944 | tf_op jit(solution)/shard_map/ppermute | solution.py:61
  16.2 12.5 %collective-permute-start.5 = (bf16[1552,128]{1,0:T(8,128)(2,1)S(1)}, bf16[1552,128]{1,0:T(8,128)(2,1)S(1)}, u32[]{:S(2)}, u32[]{:S(2)}) collective-permute-start(bf16[1552,128]{1,0:T(8,128)(2,1)S(1)} %collective-permute-done.2.refs_1_), channel_id=1, source_target_pairs={{0,2},{1,3},{2,0},{3,1},{4,6},{5,7},{6,4},{7,5},{8,10},{9,11},{10,... | collective-permute-start | bytes 1191944 | tf_op jit(solution)/shard_map/ppermute | solution.py:61
  17.5 13.7 %collective-permute-start.6 = (bf16[1552,128]{1,0:T(8,128)(2,1)S(1)}, bf16[1552,128]{1,0:T(8,128)(2,1)S(1)}, u32[]{:S(2)}, u32[]{:S(2)}) collective-permute-start(bf16[1552,128]{1,0:T(8,128)(2,1)S(1)} %collective-permute-done.2.refs_1_), channel_id=1, source_target_pairs={{0,1},{1,0},{2,3},{3,2},{4,5},{5,4},{6,7},{7,6},{8,9},{9,8},{10,11... | collective-permute-start | bytes 1191944 | tf_op jit(solution)/shard_map/ppermute | solution.py:61
  19.2 15.3 %collective-permute-start.7 = (bf16[1552,128]{1,0:T(8,128)(2,1)S(1)}, bf16[1552,128]{1,0:T(8,128)(2,1)S(1)}, u32[]{:S(2)}, u32[]{:S(2)}) collective-permute-start(bf16[1552,128]{1,0:T(8,128)(2,1)S(1)} %collective-permute-done.3.refs_2_), channel_id=1, source_target_pairs={{0,4},{1,5},{2,6},{3,7},{4,12},{5,13},{6,14},{7,15},{8,0},{9,1},{1... | collective-permute-start | bytes 1191944 | tf_op jit(solution)/shard_map/ppermute | solution.py:61
  23.2 12.5 %collective-permute-start.10 = (bf16[1552,128]{1,0:T(8,128)(2,1)S(1)}, bf16[1552,128]{1,0:T(8,128)(2,1)S(1)}, u32[]{:S(2)}, u32[]{:S(2)}) collective-permute-start(bf16[1552,128]{1,0:T(8,128)(2,1)S(1)} %collective-permute-done.refs_0_), channel_id=1, source_target_pairs={{0,2},{1,3},{2,0},{3,1},{4,6},{5,7},{6,4},{7,5},{8,10},{9,11},{10,... | collective-permute-start | bytes 1191944 | tf_op jit(solution)/shard_map/ppermute | solution.py:61
  26.9 16.0 %collective-permute-start.9 = (bf16[1552,128]{1,0:T(8,128)(2,1)S(1)}, bf16[1552,128]{1,0:T(8,128)(2,1)S(1)}, u32[]{:S(2)}, u32[]{:S(2)}) collective-permute-start(bf16[1552,128]{1,0:T(8,128)(2,1)S(1)} %collective-permute-done.4.refs_0_), channel_id=1, source_target_pairs={{0,4},{1,5},{2,6},{3,7},{4,12},{5,13},{6,14},{7,15},{8,0},{9,1},{1... | collective-permute-start | bytes 1191944 | tf_op jit(solution)/shard_map/ppermute | solution.py:61
  28.7 15.5 %collective-permute-start.15 = (bf16[1552,128]{1,0:T(8,128)(2,1)S(1)}, bf16[1552,128]{1,0:T(8,128)(2,1)S(1)}, u32[]{:S(2)}, u32[]{:S(2)}) collective-permute-start(bf16[1552,128]{1,0:T(8,128)(2,1)S(1)} %collective-permute-done.4.refs_0_), channel_id=1, source_target_pairs={{0,1},{1,0},{2,3},{3,2},{4,5},{5,4},{6,7},{7,6},{8,9},{9,8},{10,11... | collective-permute-start | bytes 1191944 | tf_op jit(solution)/shard_map/ppermute | solution.py:61
  31.2 17.1 %collective-permute-start.14 = (bf16[1552,128]{1,0:T(8,128)(2,1)S(1)}, bf16[1552,128]{1,0:T(8,128)(2,1)S(1)}, u32[]{:S(2)}, u32[]{:S(2)}) collective-permute-start(bf16[1552,128]{1,0:T(8,128)(2,1)S(1)} %collective-permute-done.4.refs_0_), channel_id=1, source_target_pairs={{0,2},{1,3},{2,0},{3,1},{4,6},{5,7},{6,4},{7,5},{8,10},{9,11},{10,... | collective-permute-start | bytes 1191944 | tf_op jit(solution)/shard_map/ppermute | solution.py:61
  34.4 14.9 %collective-permute-start.13 = (bf16[1552,128]{1,0:T(8,128)(2,1)S(1)}, bf16[1552,128]{1,0:T(8,128)(2,1)S(1)}, u32[]{:S(2)}, u32[]{:S(2)}) collective-permute-start(bf16[1552,128]{1,0:T(8,128)(2,1)S(1)} %collective-permute-done.5.refs_0_), channel_id=1, source_target_pairs={{0,1},{1,0},{2,3},{3,2},{4,5},{5,4},{6,7},{7,6},{8,9},{9,8},{10,11... | collective-permute-start | bytes 1191944 | tf_op jit(solution)/shard_map/ppermute | solution.py:61
  35.7 15.7 %collective-permute-start.8 = (bf16[1552,128]{1,0:T(8,128)(2,1)S(1)}, bf16[1552,128]{1,0:T(8,128)(2,1)S(1)}, u32[]{:S(2)}, u32[]{:S(2)}) collective-permute-start(bf16[1552,128]{1,0:T(8,128)(2,1)S(1)} %collective-permute-done.7.refs_0_), channel_id=1, source_target_pairs={{0,4},{1,5},{2,6},{3,7},{4,12},{5,13},{6,14},{7,15},{8,0},{9,1},{1... | collective-permute-start | bytes 1191944 | tf_op jit(solution)/shard_map/ppermute | solution.py:61
  43.0 11.0 %collective-permute-start.12 = (bf16[1552,128]{1,0:T(8,128)(2,1)S(1)}, bf16[1552,128]{1,0:T(8,128)(2,1)S(1)}, u32[]{:S(2)}, u32[]{:S(2)}) collective-permute-start(bf16[1552,128]{1,0:T(8,128)(2,1)S(1)} %collective-permute-done.9.refs_0_), channel_id=1, source_target_pairs={{0,1},{1,0},{2,3},{3,2},{4,5},{5,4},{6,7},{7,6},{8,9},{9,8},{10,11... | collective-permute-start | bytes 1191944 | tf_op jit(solution)/shard_map/ppermute | solution.py:61
  44.2 9.8 %collective-permute-start.11 = (bf16[1552,128]{1,0:T(8,128)(2,1)S(1)}, bf16[1552,128]{1,0:T(8,128)(2,1)S(1)}, u32[]{:S(2)}, u32[]{:S(2)}) collective-permute-start(bf16[1552,128]{1,0:T(8,128)(2,1)S(1)} %collective-permute-done.9.refs_0_), channel_id=1, source_target_pairs={{0,2},{1,3},{2,0},{3,1},{4,6},{5,7},{6,4},{7,5},{8,10},{9,11},{10,... | collective-permute-start | bytes 1191944 | tf_op jit(solution)/shard_map/ppermute | solution.py:61

commit v6 on v4

--- a/solution.py
+++ b/solution.py
@@ -13,28 +13,29 @@
 
 PARTS = ((0, 12),)
 PLAN = [
+    (0, 2, 1),
+    (0, 12, 3),
     (0, 1, 0),
-    (0, 12, 3),
-    (0, 2, 1),
     [(0, 0)],
+    (0, 6, 2),
+    (0, 13, 0),
+    (0, 14, 1),
+    [(0, 2), (0, 12)],
     (0, 5, 2),
-    (0, 14, 1),
-    (0, 13, 0),
-    (0, 6, 2),
-    [(0, 1), (0, 12), (0, 2)],
-    (0, 3, 1),
-    (0, 4, 0),
+    [(0, 1)],
+    (0, 3, 0),
+    (0, 4, 1),
+    (0, 10, 2),
+    [(0, 6), (0, 13)],
+    (0, 7, 0),
+    [(0, 14)],
+    (0, 15, 1),
     [(0, 5)],
     (0, 9, 2),
-    [(0, 14)],
-    (0, 7, 1),
-    [(0, 13)],
-    (0, 15, 0),
-    (0, 10, 2),
-    [(0, 6), (0, 3)],
-    (0, 11, 1),
-    (0, 8, 0),
-    [(0, 9), (0, 4)],
+    [(0, 3)],
+    (0, 11, 0),
+    (0, 8, 1),
+    [(0, 10), (0, 4)],
     [(0, 7)],
     [(0, 15)],
 ]

time: 57 us -> 57 us (level)
  Pallas kernels: 15.2 us -> 15.9 us
  waiting for transfers between devices: 11.3 us -> 10.7 us
    pallas_call x10 -> x11, Pallas kernels: 12.9 us -> 13.6 us  [fold(): pl.pallas_call(functools.partial(last_kernel if last else fold_kernel, sl...]
  transfers between devices with their start and end apart: 16 -> 16, of which waited for: 6 -> 7; matrix products, arithmetic and copies ran while one was open for 0% -> 0% of each run, Pallas kernels for 22% -> 23%
where the time goes in v6:
time: 57 us; the launch traced here: 56.8 us
  starting transfers between devices  30 us (53%)
  Pallas kernels  15.9 us (28%)
  waiting for transfers between devices  10.7 us (19%)
    ppermute x15, starting transfers between devices, hop(): return lax.ppermute(unit, ('row', 'col'), pairs)  29.6 us
    pallas_call x11, Pallas kernels, fold(): pl.pallas_call(functools.partial(last_kernel if last else fold_kernel, sl...  13.6 us
    ppermute x15, waiting for transfers between devices, hop(): return lax.ppermute(unit, ('row', 'col'), pairs)  10.7 us
    pallas_call x1, Pallas kernels, whole_panels(): pl.pallas_call(functools.partial(panel_kernel, n_row=n_row), out_shape=(p...  1.24 us
  transfers between devices with their start and end apart: 16, of which 7 were waited for; matrix products, arithmetic and copies ran while one was open for 0% of the time, Pallas kernels for 23%

profile of v6, /device:TPU:0, one launch (start us, length us, event | category | flops | bytes accessed | tf_op | source)
XLA Modules:
  0.0 56.8 jit_solution(7898348232897939666)
XLA Ops:
  0.0 0.5 collective-permute-start.1
  0.5 1.0 %pack.1.refs_0_ = bf16[1552,128]{1,0:T(8,128)(2,1)S(1)} custom-call(s32[2,1,6]{2,1,0:T(1,128)} %rows_hbm.1, s32[2,1,6]{2,1,0:T(1,128)} %cols_hbm.1, s32[2]{0:T(128)} %bitcast.3, bf16[1536,128]{1,0:T(8,128)(2,1)} %bitcast.2), custom_call_target="tpu_custom_call" | custom-call | tf_op jit(solution)/shard_map/pack/pallas_call | solution.py:119
  1.5 2.6 %collective-permute-start = (bf16[1552,128]{1,0:T(8,128)(2,1)S(1)}, bf16[1552,128]{1,0:T(8,128)(2,1)S(1)}, u32[]{:S(2)}, u32[]{:S(2)}) collective-permute-start(bf16[1552,128]{1,0:T(8,128)(2,1)S(1)} %pack.1.refs_0_), channel_id=1, source_target_pairs={{0,2},{1,3},{2,0},{3,1},{4,6},{5,7},{6,4},{7,5},{8,10},{9,11},{10,... | collective-permute-start | bytes 1191944 | tf_op jit(solution)/shard_map/ppermute | solution.py:61
  4.1 2.6 %collective-permute-start.2 = (bf16[1552,128]{1,0:T(8,128)(2,1)S(1)}, bf16[1552,128]{1,0:T(8,128)(2,1)S(1)}, u32[]{:S(2)}, u32[]{:S(2)}) collective-permute-start(bf16[1552,128]{1,0:T(8,128)(2,1)S(1)} %pack.1.refs_0_), channel_id=1, source_target_pairs={{0,8},{1,9},{2,10},{3,11},{4,0},{5,1},{6,2},{7,3},{8,12},{9,13},{1... | collective-permute-start | bytes 1191944 | tf_op jit(solution)/shard_map/ppermute | solution.py:61
  6.7 1.5 %collective-permute-start.3 = (bf16[1552,128]{1,0:T(8,128)(2,1)S(1)}, bf16[1552,128]{1,0:T(8,128)(2,1)S(1)}, u32[]{:S(2)}, u32[]{:S(2)}) collective-permute-start(bf16[1552,128]{1,0:T(8,128)(2,1)S(1)} %pack.1.refs_0_), channel_id=1, source_target_pairs={{0,1},{1,0},{2,3},{3,2},{4,5},{5,4},{6,7},{7,6},{8,9},{9,8},{10,11... | collective-permute-start | bytes 1191944 | tf_op jit(solution)/shard_map/ppermute | solution.py:61
  8.2 0.0 collective-permute-done.1.refs_1_
  8.2 1.2 %panels.1 = (bf16[2,2048,256]{2,1,0:T(8,128)(2,1)S(1)}, f32[4224,256]{1,0:T(8,128)S(1)}) custom-call(bf16[2,1024,256]{2,1,0:T(8,128)(2,1)} %refs_0_.1, bf16[2,1024,256]{2,1,0:T(8,128)(2,1)S(1)} %collective-permute-done.1.refs_1_), custom_call_target="tpu_custom_call" | custom-call | tf_op jit(solution)/shard_map/panels/pallas_call | solution.py:160
  9.4 1.0 %fold.10.refs_3_ = f32[4224,256]{1,0:T(8,128)S(1)} custom-call(bf16[1552,128]{1,0:T(8,128)(2,1)S(1)} %pack.1.refs_0_, bf16[2,2048,256]{2,1,0:T(8,128)(2,1)S(1)} %get-tuple-element.40.refs_1_.refs_2_.refs_3_, f32[4224,256]{1,0:T(8,128)S(1)} %get-tuple-element.41.refs_2_), custom_call_target="tpu_custom_call", output_to_operand_aliasing={{}: (2, {})} | custom-call | flops 100663296 | bytes 393216 | tf_op jit(solution)/shard_map/fold/pallas_call | solution.py:244
  10.4 0.1 collective-permute-done.refs_0_
  10.5 4.8 %collective-permute-start.4 = (bf16[1552,128]{1,0:T(8,128)(2,1)S(1)}, bf16[1552,128]{1,0:T(8,128)(2,1)S(1)}, u32[]{:S(2)}, u32[]{:S(2)}) collective-permute-start(bf16[1552,128]{1,0:T(8,128)(2,1)S(1)} %collective-permute-done.refs_0_), channel_id=1, source_target_pairs={{0,4},{1,5},{2,6},{3,7},{4,12},{5,13},{6,14},{7,15},{8,0},{9,1},{1... | collective-permute-start | bytes 1191944 | tf_op jit(solution)/shard_map/ppermute | solution.py:61
  15.3 0.9 %collective-permute-done.2.refs_1_ = bf16[1552,128]{1,0:T(8,128)(2,1)S(1)} collective-permute-done((bf16[1552,128]{1,0:T(8,128)(2,1)S(1)}, bf16[1552,128]{1,0:T(8,128)(2,1)S(1)}, u32[]{:S(2)}, u32[]{:S(2)}) %collective-permute-start.2) | collective-permute-done | bytes 397344 | tf_op jit(solution)/shard_map/ppermute | solution.py:61
  16.2 1.3 %collective-permute-start.5 = (bf16[1552,128]{1,0:T(8,128)(2,1)S(1)}, bf16[1552,128]{1,0:T(8,128)(2,1)S(1)}, u32[]{:S(2)}, u32[]{:S(2)}) collective-permute-start(bf16[1552,128]{1,0:T(8,128)(2,1)S(1)} %collective-permute-done.2.refs_1_), channel_id=1, source_target_pairs={{0,1},{1,0},{2,3},{3,2},{4,5},{5,4},{6,7},{7,6},{8,9},{9,8},{10,11... | collective-permute-start | bytes 1191944 | tf_op jit(solution)/shard_map/ppermute | solution.py:61
  17.5 1.7 %collective-permute-start.6 = (bf16[1552,128]{1,0:T(8,128)(2,1)S(1)}, bf16[1552,128]{1,0:T(8,128)(2,1)S(1)}, u32[]{:S(2)}, u32[]{:S(2)}) collective-permute-start(bf16[1552,128]{1,0:T(8,128)(2,1)S(1)} %collective-permute-done.2.refs_1_), channel_id=1, source_target_pairs={{0,2},{1,3},{2,0},{3,1},{4,6},{5,7},{6,4},{7,5},{8,10},{9,11},{10,... | collective-permute-start | bytes 1191944 | tf_op jit(solution)/shard_map/ppermute | solution.py:61
  19.2 1.3 %fold.11.refs_2_ = f32[4224,256]{1,0:T(8,128)S(1)} custom-call(bf16[1552,128]{1,0:T(8,128)(2,1)S(1)} %collective-permute-done.refs_0_, bf16[1552,128]{1,0:T(8,128)(2,1)S(1)} %collective-permute-done.2.refs_1_, bf16[2,2048,256]{2,1,0:T(8,128)(2,1)S(1)} %get-tuple-element.40.refs_1_.refs_2_.refs_3_, ...), custom_call_target="tpu_custom_call", output_to_operand_aliasing={{}: (3, {})} | custom-call | flops 201326592 | bytes 786432 | tf_op jit(solution)/shard_map/fold/pallas_call | solution.py:244
  20.5 0.0 collective-permute-done.3.refs_0_
  20.5 2.5 %collective-permute-start.7 = (bf16[1552,128]{1,0:T(8,128)(2,1)S(1)}, bf16[1552,128]{1,0:T(8,128)(2,1)S(1)}, u32[]{:S(2)}, u32[]{:S(2)}) collective-permute-start(bf16[1552,128]{1,0:T(8,128)(2,1)S(1)} %collective-permute-done.3.refs_0_), channel_id=1, source_target_pairs={{0,4},{1,5},{2,6},{3,7},{4,12},{5,13},{6,14},{7,15},{8,0},{9,1},{1... | collective-permute-start | bytes 1191944 | tf_op jit(solution)/shard_map/ppermute | solution.py:61
  23.0 1.0 %fold.12.refs_3_ = f32[4224,256]{1,0:T(8,128)S(1)} custom-call(bf16[1552,128]{1,0:T(8,128)(2,1)S(1)} %collective-permute-done.3.refs_0_, bf16[2,2048,256]{2,1,0:T(8,128)(2,1)S(1)} %get-tuple-element.40.refs_1_.refs_2_.refs_3_, f32[4224,256]{1,0:T(8,128)S(1)} %fold.11.refs_2_), custom_call_target="tpu_custom_call", output_to_operand_aliasing={{}: (2, {})} | custom-call | flops 100663296 | bytes 393216 | tf_op jit(solution)/shard_map/fold/pallas_call | solution.py:244
  24.0 0.1 collective-permute-start.10
  24.1 1.8 %collective-permute-done.4.refs_0_ = bf16[1552,128]{1,0:T(8,128)(2,1)S(1)} collective-permute-done((bf16[1552,128]{1,0:T(8,128)(2,1)S(1)}, bf16[1552,128]{1,0:T(8,128)(2,1)S(1)}, u32[]{:S(2)}, u32[]{:S(2)}) %collective-permute-start.4) | collective-permute-done | bytes 397344 | tf_op jit(solution)/shard_map/ppermute | solution.py:61
  25.9 1.8 %collective-permute-start.9 = (bf16[1552,128]{1,0:T(8,128)(2,1)S(1)}, bf16[1552,128]{1,0:T(8,128)(2,1)S(1)}, u32[]{:S(2)}, u32[]{:S(2)}) collective-permute-start(bf16[1552,128]{1,0:T(8,128)(2,1)S(1)} %collective-permute-done.4.refs_0_), channel_id=1, source_target_pairs={{0,4},{1,5},{2,6},{3,7},{4,12},{5,13},{6,14},{7,15},{8,0},{9,1},{1... | collective-permute-start | bytes 1191944 | tf_op jit(solution)/shard_map/ppermute | solution.py:61
  27.7 0.0 collective-permute-done.5.refs_1_
  27.7 1.5 %collective-permute-start.15 = (bf16[1552,128]{1,0:T(8,128)(2,1)S(1)}, bf16[1552,128]{1,0:T(8,128)(2,1)S(1)}, u32[]{:S(2)}, u32[]{:S(2)}) collective-permute-start(bf16[1552,128]{1,0:T(8,128)(2,1)S(1)} %collective-permute-done.4.refs_0_), channel_id=1, source_target_pairs={{0,2},{1,3},{2,0},{3,1},{4,6},{5,7},{6,4},{7,5},{8,10},{9,11},{10,... | collective-permute-start | bytes 1191944 | tf_op jit(solution)/shard_map/ppermute | solution.py:61
  29.2 1.3 %fold.13.refs_2_ = f32[4224,256]{1,0:T(8,128)S(1)} custom-call(bf16[1552,128]{1,0:T(8,128)(2,1)S(1)} %collective-permute-done.4.refs_0_, bf16[1552,128]{1,0:T(8,128)(2,1)S(1)} %collective-permute-done.5.refs_1_, bf16[2,2048,256]{2,1,0:T(8,128)(2,1)S(1)} %get-tuple-element.40.refs_1_.refs_2_.refs_3_, ...), custom_call_target="tpu_custom_call", output_to_operand_aliasing={{}: (3, {})} | custom-call | flops 201326592 | bytes 786432 | tf_op jit(solution)/shard_map/fold/pallas_call | solution.py:244
  30.5 0.0 collective-permute-done.6.refs_0_
  30.5 2.2 %collective-permute-start.14 = (bf16[1552,128]{1,0:T(8,128)(2,1)S(1)}, bf16[1552,128]{1,0:T(8,128)(2,1)S(1)}, u32[]{:S(2)}, u32[]{:S(2)}) collective-permute-start(bf16[1552,128]{1,0:T(8,128)(2,1)S(1)} %collective-permute-done.4.refs_0_), channel_id=1, source_target_pairs={{0,1},{1,0},{2,3},{3,2},{4,5},{5,4},{6,7},{7,6},{8,9},{9,8},{10,11... | collective-permute-start | bytes 1191944 | tf_op jit(solution)/shard_map/ppermute | solution.py:61
  32.7 1.0 %fold.14.refs_2_ = f32[4224,256]{1,0:T(8,128)S(1)} custom-call(bf16[1552,128]{1,0:T(8,128)(2,1)S(1)} %collective-permute-done.6.refs_0_, bf16[2,2048,256]{2,1,0:T(8,128)(2,1)S(1)} %get-tuple-element.40.refs_1_.refs_2_.refs_3_, f32[4224,256]{1,0:T(8,128)S(1)} %fold.13.refs_2_), custom_call_target="tpu_custom_call", output_to_operand_aliasing={{}: (2, {})} | custom-call | flops 100663296 | bytes 393216 | tf_op jit(solution)/shard_map/fold/pallas_call | solution.py:244
  33.7 0.7 %collective-permute-done.7.refs_0_ = bf16[1552,128]{1,0:T(8,128)(2,1)S(1)} collective-permute-done((bf16[1552,128]{1,0:T(8,128)(2,1)S(1)}, bf16[1552,128]{1,0:T(8,128)(2,1)S(1)}, u32[]{:S(2)}, u32[]{:S(2)}) %collective-permute-start.7) | collective-permute-done | bytes 397344 | tf_op jit(solution)/shard_map/ppermute | solution.py:61
  34.4 1.3 %collective-permute-start.13 = (bf16[1552,128]{1,0:T(8,128)(2,1)S(1)}, bf16[1552,128]{1,0:T(8,128)(2,1)S(1)}, u32[]{:S(2)}, u32[]{:S(2)}) collective-permute-start(bf16[1552,128]{1,0:T(8,128)(2,1)S(1)} %collective-permute-done.5.refs_1_), channel_id=1, source_target_pairs={{0,2},{1,3},{2,0},{3,1},{4,6},{5,7},{6,4},{7,5},{8,10},{9,11},{10,... | collective-permute-start | bytes 1191944 | tf_op jit(solution)/shard_map/ppermute | solution.py:61
  35.7 1.0 %fold.15.refs_2_ = f32[4224,256]{1,0:T(8,128)S(1)} custom-call(bf16[1552,128]{1,0:T(8,128)(2,1)S(1)} %collective-permute-done.7.refs_0_, bf16[2,2048,256]{2,1,0:T(8,128)(2,1)S(1)} %get-tuple-element.40.refs_1_.refs_2_.refs_3_, f32[4224,256]{1,0:T(8,128)S(1)} %fold.14.refs_2_), custom_call_target="tpu_custom_call", output_to_operand_aliasing={{}: (2, {})} | custom-call | flops 100663296 | bytes 393216 | tf_op jit(solution)/shard_map/fold/pallas_call | solution.py:244
  36.7 0.0 collective-permute-done.10.refs_0_
  36.7 2.5 %collective-permute-start.8 = (bf16[1552,128]{1,0:T(8,128)(2,1)S(1)}, bf16[1552,128]{1,0:T(8,128)(2,1)S(1)}, u32[]{:S(2)}, u32[]{:S(2)}) collective-permute-start(bf16[1552,128]{1,0:T(8,128)(2,1)S(1)} %collective-permute-done.7.refs_0_), channel_id=1, source_target_pairs={{0,4},{1,5},{2,6},{3,7},{4,12},{5,13},{6,14},{7,15},{8,0},{9,1},{1... | collective-permute-start | bytes 1191944 | tf_op jit(solution)/shard_map/ppermute | solution.py:61
  39.2 1.0 %fold.16.refs_3_ = f32[4224,256]{1,0:T(8,128)S(1)} custom-call(bf16[1552,128]{1,0:T(8,128)(2,1)S(1)} %collective-permute-done.10.refs_0_, bf16[2,2048,256]{2,1,0:T(8,128)(2,1)S(1)} %get-tuple-element.40.refs_1_.refs_2_.refs_3_, f32[4224,256]{1,0:T(8,128)S(1)} %fold.15.refs_2_), custom_call_target="tpu_custom_call", output_to_operand_aliasing={{}: (2, {})} | custom-call | flops 100663296 | bytes 393216 | tf_op jit(solution)/shard_map/fold/pallas_call | solution.py:244
  40.2 2.7 %collective-permute-done.9.refs_0_ = bf16[1552,128]{1,0:T(8,128)(2,1)S(1)} collective-permute-done((bf16[1552,128]{1,0:T(8,128)(2,1)S(1)}, bf16[1552,128]{1,0:T(8,128)(2,1)S(1)}, u32[]{:S(2)}, u32[]{:S(2)}) %collective-permute-start.9) | collective-permute-done | bytes 397344 | tf_op jit(solution)/shard_map/ppermute | solution.py:61
  42.9 1.3 %collective-permute-start.12 = (bf16[1552,128]{1,0:T(8,128)(2,1)S(1)}, bf16[1552,128]{1,0:T(8,128)(2,1)S(1)}, u32[]{:S(2)}, u32[]{:S(2)}) collective-permute-start(bf16[1552,128]{1,0:T(8,128)(2,1)S(1)} %collective-permute-done.9.refs_0_), channel_id=1, source_target_pairs={{0,2},{1,3},{2,0},{3,1},{4,6},{5,7},{6,4},{7,5},{8,10},{9,11},{10,... | collective-permute-start | bytes 1191944 | tf_op jit(solution)/shard_map/ppermute | solution.py:61
  44.2 0.0 collective-permute-done.15.refs_1_
  44.2 2.1 %collective-permute-start.11 = (bf16[1552,128]{1,0:T(8,128)(2,1)S(1)}, bf16[1552,128]{1,0:T(8,128)(2,1)S(1)}, u32[]{:S(2)}, u32[]{:S(2)}) collective-permute-start(bf16[1552,128]{1,0:T(8,128)(2,1)S(1)} %collective-permute-done.9.refs_0_), channel_id=1, source_target_pairs={{0,1},{1,0},{2,3},{3,2},{4,5},{5,4},{6,7},{7,6},{8,9},{9,8},{10,11... | collective-permute-start | bytes 1191944 | tf_op jit(solution)/shard_map/ppermute | solution.py:61
  46.3 1.3 %fold.17.refs_2_ = f32[4224,256]{1,0:T(8,128)S(1)} custom-call(bf16[1552,128]{1,0:T(8,128)(2,1)S(1)} %collective-permute-done.9.refs_0_, bf16[1552,128]{1,0:T(8,128)(2,1)S(1)} %collective-permute-done.15.refs_1_, bf16[2,2048,256]{2,1,0:T(8,128)(2,1)S(1)} %get-tuple-element.40.refs_1_.refs_2_.refs_3_, ...), custom_call_target="tpu_custom_call", output_to_operand_aliasing={{}: (3, {})} | custom-call | flops 201326592 | bytes 786432 | tf_op jit(solution)/shard_map/fold/pallas_call | solution.py:244
  47.6 0.0 collective-permute-done.14.refs_0_
  47.6 1.0 %fold.18.refs_2_ = f32[4224,256]{1,0:T(8,128)S(1)} custom-call(bf16[1552,128]{1,0:T(8,128)(2,1)S(1)} %collective-permute-done.14.refs_0_, bf16[2,2048,256]{2,1,0:T(8,128)(2,1)S(1)} %get-tuple-element.40.refs_1_.refs_2_.refs_3_, f32[4224,256]{1,0:T(8,128)S(1)} %fold.17.refs_2_), custom_call_target="tpu_custom_call", output_to_operand_aliasing={{}: (2, {})} | custom-call | flops 100663296 | bytes 393216 | tf_op jit(solution)/shard_map/fold/pallas_call | solution.py:244
  48.6 0.0 collective-permute-done.13.refs_0_
  48.6 1.0 %fold.19.refs_4_ = f32[4224,256]{1,0:T(8,128)S(1)} custom-call(bf16[1552,128]{1,0:T(8,128)(2,1)S(1)} %collective-permute-done.13.refs_0_, bf16[2,2048,256]{2,1,0:T(8,128)(2,1)S(1)} %get-tuple-element.40.refs_1_.refs_2_.refs_3_, f32[4224,256]{1,0:T(8,128)S(1)} %fold.18.refs_2_), custom_call_target="tpu_custom_call", output_to_operand_aliasing={{}: (2, {})} | custom-call | flops 100663296 | bytes 393216 | tf_op jit(solution)/shard_map/fold/pallas_call | solution.py:244
  49.6 1.8 %collective-permute-done.8.refs_0_ = bf16[1552,128]{1,0:T(8,128)(2,1)S(1)} collective-permute-done((bf16[1552,128]{1,0:T(8,128)(2,1)S(1)}, bf16[1552,128]{1,0:T(8,128)(2,1)S(1)}, u32[]{:S(2)}, u32[]{:S(2)}) %collective-permute-start.8) | collective-permute-done | bytes 397344 | tf_op jit(solution)/shard_map/ppermute | solution.py:61
  51.4 2.6 %collective-permute-done.12.refs_2_ = bf16[1552,128]{1,0:T(8,128)(2,1)S(1)} collective-permute-done((bf16[1552,128]{1,0:T(8,128)(2,1)S(1)}, bf16[1552,128]{1,0:T(8,128)(2,1)S(1)}, u32[]{:S(2)}, u32[]{:S(2)}) %collective-permute-start.12) | collective-permute-done | bytes 397344 | tf_op jit(solution)/shard_map/ppermute | solution.py:61
  54.0 0.0 collective-permute-done.11.refs_1_
  54.0 2.8 %last.1 = (f32[4224,256]{1,0:T(8,128)S(1)}, f32[4096,256]{1,0:T(8,128)}) custom-call(bf16[1552,128]{1,0:T(8,128)(2,1)S(1)} %collective-permute-done.8.refs_0_, bf16[1552,128]{1,0:T(8,128)(2,1)S(1)} %collective-permute-done.11.refs_1_, bf16[1552,128]{1,0:T(8,128)(2,1)S(1)} %collective-permute-done.12.refs_2_, ...), custom_call_target="tpu_custom_call", output_to_operand_aliasing={{0}: (4, {})} | custom-call | flops 301989888 | bytes 1179648 | tf_op jit(solution)/shard_map/last/pallas_call | solution.py:244
Async XLA Ops:
  0.0 8.2 %collective-permute-start.1 = (bf16[2,1024,256]{2,1,0:T(8,128)(2,1)}, bf16[2,1024,256]{2,1,0:T(8,128)(2,1)S(1)}, u32[]{:S(2)}, u32[]{:S(2)}) collective-permute-start(bf16[2,1024,256]{2,1,0:T(8,128)(2,1)} %refs_0_.1), channel_id=1, source_target_pairs={{0,16},{16,0},{1,17},{17,1},{2,18},{18,2},{3,19},{19,3},{4,20},{20... | collective-permute-start | bytes 3145736 | tf_op jit(solution)/shard_map/ppermute | solution.py:266
  1.5 9.1 %collective-permute-start = (bf16[1552,128]{1,0:T(8,128)(2,1)S(1)}, bf16[1552,128]{1,0:T(8,128)(2,1)S(1)}, u32[]{:S(2)}, u32[]{:S(2)}) collective-permute-start(bf16[1552,128]{1,0:T(8,128)(2,1)S(1)} %pack.1.refs_0_), channel_id=1, source_target_pairs={{0,2},{1,3},{2,0},{3,1},{4,6},{5,7},{6,4},{7,5},{8,10},{9,11},{10,... | collective-permute-start | bytes 1191944 | tf_op jit(solution)/shard_map/ppermute | solution.py:61
  4.1 12.1 %collective-permute-start.2 = (bf16[1552,128]{1,0:T(8,128)(2,1)S(1)}, bf16[1552,128]{1,0:T(8,128)(2,1)S(1)}, u32[]{:S(2)}, u32[]{:S(2)}) collective-permute-start(bf16[1552,128]{1,0:T(8,128)(2,1)S(1)} %pack.1.refs_0_), channel_id=1, source_target_pairs={{0,8},{1,9},{2,10},{3,11},{4,0},{5,1},{6,2},{7,3},{8,12},{9,13},{1... | collective-permute-start | bytes 1191944 | tf_op jit(solution)/shard_map/ppermute | solution.py:61
  6.7 13.8 %collective-permute-start.3 = (bf16[1552,128]{1,0:T(8,128)(2,1)S(1)}, bf16[1552,128]{1,0:T(8,128)(2,1)S(1)}, u32[]{:S(2)}, u32[]{:S(2)}) collective-permute-start(bf16[1552,128]{1,0:T(8,128)(2,1)S(1)} %pack.1.refs_0_), channel_id=1, source_target_pairs={{0,1},{1,0},{2,3},{3,2},{4,5},{5,4},{6,7},{7,6},{8,9},{9,8},{10,11... | collective-permute-start | bytes 1191944 | tf_op jit(solution)/shard_map/ppermute | solution.py:61
  10.5 15.4 %collective-permute-start.4 = (bf16[1552,128]{1,0:T(8,128)(2,1)S(1)}, bf16[1552,128]{1,0:T(8,128)(2,1)S(1)}, u32[]{:S(2)}, u32[]{:S(2)}) collective-permute-start(bf16[1552,128]{1,0:T(8,128)(2,1)S(1)} %collective-permute-done.refs_0_), channel_id=1, source_target_pairs={{0,4},{1,5},{2,6},{3,7},{4,12},{5,13},{6,14},{7,15},{8,0},{9,1},{1... | collective-permute-start | bytes 1191944 | tf_op jit(solution)/shard_map/ppermute | solution.py:61
  16.2 11.5 %collective-permute-start.5 = (bf16[1552,128]{1,0:T(8,128)(2,1)S(1)}, bf16[1552,128]{1,0:T(8,128)(2,1)S(1)}, u32[]{:S(2)}, u32[]{:S(2)}) collective-permute-start(bf16[1552,128]{1,0:T(8,128)(2,1)S(1)} %collective-permute-done.2.refs_1_), channel_id=1, source_target_pairs={{0,1},{1,0},{2,3},{3,2},{4,5},{5,4},{6,7},{7,6},{8,9},{9,8},{10,11... | collective-permute-start | bytes 1191944 | tf_op jit(solution)/shard_map/ppermute | solution.py:61
  17.5 13.0 %collective-permute-start.6 = (bf16[1552,128]{1,0:T(8,128)(2,1)S(1)}, bf16[1552,128]{1,0:T(8,128)(2,1)S(1)}, u32[]{:S(2)}, u32[]{:S(2)}) collective-permute-start(bf16[1552,128]{1,0:T(8,128)(2,1)S(1)} %collective-permute-done.2.refs_1_), channel_id=1, source_target_pairs={{0,2},{1,3},{2,0},{3,1},{4,6},{5,7},{6,4},{7,5},{8,10},{9,11},{10,... | collective-permute-start | bytes 1191944 | tf_op jit(solution)/shard_map/ppermute | solution.py:61
  20.5 13.9 %collective-permute-start.7 = (bf16[1552,128]{1,0:T(8,128)(2,1)S(1)}, bf16[1552,128]{1,0:T(8,128)(2,1)S(1)}, u32[]{:S(2)}, u32[]{:S(2)}) collective-permute-start(bf16[1552,128]{1,0:T(8,128)(2,1)S(1)} %collective-permute-done.3.refs_0_), channel_id=1, source_target_pairs={{0,4},{1,5},{2,6},{3,7},{4,12},{5,13},{6,14},{7,15},{8,0},{9,1},{1... | collective-permute-start | bytes 1191944 | tf_op jit(solution)/shard_map/ppermute | solution.py:61
  24.0 12.7 %collective-permute-start.10 = (bf16[1552,128]{1,0:T(8,128)(2,1)S(1)}, bf16[1552,128]{1,0:T(8,128)(2,1)S(1)}, u32[]{:S(2)}, u32[]{:S(2)}) collective-permute-start(bf16[1552,128]{1,0:T(8,128)(2,1)S(1)} %collective-permute-done.refs_0_), channel_id=1, source_target_pairs={{0,1},{1,0},{2,3},{3,2},{4,5},{5,4},{6,7},{7,6},{8,9},{9,8},{10,11... | collective-permute-start | bytes 1191944 | tf_op jit(solution)/shard_map/ppermute | solution.py:61
  25.9 17.0 %collective-permute-start.9 = (bf16[1552,128]{1,0:T(8,128)(2,1)S(1)}, bf16[1552,128]{1,0:T(8,128)(2,1)S(1)}, u32[]{:S(2)}, u32[]{:S(2)}) collective-permute-start(bf16[1552,128]{1,0:T(8,128)(2,1)S(1)} %collective-permute-done.4.refs_0_), channel_id=1, source_target_pairs={{0,4},{1,5},{2,6},{3,7},{4,12},{5,13},{6,14},{7,15},{8,0},{9,1},{1... | collective-permute-start | bytes 1191944 | tf_op jit(solution)/shard_map/ppermute | solution.py:61
  27.7 16.5 %collective-permute-start.15 = (bf16[1552,128]{1,0:T(8,128)(2,1)S(1)}, bf16[1552,128]{1,0:T(8,128)(2,1)S(1)}, u32[]{:S(2)}, u32[]{:S(2)}) collective-permute-start(bf16[1552,128]{1,0:T(8,128)(2,1)S(1)} %collective-permute-done.4.refs_0_), channel_id=1, source_target_pairs={{0,2},{1,3},{2,0},{3,1},{4,6},{5,7},{6,4},{7,5},{8,10},{9,11},{10,... | collective-permute-start | bytes 1191944 | tf_op jit(solution)/shard_map/ppermute | solution.py:61
  30.5 17.1 %collective-permute-start.14 = (bf16[1552,128]{1,0:T(8,128)(2,1)S(1)}, bf16[1552,128]{1,0:T(8,128)(2,1)S(1)}, u32[]{:S(2)}, u32[]{:S(2)}) collective-permute-start(bf16[1552,128]{1,0:T(8,128)(2,1)S(1)} %collective-permute-done.4.refs_0_), channel_id=1, source_target_pairs={{0,1},{1,0},{2,3},{3,2},{4,5},{5,4},{6,7},{7,6},{8,9},{9,8},{10,11... | collective-permute-start | bytes 1191944 | tf_op jit(solution)/shard_map/ppermute | solution.py:61
  34.4 14.2 %collective-permute-start.13 = (bf16[1552,128]{1,0:T(8,128)(2,1)S(1)}, bf16[1552,128]{1,0:T(8,128)(2,1)S(1)}, u32[]{:S(2)}, u32[]{:S(2)}) collective-permute-start(bf16[1552,128]{1,0:T(8,128)(2,1)S(1)} %collective-permute-done.5.refs_1_), channel_id=1, source_target_pairs={{0,2},{1,3},{2,0},{3,1},{4,6},{5,7},{6,4},{7,5},{8,10},{9,11},{10,... | collective-permute-start | bytes 1191944 | tf_op jit(solution)/shard_map/ppermute | solution.py:61
  36.7 14.6 %collective-permute-start.8 = (bf16[1552,128]{1,0:T(8,128)(2,1)S(1)}, bf16[1552,128]{1,0:T(8,128)(2,1)S(1)}, u32[]{:S(2)}, u32[]{:S(2)}) collective-permute-start(bf16[1552,128]{1,0:T(8,128)(2,1)S(1)} %collective-permute-done.7.refs_0_), channel_id=1, source_target_pairs={{0,4},{1,5},{2,6},{3,7},{4,12},{5,13},{6,14},{7,15},{8,0},{9,1},{1... | collective-permute-start | bytes 1191944 | tf_op jit(solution)/shard_map/ppermute | solution.py:61
  42.9 11.0 %collective-permute-start.12 = (bf16[1552,128]{1,0:T(8,128)(2,1)S(1)}, bf16[1552,128]{1,0:T(8,128)(2,1)S(1)}, u32[]{:S(2)}, u32[]{:S(2)}) collective-permute-start(bf16[1552,128]{1,0:T(8,128)(2,1)S(1)} %collective-permute-done.9.refs_0_), channel_id=1, source_target_pairs={{0,2},{1,3},{2,0},{3,1},{4,6},{5,7},{6,4},{7,5},{8,10},{9,11},{10,... | collective-permute-start | bytes 1191944 | tf_op jit(solution)/shard_map/ppermute | solution.py:61
  44.2 9.8 %collective-permute-start.11 = (bf16[1552,128]{1,0:T(8,128)(2,1)S(1)}, bf16[1552,128]{1,0:T(8,128)(2,1)S(1)}, u32[]{:S(2)}, u32[]{:S(2)}) collective-permute-start(bf16[1552,128]{1,0:T(8,128)(2,1)S(1)} %collective-permute-done.9.refs_0_), channel_id=1, source_target_pairs={{0,1},{1,0},{2,3},{3,2},{4,5},{5,4},{6,7},{7,6},{8,9},{9,8},{10,11... | collective-permute-start | bytes 1191944 | tf_op jit(solution)/shard_map/ppermute | solution.py:61
